TPU v7x, 256 devices: a whole 4x4x8 slice. The times are simulated.
256 devices in a mesh: tm: 8 (over y, x_lo), lon: 32 (over x_hi, z, core).
Axes of the slice: x: 4 (x_hi: 2, x_lo: 2; x = x_hi * 2 + x_lo), y: 4, z: 8, core: 2. Of those that a mesh axis runs over, the one named last changes fastest.
Arguments:
- first_guess: float32 [16, 256, 80, 64], P('tm', 'lon'), may hold values from -6 to 6
- background: float32 [256, 80, 64], P('lon'), may hold values from -6 to 6
- opening_kernel_matrix: bfloat16 [256, 720], replicated, may hold values from -0.21875 to 0.21875
- hidden_layer_shift: float32 [256], replicated, may hold values from -3 to 3
- closing_kernel_matrix: bfloat16 [80, 2304], replicated, may hold values from -0.125 to 0.125
- output_layer_shift: float32 [80], replicated, may hold values from -2 to 2
- model_weight: float32 [80], replicated, may hold values from 0.5 to 2
- background_weight: float32 [80], replicated, may hold values from 0.5 to 2
- obs_cell: int32 [16, 8192], P('tm', 'lon'), may hold values from 0 to 511
- obs_chan: int32 [16, 8192], P('tm', 'lon'), may hold values from 0 to 79
- obs_value: float32 [16, 8192], P('tm', 'lon'), may hold values from -6 to 6
- obs_weight: float32 [16, 8192], P('tm', 'lon'), may hold values from 0.5 to 4
- step_size: float32 [], replicated, may hold values from 0.3 to 0.6
Outputs:
- analysis: float32 [16, 256, 80, 64], P('tm', 'lon')
- costs: float32 [2], replicated
Inputs may be any that keep to these rules, and one draw needn't show every extreme that they name: `obs_cell`: the band of an observation is its column block of 256; the value counts cells of that band, longitude-major.
All inputs are finite; a program needn't handle non-finite values.
Results may differ from a plain program's by a relative error of at most 0.0085.
Values may be sent and summed in bfloat16 or wider, within the bound.
No kernel may reach another device: no remote copies, remote signals or barrier semaphores. Data moves between devices by JAX's collectives and lax.ppermute only.
A program may use at most 64 MiB of HBM per device.

v0:
```python
import functools

import jax
import jax.numpy as jnp
from jax import lax
from jax.experimental import pallas as pl
from jax.experimental.pallas import tpu as pltpu
from jax.sharding import Mesh
from jax.sharding import PartitionSpec as P


LON = ("lon_0", "lon_1", "lon_2")
TM = ("tm_0", "tm_1")
TM_LON = TM + LON
C = 80
F = 256
LAT = 64
BAND = 8
HALO = 4
OBS = 256
W2 = 2 * LAT
F32 = jnp.float32
BF16 = jnp.bfloat16
KC = 0.7978845608028654


def lanes(rows=C):
    return lax.broadcasted_iota(jnp.int32, (rows, W2), 1)


def call(kernel, ins, outs, scratch=(), limit=8, scalars=0):
    smem = pl.BlockSpec(memory_space=pltpu.SMEM)
    vmem = pl.BlockSpec(memory_space=pltpu.VMEM)
    return pl.pallas_call(
        kernel,
        out_shape=tuple(jax.ShapeDtypeStruct(shape, dtype) for shape, dtype in outs),
        in_specs=[smem] * scalars + [vmem] * (len(ins) - scalars),
        out_specs=tuple(vmem for _ in outs),
        scratch_shapes=list(scratch),
        compiler_params=pltpu.CompilerParams(vmem_limit_bytes=limit << 20),
    )(*ins)


def dot(a, b):
    return jnp.dot(a, b, preferred_element_type=F32)


def earlier_lat(v):
    lane = lanes(v.shape[0])
    return jnp.where((lane == 0) | (lane == LAT), 0.0, pltpu.roll(v, 1, 1))


def later_lat(v):
    lane = lanes(v.shape[0])
    return jnp.where((lane == LAT - 1) | (lane == W2 - 1), 0.0, pltpu.roll(v, W2 - 1, 1))


def halves(v):
    return pltpu.roll(v, LAT, 1)


def pack_kernel(place_ref, step_ref, x_ref, xp_ref, xl_ref, xr_ref, place_row, step_row):
    place_row[...] = jnp.full((1, W2), place_ref[0], jnp.int32)
    step_row[...] = jnp.full((1, W2), step_ref[0], F32)
    for i in range(BAND):
        v = jnp.concatenate([x_ref[0, i], x_ref[1, i]], axis=0).T
        xp_ref[i] = v
        half = xl_ref if i < HALO else xr_ref
        half[i % HALO] = v.astype(BF16)


def pack(place, step, x):
    edge = ((HALO, C, W2), BF16)
    outs = [((BAND, C, W2), F32), edge, edge, ((1, W2), jnp.int32), ((1, W2), F32)]
    return call(pack_kernel, [place, step, x], outs, scalars=2)


def weights_kernel(ot_ref, c_ref, b1_ref, b2_ref, mw_ref, bw_ref, bg_ref,
                   o_ref, k2_ref, wia_ref, woa_ref, bias_ref, small_ref, bgp_ref, tall, row):
    tall[9 * C :, :] = jnp.zeros((768 - 9 * C, F), F32)
    tall[: 9 * C, :] = ot_ref[...].astype(F32)
    o_ref[...] = tall[...].T[:, : 9 * C].astype(BF16)
    turned = ot_ref
    for t in range(9):
        a, b = divmod(t, 3)
        block = c_ref[:, F * t : F * (t + 1)]
        k2_ref[C * b : C * (b + 1), F * a : F * (a + 1)] = block
        tall[C * (8 - t) : C * (9 - t), :] = block.astype(F32)
        wia_ref[C * b : C * (b + 1), F * a : F * (a + 1)] = turned[C * (8 - t) : C * (9 - t), :]
    back = tall[...].T
    woa_ref[...] = back[:, : 9 * C].astype(BF16)
    bias_ref[...] = jnp.broadcast_to(b1_ref[...], (W2, F)).T
    row[...] = jnp.zeros((W2, W2), F32)
    for n, ref in enumerate((b2_ref, mw_ref, bw_ref)):
        row[:, :C] = jnp.broadcast_to(ref[...], (W2, C))
        small_ref[n] = row[...].T[:C]
    for i in range(BAND):
        bgp_ref[i] = jnp.concatenate([bg_ref[i], jnp.zeros((LAT, C), F32)], axis=0).T


def prepare_weights(opening_t, closing, b1, b2, mw, bw, bg):
    ins = [opening_t, closing, b1[None], b2[None], mw[None], bw[None], bg]
    outs = [((F, 9 * C), BF16), ((3 * C, 3 * F), BF16), ((3 * C, 3 * F), BF16), ((F, 9 * C), BF16)]
    outs += [((F, W2), F32), ((3, C, W2), F32), ((BAND, C, W2), F32)]
    return call(
        weights_kernel,
        ins,
        outs,
        [pltpu.VMEM((768, F), F32), pltpu.VMEM((W2, W2), F32)],
    )


def split3(v):
    hi = v.astype(BF16)
    rest = v - hi.astype(F32)
    mid = rest.astype(BF16)
    low = (rest - mid.astype(F32)).astype(BF16)
    return jnp.concatenate([hi, mid, low], axis=0)


def join3(v):
    return (v[2 * C :] + v[C : 2 * C]) + v[:C]


def obs_kernel(cell_ref, chan_ref, val_ref, wt_ref, x_ref, r_ref, s_ref, hot, plain=False):
    def line(ref):
        return jnp.concatenate([ref[0:1, :], ref[1:2, :]], axis=1)

    cell = line(cell_ref)
    sub = (lax.broadcasted_iota(jnp.int32, cell.shape, 1) >= OBS).astype(jnp.int32)
    spot = (cell >> 6) * W2 + sub * LAT + (cell & (LAT - 1))
    rows = 2 * W2
    for p in range(BAND // 2):
        at = lax.broadcasted_iota(jnp.int32, (rows, 2 * OBS), 0) + p * rows
        hot[p] = jnp.where(at == spot, 1.0, 0.0).astype(BF16)
    total = jnp.zeros((3 * C, 2 * OBS), F32)
    for p in range(BAND // 2):
        total = total + dot(split3(jnp.concatenate([x_ref[2 * p], x_ref[2 * p + 1]], axis=1)), hot[p])
    mine = lax.broadcasted_iota(jnp.int32, (C, 2 * OBS), 0) == line(chan_ref)
    r = jnp.sum(jnp.where(mine, join3(total), 0.0), axis=0, keepdims=True)
    if not plain:
        r = r - line(val_ref)
    r_ref[0:1, :] = r[:, :OBS]
    r_ref[1:2, :] = r[:, OBS:]
    spread = split3(jnp.where(mine, line(wt_ref) * r, 0.0))
    for p in range(BAND // 2):
        got = lax.dot_general(spread, hot[p], (((1,), (1,)), ((), ())), preferred_element_type=F32)
        got = join3(got)
        s_ref[2 * p] = got[:, :W2]
        s_ref[2 * p + 1] = got[:, W2:]


def observe(cell, chan, val, wt, field, plain):
    return call(
        functools.partial(obs_kernel, plain=plain),
        [cell, chan, val, wt, field],
        [((2, OBS), F32), ((BAND, C, W2), F32)],
        [pltpu.VMEM((BAND // 2, 2 * W2, 2 * OBS), BF16)],
    )


def strip_kernel(l_ref, a_ref, b_ref, r_ref, up_ref, down_ref):
    def at(e):
        if e < 0:
            return l_ref[HALO + e].astype(F32)
        if e < HALO:
            return a_ref[e].astype(F32)
        if e < BAND:
            return b_ref[e - HALO].astype(F32)
        return r_ref[e - BAND].astype(F32)

    left = lanes() < LAT
    for p in range(6):
        one, two = at(p - 2), at(p + 4)
        up_ref[p] = jnp.where(left, one, halves(two)).astype(BF16)
        down_ref[p] = jnp.where(left, halves(one), two).astype(BF16)


def strips(from_left, mine_left, mine_right, from_right):
    strip = ((6, C, W2), BF16)
    return call(strip_kernel, [from_left, mine_left, mine_right, from_right], [strip, strip])


def gelu_pair(v):
    sq = v * v
    t = jnp.tanh(v * (KC + (KC * 0.044715) * sq))
    half = 0.5 * (1.0 + t)
    slope = half + (0.5 * v) * (1.0 - t * t) * (KC + (3 * KC * 0.044715) * sq)
    return v * half, slope


def stack_lats(ref, n, v):
    ref[3 * C * n : 3 * C * n + C] = earlier_lat(v).astype(BF16)
    ref[3 * C * n + C : 3 * C * n + 2 * C] = v.astype(BF16)
    ref[3 * C * n + 2 * C : 3 * C * n + 3 * C] = later_lat(v).astype(BF16)


def window(ref, n, rows):
    return jnp.concatenate([ref[rows * n : rows * (n + 3)], ref[rows * (n + 1) : rows * (n + 4)]], axis=1)


def sum_lats(s):
    res = []
    for k in range(2):
        part = s[:, W2 * k : W2 * (k + 1)]
        res.append(earlier_lat(part[:C]) + part[C : 2 * C] + later_lat(part[2 * C :]))
    return res


def step_from(sums, step, total):
    whole = jnp.sum(sums, axis=0, keepdims=True)
    lane = lax.broadcasted_iota(jnp.int32, whole.shape, 1)
    norm = jnp.sum(jnp.where(lane == 0, whole, 0.0), axis=1, keepdims=True)
    return step[:, :1] / jnp.sqrt(norm / total + 1e-06)


def gradient_kernel(total, second, n_tm, n_all):
    def kernel(*refs):
        refs = list(refs)
        take = lambda n: [refs.pop(0) for _ in range(n)]
        (place_ref,) = take(1)
        if second:
            step_ref, sums_ref = take(2)
            g0_ref, glft, grgt, upp1, dwn1, r1_ref, s1_ref = take(7)
        own_ref, lft, rgt, upp0, dwn0, r0_ref, s0_ref = take(7)
        bg_ref, wt_ref, o_ref, k2_ref, wia_ref, woa_ref, bias_ref, small_ref = take(8)
        if second:
            g_ref, x1_ref, row_ref = take(3)
        else:
            g_ref, gl_ref, gr_ref, row_ref = take(4)
        vx, hid, slope, vl, x_ext, x_prev, ln, gh = refs
        place = place_ref[...]
        left = lanes() < LAT
        if second:
            alpha = step_from(sums_ref[...], step_ref[...], total)

            def upp(n):
                return upp0[n].astype(F32) - alpha * upp1[n].astype(F32)

            def dwn(n):
                return dwn0[n].astype(F32) - alpha * dwn1[n].astype(F32)

            def obs(n):
                return s0_ref[n] - alpha * s1_ref[n]

            for e in range(16):
                v = lft[e] if e < HALO else own_ref[e - HALO] if e < HALO + BAND else rgt[e - HALO - BAND]
                g = glft[e] if e < HALO else g0_ref[e - HALO] if e < HALO + BAND else grgt[e - HALO - BAND]
                v = v.astype(F32) - alpha * g.astype(F32)
                x_ext[e] = v
                if HALO <= e < HALO + BAND:
                    x1_ref[e - HALO] = v
                stack_lats(vx, e, v)
        else:

            def upp(n):
                return upp0[n].astype(F32)

            def dwn(n):
                return dwn0[n].astype(F32)

            def obs(n):
                return s0_ref[n]

            for e in range(16):
                v = lft[e] if e < HALO else own_ref[e - HALO] if e < HALO + BAND else rgt[e - HALO - BAND]
                v = v.astype(F32)
                x_ext[e] = v
                stack_lats(vx, e, v)
        bias = bias_ref[...]
        bias2 = jnp.concatenate([bias, bias], axis=1)
        b2 = small_ref[0]
        mw = small_ref[1]
        bw = small_ref[2]
        for h in range(0, 14, 2):
            pre = dot(o_ref[...], window(vx, h, 3 * C)) + bias2
            act, sl = gelu_pair(pre)
            for k in range(2):
                n = h + k
                hid[F * n : F * (n + 1)] = act[:, W2 * k : W2 * (k + 1)].astype(BF16)
                if 2 <= n < 12:
                    slope[n - 2] = sl[:, W2 * k : W2 * (k + 1)]
        for o in range(0, 12, 2):
            s = sum_lats(dot(k2_ref[...], window(hid, o, F)))
            for k in range(2):
                n = o + k
                x = x_ext[n + 2]
                m = x + s[k] + b2
                u = upp(n % 6)
                nxt = jnp.where(left, halves(x), u if n >= 6 else halves(u))
                keep = left | (place < n_tm - 1)
                lv = jnp.where(keep, mw * (nxt - m), 0.0)
                ln[n] = lv
                stack_lats(vl, n, lv)
        for h in range(0, 10, 2):
            z = dot(woa_ref[...], window(vl, h, 3 * C))
            for k in range(2):
                n = h + k
                hid[F * n : F * (n + 1)] = (slope[n] * z[:, W2 * k : W2 * (k + 1)]).astype(BF16)
        for o in range(0, BAND, 2):
            s = sum_lats(dot(wia_ref[...], window(hid, o, F)))
            for k in range(2):
                gh[o + k] = ln[o + k + 2] + s[k]
        for r in range(8):
            one = dwn(r) if r < 6 else halves(dwn(r - 6))
            two = dwn(r - 2) if r >= 2 else halves(dwn(r + 4))
            v = jnp.where(left, one, two)
            x_prev[r] = v
            stack_lats(vx, r, v)
        for h in range(0, 6, 2):
            act, _ = gelu_pair(dot(o_ref[...], window(vx, h, 3 * C)) + bias2)
            for k in range(2):
                n = h + k
                hid[F * n : F * (n + 1)] = act[:, W2 * k : W2 * (k + 1)].astype(BF16)
        squares = jnp.zeros((C, W2), F32)
        cost = jnp.zeros((C, W2), F32)
        for o in range(0, 4, 2):
            s = sum_lats(dot(k2_ref[...], window(hid, o, F)))
            for k in range(2):
                m = x_prev[o + k + 2] + s[k] + b2
                for side in range(2):
                    i = o + k + 4 * side
                    x = x_ext[i + HALO]
                    before = m if side == 0 else halves(m)
                    first = jnp.where(place > 0, mw * (x - before), 0.0)
                    lo = jnp.where(left, first, halves(ln[i + 2]))
                    dep = jnp.where(left & (place == 0), x - bg_ref[i], 0.0)
                    g = lo - gh[i] + obs(i) + bw * dep
                    g_ref[i] = g
                    if not second:
                        edge = gl_ref if i < HALO else gr_ref
                        edge[i % HALO] = g.astype(BF16)
                    squares = squares + g * g
                    cost = cost + lo * lo / mw + bw * dep * dep
        r = r0_ref[...]
        if second:
            r = r - alpha * r1_ref[...]
        paid = jnp.sum(jnp.sum(wt_ref[...] * r * r, axis=0, keepdims=True), axis=1, keepdims=True)
        norm = jnp.sum(jnp.sum(squares, axis=0, keepdims=True), axis=1, keepdims=True)
        paid = 0.5 * (paid + jnp.sum(jnp.sum(cost, axis=0, keepdims=True), axis=1, keepdims=True))
        lane = lax.broadcasted_iota(jnp.int32, (n_all, W2), 1)
        row_ref[...] = jnp.where(lane == 0, norm, jnp.where(lane == 1, paid, 0.0))

    return kernel


def gradient(total, n_tm, n_all, ins, second):
    full = ((BAND, C, W2), F32)
    edge = ((HALO, C, W2), BF16)
    row = ((n_all, W2), F32)
    outs = [full, full, row] if second else [full, edge, edge, row]
    return call(
        gradient_kernel(total, second, n_tm, n_all),
        ins,
        outs,
        [
            pltpu.VMEM((16 * 3 * C, W2), BF16),
            pltpu.VMEM((14 * F, W2), BF16),
            pltpu.VMEM((10, F, W2), F32),
            pltpu.VMEM((12 * 3 * C, W2), BF16),
            pltpu.VMEM((16, C, W2), F32),
            pltpu.VMEM((8, C, W2), F32),
            pltpu.VMEM((12, C, W2), F32),
            pltpu.VMEM((BAND, C, W2), F32),
        ],
        limit=24,
    )


def final_kernel(total):
    def kernel(step_ref, first_ref, sums_ref, x_ref, g_ref, x_out, cost_out):
        alpha = step_from(sums_ref[...], step_ref[...], total)
        for i in range(BAND):
            v = x_ref[i] - alpha * g_ref[i]
            v = jnp.concatenate([v, jnp.zeros((W2 - C, W2), F32)], axis=0).T[:, :C]
            x_out[0, i] = v[:LAT]
            x_out[1, i] = v[LAT:]
        c0 = jnp.sum(first_ref[...], axis=0, keepdims=True)
        c1 = jnp.sum(sums_ref[...], axis=0, keepdims=True)
        lane = lax.broadcasted_iota(jnp.int32, c0.shape, 1)
        one = jnp.sum(jnp.where(lane == 1, c0, 0.0), axis=1, keepdims=True)
        two = jnp.sum(jnp.where(lane == 1, c1, 0.0), axis=1, keepdims=True)
        cost_out[...] = jnp.where(lane == 0, one, two)[:, :2]

    return kernel


def shifted(value, axes, by, closed):
    n = lax.axis_size(axes)
    pairs = [(i, (i + by) % n) for i in range(n) if closed or 0 <= i + by < n]
    return lax.ppermute(value, axes, pairs)


def exchange(mine_left, mine_right):
    from_right = shifted(mine_left, LON, -1, True)
    from_left = shifted(mine_right, LON, 1, True)
    up, down = strips(from_left, mine_left, mine_right, from_right)
    after = shifted(up, TM, -1, False)
    before = shifted(down, TM, 1, False)
    return from_left, from_right, after, before


def per_device(x, background, opening, b1, closing, b2, mw, bw, cell, chan, val, wt, step):
    n_tm = lax.axis_size(TM)
    n_all = n_tm * lax.axis_size(LON)
    total = float(2 * BAND * C * LAT * n_all)
    place = lax.axis_index(TM).astype(jnp.int32)[None]
    step = step[None]
    xp, xl, xr, place, step = pack(place, step, jnp.swapaxes(x, 2, 3))
    halo = exchange(xl, xr)
    o, k2, wia, woa, bias, small, bgp = prepare_weights(
        opening.T, closing, b1, b2, mw, bw, jnp.swapaxes(background, 1, 2)
    )
    r0, s0 = observe(cell, chan, val, wt, xp, False)
    consts = (bgp, wt, o, k2, wia, woa, bias, small)
    base = (xp,) + halo + (r0, s0)
    g0, gl, gr, row = gradient(total, n_tm, n_all, (place,) + base + consts, False)
    ghalo = exchange(gl, gr)
    rg, sg = observe(cell, chan, val, wt, g0, True)
    row, rg, _, _ = lax.optimization_barrier((row, rg) + ghalo[:2])
    sums0 = lax.all_to_all(row, TM_LON, 0, 0, tiled=True)
    ins = (place, step, sums0, g0) + ghalo + (rg, sg) + base + consts
    g1, x1, row = gradient(total, n_tm, n_all, ins, True)
    sums1 = lax.all_to_all(row, TM_LON, 0, 0, tiled=True)
    x2, costs = call(
        final_kernel(total),
        [step, sums0, sums1, x1, g1],
        [((2, BAND, LAT, C), F32), ((1, 2), F32)],
    )
    return jnp.swapaxes(x2, 2, 3), costs.reshape(2)


def solution(mesh):
    n_tm, n_lon = mesh.devices.shape
    if (n_tm, n_lon) == (8, 32):
        shape = (4, 2, 2, 8, 2)
    else:
        shape = (n_tm, 1, 1, n_lon // 2, 2)
    split = Mesh(mesh.devices.reshape(shape), TM_LON)
    placed = (
        P(TM, LON, None, None),
        P(LON, None, None),
        P(), P(), P(), P(), P(), P(),
        P(TM, LON), P(TM, LON), P(TM, LON), P(TM, LON),
        P(),
    )
    return jax.shard_map(
        per_device,
        mesh=split,
        in_specs=placed,
        out_specs=(P(TM, LON, None, None), P()),
        check_vma=False,
    )
```

profile of v0, /device:TPU:1, one launch (start us, length us, event | category | flops | bytes accessed | tf_op | source)
XLA Modules:
  0.0 99.4 jit_solution(5350974107705075274)
XLA Ops:
  1.3 0.0 copy-start
  1.3 1.0 %copy-done = f32[2,8,80,64]{2,3,1,0:T(8,128)S(1)} copy-done((f32[2,8,80,64]{2,3,1,0:T(8,128)S(1)}, f32[2,8,80,64]{2,3,1,0:T(8,128)}, u32[]{:S(2)}) %copy-start) | copy-done | bytes 327704
  2.3 0.0 copy-start.4
  2.3 0.2 shard_map.140
  2.5 0.0 copy-start.3
  2.6 3.1 %collective-permute-start = (bf16[4,80,128]{2,1,0:T(8,128)(2,1)S(1)}, bf16[4,80,128]{2,1,0:T(8,128)(2,1)S(1)}, u32[]{:S(2)}, u32[]{:S(2)}) collective-permute-start(bf16[4,80,128]{2,1,0:T(8,128)(2,1)S(1)} %get-tuple-element.36.b_ref), channel_id=1, source_target_pairs={{0,1},{1,2},{2,3},{3,4},{4,5},{5,6},{6,7},{7,8},{8,9},{9,10},{10,1... | collective-permute-start | bytes 245768 | tf_op jit(solution)/shard_map/ppermute | solution.py:391
  5.6 0.3 collective-permute-start.1
  5.9 1.2 %collective-permute-done.l_ref.refs_2_.refs_11_ = bf16[4,80,128]{2,1,0:T(8,128)(2,1)S(1)} collective-permute-done((bf16[4,80,128]{2,1,0:T(8,128)(2,1)S(1)}, bf16[4,80,128]{2,1,0:T(8,128)(2,1)S(1)}, u32[]{:S(2)}, u32[]{:S(2)}) %collective-permute-start) | collective-permute-done | bytes 81952 | tf_op jit(solution)/shard_map/ppermute | solution.py:391
  7.1 2.4 %collective-permute-done.1.r_ref.refs_3_.refs_12_ = bf16[4,80,128]{2,1,0:T(8,128)(2,1)S(1)} collective-permute-done((bf16[4,80,128]{2,1,0:T(8,128)(2,1)S(1)}, bf16[4,80,128]{2,1,0:T(8,128)(2,1)S(1)}, u32[]{:S(2)}, u32[]{:S(2)}) %collective-permute-start.1) | collective-permute-done | bytes 81952 | tf_op jit(solution)/shard_map/ppermute | solution.py:391
  9.5 0.1 shard_map.141
  9.7 1.3 %collective-permute-start.2 = (bf16[6,80,128]{2,1,0:T(8,128)(2,1)S(1)}, bf16[6,80,128]{2,1,0:T(8,128)(2,1)S(1)}, u32[]{:S(2)}, u32[]{:S(2)}) collective-permute-start(bf16[6,80,128]{2,1,0:T(8,128)(2,1)S(1)} %get-tuple-element.38), channel_id=1, source_target_pairs={{32,0},{64,32},{96,64},{128,96},{160,128},{192,160},{224,192},{33,... | collective-permute-start | bytes 368648 | tf_op jit(solution)/shard_map/ppermute | solution.py:391
  11.0 4.0 %collective-permute-start.3 = (bf16[6,80,128]{2,1,0:T(8,128)(2,1)S(1)}, bf16[6,80,128]{2,1,0:T(8,128)(2,1)S(1)}, u32[]{:S(2)}, u32[]{:S(2)}) collective-permute-start(bf16[6,80,128]{2,1,0:T(8,128)(2,1)S(1)} %get-tuple-element.39), channel_id=1, source_target_pairs={{0,32},{32,64},{64,96},{96,128},{128,160},{160,192},{192,224},{1,3... | collective-permute-start | bytes 368648 | tf_op jit(solution)/shard_map/ppermute | solution.py:391
  15.0 0.0 copy-done.23
  15.0 0.0 copy-done.24
  15.0 0.0 copy-start.29
  15.0 0.0 copy-start.30
  15.0 0.9 shard_map.142
  15.9 0.0 copy-start.27
  16.0 0.0 copy-start.28
  16.0 0.0 copy-done.4
  16.0 0.0 copy-done.3
  16.0 0.0 copy-done.13
  16.0 0.0 copy-done.29
  16.0 0.0 copy-done.30
  16.0 0.6 copy-done.27
  16.6 0.5 shard_map.143
  17.1 0.0 collective-permute-done.2.refs_4_.refs_13_
  17.1 0.0 collective-permute-done.3.refs_5_.refs_14_
  17.1 4.1 %shard_map.144 = (f32[8,80,128]{2,1,0:T(8,128)S(1)}, bf16[4,80,128]{2,1,0:T(8,128)(2,1)S(1)}, bf16[4,80,128]{2,1,0:T(8,128)(2,1)S(1)}, f32[256,128]{1,0:T(8,128)S(1)}) custom-call(s32[1,128]{1,0:T(1,128)S(1)} %get-tuple-element.34.refs_0_, f32[8,80,128]{2,1,0:T(8,128)S(1)} %get-tuple-element.35.x_ref.refs_1_.refs_10_, ...), custom_call_target="tpu_custom_call" | custom-call | tf_op jit(solution)/shard_map/pallas_call | solution.py:34
  21.3 0.0 copy-done.1
  21.3 0.0 copy-start.14
  21.3 0.0 copy-start.19
  21.3 0.0 copy-start.21
  21.3 1.4 %collective-permute-start.4 = (bf16[4,80,128]{2,1,0:T(8,128)(2,1)S(1)}, bf16[4,80,128]{2,1,0:T(8,128)(2,1)S(1)}, u32[]{:S(2)}, u32[]{:S(2)}) collective-permute-start(bf16[4,80,128]{2,1,0:T(8,128)(2,1)S(1)} %get-tuple-element.52.b_ref), channel_id=1, source_target_pairs={{0,1},{1,2},{2,3},{3,4},{4,5},{5,6},{6,7},{7,8},{8,9},{9,10},{10,1... | collective-permute-start | bytes 245768 | tf_op jit(solution)/shard_map/ppermute | solution.py:391
  22.7 4.1 %collective-permute-start.5 = (bf16[4,80,128]{2,1,0:T(8,128)(2,1)S(1)}, bf16[4,80,128]{2,1,0:T(8,128)(2,1)S(1)}, u32[]{:S(2)}, u32[]{:S(2)}) collective-permute-start(bf16[4,80,128]{2,1,0:T(8,128)(2,1)S(1)} %get-tuple-element.53.a_ref), channel_id=1, source_target_pairs={{0,31},{1,0},{2,1},{3,2},{4,3},{5,4},{6,5},{7,6},{8,7},{9,8},{10,9... | collective-permute-start | bytes 245768 | tf_op jit(solution)/shard_map/ppermute | solution.py:391
  26.8 0.9 shard_map.145
  27.8 0.0 copy-start.5
  27.8 0.7 copy-done.5
  28.5 0.0 collective-permute-done.4.l_ref.refs_4_
  28.5 0.6 copy-done.7
  29.1 0.0 collective-permute-done.5.r_ref.refs_5_
  29.1 0.6 copy-done.10
  29.8 16.8 %all-to-all-start = ((f32[256,1,128]{2,1,0:T(1,128)}), f32[256,1,128]{2,1,0:T(1,128)S(1)}, u32[]{:S(2)}, u32[]{:S(2)}) async-start(f32[256,1,128]{2,1,0:T(1,128)} %bitcast.26), calls=%async_computation | async-start | bytes 262144 | tf_op jit(solution)/shard_map/all_to_all | solution.py:421
  46.6 0.9 copy-done.8
  47.5 0.9 copy-done.11
  48.4 0.9 copy-done.20
  49.3 0.9 copy-done.22
  50.2 0.1 shard_map.146
  50.3 1.3 %collective-permute-start.6 = (bf16[6,80,128]{2,1,0:T(8,128)(2,1)S(1)}, bf16[6,80,128]{2,1,0:T(8,128)(2,1)S(1)}, u32[]{:S(2)}, u32[]{:S(2)}) collective-permute-start(bf16[6,80,128]{2,1,0:T(8,128)(2,1)S(1)} %get-tuple-element.55), channel_id=1, source_target_pairs={{32,0},{64,32},{96,64},{128,96},{160,128},{192,160},{224,192},{33,... | collective-permute-start | bytes 368648 | tf_op jit(solution)/shard_map/ppermute | solution.py:391
  51.6 4.2 %collective-permute-start.7 = (bf16[6,80,128]{2,1,0:T(8,128)(2,1)S(1)}, bf16[6,80,128]{2,1,0:T(8,128)(2,1)S(1)}, u32[]{:S(2)}, u32[]{:S(2)}) collective-permute-start(bf16[6,80,128]{2,1,0:T(8,128)(2,1)S(1)} %get-tuple-element.56), channel_id=1, source_target_pairs={{0,32},{32,64},{64,96},{96,128},{128,160},{160,192},{192,224},{1,3... | collective-permute-start | bytes 368648 | tf_op jit(solution)/shard_map/ppermute | solution.py:391
  55.8 0.5 collective-permute-done.6.refs_6_
  56.3 0.6 copy-done.15
  56.9 0.5 collective-permute-done.7.refs_7_
  57.4 0.6 copy-done.17
  58.1 1.4 %all-to-all-done = f32[256,1,128]{2,1,0:T(1,128)S(1)} async-done(((f32[256,1,128]{2,1,0:T(1,128)}), f32[256,1,128]{2,1,0:T(1,128)S(1)}, u32[]{:S(2)}, u32[]{:S(2)}) %all-to-all-start) | async-done | bytes 131104 | tf_op jit(solution)/shard_map/all_to_all | solution.py:421
  59.5 0.9 copy-done.2
  60.4 1.0 copy-done.6
  61.4 0.9 copy-done.9
  62.2 0.9 copy-done.12
  63.1 0.9 copy-done.16
  64.0 0.9 copy-done.18
  64.9 4.3 %shard_map.147 = (f32[8,80,128]{2,1,0:T(8,128)S(1)}, f32[8,80,128]{2,1,0:T(8,128)S(1)}, f32[256,128]{1,0:T(8,128)S(1)}) custom-call(s32[1,128]{1,0:T(1,128)S(1)} %get-tuple-element.34.refs_0_, f32[1,128]{1,0:T(1,128)S(1)} %get-tuple-element.33.refs_1_.step_ref, f32[256,128]{1,0:T(8,128)S(1)} %bitcast.20, f32[8,80,128]{2,1,0:T(8,128)S(1)} %get-tuple-element.50.x_ref.refs_3_, ...), custom_call_target="tpu_custom_call" | custom-call | tf_op jit(solution)/shard_map/pallas_call | solution.py:34
  69.3 28.9 %all_to_all.22 = f32[256,1,128]{2,1,0:T(1,128)S(1)} all-to-all(f32[256,1,128]{2,1,0:T(1,128)S(1)} %bitcast.27), channel_id=1, replica_groups=mesh['tm_0'=4,'tm_1'=2,'lon_0'=2,'lon_1'=8,'lon_2'=2] {'tm_0','tm_1','lo..., dimensions={0} | all-to-all | bytes 262144 | tf_op jit(solution)/shard_map/all_to_all | solution.py:424
  98.1 1.2 %shard_map.148 = (f32[2,8,64,80]{3,2,1,0:T(8,128)}, f32[1,2]{1,0:T(1,128)}) custom-call(f32[1,128]{1,0:T(1,128)S(1)} %get-tuple-element.33.refs_1_.step_ref, f32[256,128]{1,0:T(8,128)S(1)} %bitcast.21, f32[256,128]{1,0:T(8,128)S(1)} %bitcast.22, f32[8,80,128]{2,1,0:T(8,128)S(1)} %get-tuple-element.60.x_ref, f32[8,80,128]{2,1,0:T(8,128)S(1)} %get-tuple-element.61.g_ref), custom_call_target="tpu_custom_call" | custom-call | tf_op jit(solution)/shard_map/pallas_call | solution.py:34
  (26 shorter events, 0.0 us)
Async XLA Ops:
  1.3 1.0 %copy-start = (f32[2,8,80,64]{2,3,1,0:T(8,128)S(1)}, f32[2,8,80,64]{2,3,1,0:T(8,128)}, u32[]{:S(2)}) copy-start(f32[2,8,80,64]{2,3,1,0:T(8,128)} %param.13) | copy-start | bytes 983044
  2.3 12.6 %copy-start.23 = (f32[2,256]{1,0:T(2,128)S(1)}, f32[2,256]{1,0:T(2,128)}, u32[]{:S(2)}) copy-start(f32[2,256]{1,0:T(2,128)} %refs_18_.1) | copy-start | bytes 6148
  2.3 12.6 %copy-start.24 = (s32[2,256]{1,0:T(2,128)S(1)}, s32[2,256]{1,0:T(2,128)}, u32[]{:S(2)}) copy-start(s32[2,256]{1,0:T(2,128)} %cell_ref.3) | copy-start | bytes 6148
  2.3 12.6 %copy-start.25 = (s32[2,256]{1,0:T(2,128)S(1)}, s32[2,256]{1,0:T(2,128)}, u32[]{:S(2)}) copy-start(s32[2,256]{1,0:T(2,128)} %chan_ref.3) | copy-start | bytes 6148
  2.3 12.7 %copy-start.26 = (f32[2,256]{1,0:T(2,128)S(1)}, f32[2,256]{1,0:T(2,128)}, u32[]{:S(2)}) copy-start(f32[2,256]{1,0:T(2,128)} %val_ref.3) | copy-start | bytes 6148
  2.3 13.6 %copy-start.4 = (bf16[80,2304]{1,0:T(8,128)(2,1)S(1)}, bf16[80,2304]{1,0:T(8,128)(2,1)}, u32[]{:S(2)}) copy-start(bf16[80,2304]{1,0:T(8,128)(2,1)} %c_ref.1) | copy-start | bytes 1105924
  2.5 13.4 %copy-start.3 = (bf16[256,720]{0,1:T(8,128)(2,1)S(1)}, bf16[256,720]{0,1:T(8,128)(2,1)}, u32[]{:S(2)}) copy-start(bf16[256,720]{0,1:T(8,128)(2,1)} %param.15) | copy-start | bytes 1105924
  2.6 4.6 %collective-permute-start = (bf16[4,80,128]{2,1,0:T(8,128)(2,1)S(1)}, bf16[4,80,128]{2,1,0:T(8,128)(2,1)S(1)}, u32[]{:S(2)}, u32[]{:S(2)}) collective-permute-start(bf16[4,80,128]{2,1,0:T(8,128)(2,1)S(1)} %get-tuple-element.36.b_ref), channel_id=1, source_target_pairs={{0,1},{1,2},{2,3},{3,4},{4,5},{5,6},{6,7},{7,8},{8,9},{9,10},{10,1... | collective-permute-start | bytes 245768 | tf_op jit(solution)/shard_map/ppermute | solution.py:391
  5.6 10.3 %copy-start.13 = (f32[8,80,64]{1,2,0:T(8,128)S(1)}, f32[8,80,64]{1,2,0:T(8,128)}, u32[]{:S(2)}) copy-start(f32[8,80,64]{1,2,0:T(8,128)} %param.14) | copy-start | bytes 491524
  5.6 3.9 %collective-permute-start.1 = (bf16[4,80,128]{2,1,0:T(8,128)(2,1)S(1)}, bf16[4,80,128]{2,1,0:T(8,128)(2,1)S(1)}, u32[]{:S(2)}, u32[]{:S(2)}) collective-permute-start(bf16[4,80,128]{2,1,0:T(8,128)(2,1)S(1)} %get-tuple-element.37.a_ref), channel_id=1, source_target_pairs={{0,31},{1,0},{2,1},{3,2},{4,3},{5,4},{6,5},{7,6},{8,7},{9,8},{10,9... | collective-permute-start | bytes 245768 | tf_op jit(solution)/shard_map/ppermute | solution.py:391
  9.7 7.5 %collective-permute-start.2 = (bf16[6,80,128]{2,1,0:T(8,128)(2,1)S(1)}, bf16[6,80,128]{2,1,0:T(8,128)(2,1)S(1)}, u32[]{:S(2)}, u32[]{:S(2)}) collective-permute-start(bf16[6,80,128]{2,1,0:T(8,128)(2,1)S(1)} %get-tuple-element.38), channel_id=1, source_target_pairs={{32,0},{64,32},{96,64},{128,96},{160,128},{192,160},{224,192},{33,... | collective-permute-start | bytes 368648 | tf_op jit(solution)/shard_map/ppermute | solution.py:391
  11.0 6.2 %collective-permute-start.3 = (bf16[6,80,128]{2,1,0:T(8,128)(2,1)S(1)}, bf16[6,80,128]{2,1,0:T(8,128)(2,1)S(1)}, u32[]{:S(2)}, u32[]{:S(2)}) collective-permute-start(bf16[6,80,128]{2,1,0:T(8,128)(2,1)S(1)} %get-tuple-element.39), channel_id=1, source_target_pairs={{0,32},{32,64},{64,96},{96,128},{128,160},{160,192},{192,224},{1,3... | collective-permute-start | bytes 368648 | tf_op jit(solution)/shard_map/ppermute | solution.py:391
  15.0 1.0 %copy-start.29 = (f32[80]{0:T(128)S(1)}, f32[80]{0:T(128)}, u32[]{:S(2)}) copy-start(f32[80]{0:T(128)} %param.19) | copy-start | bytes 964
  15.0 1.0 %copy-start.30 = (f32[80]{0:T(128)S(1)}, f32[80]{0:T(128)}, u32[]{:S(2)}) copy-start(f32[80]{0:T(128)} %param.20) | copy-start | bytes 964
  15.9 0.7 copy-start.27
  16.0 0.7 copy-start.28
  17.1 4.2 %copy-start.1 = (f32[3,80,128]{2,1,0:T(8,128)}, f32[3,80,128]{2,1,0:T(8,128)S(1)}, u32[]{:S(2)}) copy-start(f32[3,80,128]{2,1,0:T(8,128)S(1)} %get-tuple-element.48.refs_15_.refs_24_) | copy-start | bytes 368644
  21.3 6.4 %copy-start.14 = (f32[256,128]{1,0:T(8,128)}, f32[256,128]{1,0:T(8,128)S(1)}, u32[]{:S(2)}) copy-start(f32[256,128]{1,0:T(8,128)S(1)} %get-tuple-element.54) | copy-start | bytes 393220
  21.3 6.4 %copy-start.19 = (bf16[4,80,128]{2,1,0:T(8,128)(2,1)}, bf16[4,80,128]{2,1,0:T(8,128)(2,1)S(1)}, u32[]{:S(2)}) copy-start(bf16[4,80,128]{2,1,0:T(8,128)(2,1)S(1)} %get-tuple-element.53.a_ref) | copy-start | bytes 245764
  21.3 6.4 %copy-start.21 = (bf16[4,80,128]{2,1,0:T(8,128)(2,1)}, bf16[4,80,128]{2,1,0:T(8,128)(2,1)S(1)}, u32[]{:S(2)}) copy-start(bf16[4,80,128]{2,1,0:T(8,128)(2,1)S(1)} %get-tuple-element.52.b_ref) | copy-start | bytes 245764
  21.3 7.2 %collective-permute-start.4 = (bf16[4,80,128]{2,1,0:T(8,128)(2,1)S(1)}, bf16[4,80,128]{2,1,0:T(8,128)(2,1)S(1)}, u32[]{:S(2)}, u32[]{:S(2)}) collective-permute-start(bf16[4,80,128]{2,1,0:T(8,128)(2,1)S(1)} %get-tuple-element.52.b_ref), channel_id=1, source_target_pairs={{0,1},{1,2},{2,3},{3,4},{4,5},{5,6},{6,7},{7,8},{8,9},{9,10},{10,1... | collective-permute-start | bytes 245768 | tf_op jit(solution)/shard_map/ppermute | solution.py:391
  22.7 6.4 %collective-permute-start.5 = (bf16[4,80,128]{2,1,0:T(8,128)(2,1)S(1)}, bf16[4,80,128]{2,1,0:T(8,128)(2,1)S(1)}, u32[]{:S(2)}, u32[]{:S(2)}) collective-permute-start(bf16[4,80,128]{2,1,0:T(8,128)(2,1)S(1)} %get-tuple-element.53.a_ref), channel_id=1, source_target_pairs={{0,31},{1,0},{2,1},{3,2},{4,3},{5,4},{6,5},{7,6},{8,7},{9,8},{10,9... | collective-permute-start | bytes 245768 | tf_op jit(solution)/shard_map/ppermute | solution.py:391
  27.8 0.7 copy-start.5
  28.5 0.6 copy-start.7
  29.1 0.6 copy-start.10
  29.8 29.7 %all-to-all-start = ((f32[256,1,128]{2,1,0:T(1,128)}), f32[256,1,128]{2,1,0:T(1,128)S(1)}, u32[]{:S(2)}, u32[]{:S(2)}) async-start(f32[256,1,128]{2,1,0:T(1,128)} %bitcast.26), calls=%async_computation | async-start | bytes 262144 | tf_op jit(solution)/shard_map/all_to_all | solution.py:421
  46.6 0.9 copy-start.8
  47.5 0.9 copy-start.11
  48.4 0.9 copy-start.20
  49.3 0.9 copy-start.22
  50.3 6.0 %collective-permute-start.6 = (bf16[6,80,128]{2,1,0:T(8,128)(2,1)S(1)}, bf16[6,80,128]{2,1,0:T(8,128)(2,1)S(1)}, u32[]{:S(2)}, u32[]{:S(2)}) collective-permute-start(bf16[6,80,128]{2,1,0:T(8,128)(2,1)S(1)} %get-tuple-element.55), channel_id=1, source_target_pairs={{32,0},{64,32},{96,64},{128,96},{160,128},{192,160},{224,192},{33,... | collective-permute-start | bytes 368648 | tf_op jit(solution)/shard_map/ppermute | solution.py:391
  51.6 5.8 %collective-permute-start.7 = (bf16[6,80,128]{2,1,0:T(8,128)(2,1)S(1)}, bf16[6,80,128]{2,1,0:T(8,128)(2,1)S(1)}, u32[]{:S(2)}, u32[]{:S(2)}) collective-permute-start(bf16[6,80,128]{2,1,0:T(8,128)(2,1)S(1)} %get-tuple-element.56), channel_id=1, source_target_pairs={{0,32},{32,64},{64,96},{96,128},{128,160},{160,192},{192,224},{1,3... | collective-permute-start | bytes 368648 | tf_op jit(solution)/shard_map/ppermute | solution.py:391
  56.3 0.6 copy-start.15
  57.4 0.7 copy-start.17
  59.5 0.9 copy-start.2
  60.4 1.0 copy-start.6
  61.4 0.9 copy-start.9
  62.2 0.9 copy-start.12
  63.1 0.9 copy-start.16
  64.0 0.9 copy-start.18
where the time goes:
time: 100 us; the launch traced here: 99.4 us
  starting transfers between devices  36.5 us (36%)
  blocking collectives  28.9 us (29%)
  local copies, waits for them, and re-layouts  14 us (14%)
  Pallas kernels  12.4 us (12%)
  waiting for transfers between devices  6.01 us (6%)
  between operations  1.63 us (2%)
    all_to_all x1, blocking collectives, per_device(): sums1 = lax.all_to_all(row, TM_LON, 0, 0, tiled=True)  28.9 us
    ppermute x8, starting transfers between devices, shifted(): return lax.ppermute(value, axes, pairs)  19.6 us
    all_to_all x1, starting transfers between devices, per_device(): sums0 = lax.all_to_all(row, TM_LON, 0, 0, tiled=True)  16.8 us
    unnamed x62, local copies, waits for them, and re-layouts  14 us
    pallas_call x9, Pallas kernels, call(): pl.pallas_call(kernel, out_shape=tuple((jax.ShapeDtypeStruct(shape, dtype...  12.4 us
    ppermute x8, waiting for transfers between devices, shifted(): return lax.ppermute(value, axes, pairs)  4.62 us
  transfers between devices with their start and end apart: 9, of which 5 were waited for; matrix products, arithmetic and copies ran while one was open for 0% of the time, Pallas kernels for 2%

commit v1 on v0

--- a/solution.py
+++ b/solution.py
@@ -397,7 +397,7 @@
     up, down = strips(from_left, mine_left, mine_right, from_right)
     after = shifted(up, TM, -1, False)
     before = shifted(down, TM, 1, False)
-    return from_left, from_right, after, before
+    return (from_left, from_right, after, before), up
 
 
 def per_device(x, background, opening, b1, closing, b2, mw, bw, cell, chan, val, wt, step):
@@ -407,7 +407,7 @@
     place = lax.axis_index(TM).astype(jnp.int32)[None]
     step = step[None]
     xp, xl, xr, place, step = pack(place, step, jnp.swapaxes(x, 2, 3))
-    halo = exchange(xl, xr)
+    halo, _ = exchange(xl, xr)
     o, k2, wia, woa, bias, small, bgp = prepare_weights(
         opening.T, closing, b1, b2, mw, bw, jnp.swapaxes(background, 1, 2)
     )
@@ -415,10 +415,10 @@
     consts = (bgp, wt, o, k2, wia, woa, bias, small)
     base = (xp,) + halo + (r0, s0)
     g0, gl, gr, row = gradient(total, n_tm, n_all, (place,) + base + consts, False)
-    ghalo = exchange(gl, gr)
-    rg, sg = observe(cell, chan, val, wt, g0, True)
-    row, rg, _, _ = lax.optimization_barrier((row, rg) + ghalo[:2])
     sums0 = lax.all_to_all(row, TM_LON, 0, 0, tiled=True)
+    ghalo, up = exchange(gl, gr)
+    later_g0, _ = lax.optimization_barrier((g0, up))
+    rg, sg = observe(cell, chan, val, wt, later_g0, True)
     ins = (place, step, sums0, g0) + ghalo + (rg, sg) + base + consts
     g1, x1, row = gradient(total, n_tm, n_all, ins, True)
     sums1 = lax.all_to_all(row, TM_LON, 0, 0, tiled=True)

time: 100 us -> 97.9 us (0.979)
  starting transfers between devices: 36.5 us -> 32.9 us
  waiting for transfers between devices: 6.01 us -> 9.41 us
  blocking collectives: 28.9 us -> 27.7 us
    ppermute x8, waiting for transfers between devices: 4.62 us -> 9.41 us  [shifted(): return lax.ppermute(value, axes, pairs)]
    ppermute x8, starting transfers between devices: 19.6 us -> 15.5 us  [shifted(): return lax.ppermute(value, axes, pairs)]
    all_to_all x1, waiting for transfers between devices: 1.39 us -> 0.01 us  [per_device(): sums0 = lax.all_to_all(row, TM_LON, 0, 0, tiled=True)]
    all_to_all x1, blocking collectives: 28.9 us -> 27.7 us  [per_device(): sums1 = lax.all_to_all(row, TM_LON, 0, 0, tiled=True)]
    unnamed x62 -> x58, local copies, waits for them, and re-layouts: 14 us -> 13.3 us
where the time goes in v1:
time: 97.9 us; the launch traced here: 97.3 us
  starting transfers between devices  32.9 us (34%)
  blocking collectives  27.7 us (28%)
  local copies, waits for them, and re-layouts  13.3 us (14%)
  Pallas kernels  12.4 us (13%)
  waiting for transfers between devices  9.41 us (10%)
  between operations  1.59 us (2%)
    all_to_all x1, blocking collectives, per_device(): sums1 = lax.all_to_all(row, TM_LON, 0, 0, tiled=True)  27.7 us
    all_to_all x1, starting transfers between devices, per_device(): sums0 = lax.all_to_all(row, TM_LON, 0, 0, tiled=True)  17.3 us
    ppermute x8, starting transfers between devices, shifted(): return lax.ppermute(value, axes, pairs)  15.5 us
    unnamed x58, local copies, waits for them, and re-layouts  13.3 us
    pallas_call x9, Pallas kernels, call(): pl.pallas_call(kernel, out_shape=tuple((jax.ShapeDtypeStruct(shape, dtype...  12.4 us
    ppermute x8, waiting for transfers between devices, shifted(): return lax.ppermute(value, axes, pairs)  9.41 us
  transfers between devices with their start and end apart: 9, of which 5 were waited for; matrix products, arithmetic and copies ran while one was open for 0% of the time, Pallas kernels for 2%

profile of v1, /device:TPU:1, one launch (start us, length us, event | category | flops | bytes accessed | tf_op | source)
XLA Modules:
  0.0 97.3 jit_solution(9761139653640337462)
XLA Ops:
  1.3 0.0 copy-start
  1.3 1.0 %copy-done = f32[2,8,80,64]{2,3,1,0:T(8,128)S(1)} copy-done((f32[2,8,80,64]{2,3,1,0:T(8,128)S(1)}, f32[2,8,80,64]{2,3,1,0:T(8,128)}, u32[]{:S(2)}) %copy-start) | copy-done | bytes 327704
  2.3 0.0 copy-start.4
  2.3 0.2 shard_map.140
  2.5 0.0 copy-start.3
  2.6 3.1 %collective-permute-start = (bf16[4,80,128]{2,1,0:T(8,128)(2,1)S(1)}, bf16[4,80,128]{2,1,0:T(8,128)(2,1)S(1)}, u32[]{:S(2)}, u32[]{:S(2)}) collective-permute-start(bf16[4,80,128]{2,1,0:T(8,128)(2,1)S(1)} %get-tuple-element.35.b_ref), channel_id=1, source_target_pairs={{0,1},{1,2},{2,3},{3,4},{4,5},{5,6},{6,7},{7,8},{8,9},{9,10},{10,1... | collective-permute-start | bytes 245768 | tf_op jit(solution)/shard_map/ppermute | solution.py:391
  5.6 0.3 collective-permute-start.1
  5.9 1.2 %collective-permute-done.l_ref.refs_2_.refs_11_ = bf16[4,80,128]{2,1,0:T(8,128)(2,1)S(1)} collective-permute-done((bf16[4,80,128]{2,1,0:T(8,128)(2,1)S(1)}, bf16[4,80,128]{2,1,0:T(8,128)(2,1)S(1)}, u32[]{:S(2)}, u32[]{:S(2)}) %collective-permute-start) | collective-permute-done | bytes 81952 | tf_op jit(solution)/shard_map/ppermute | solution.py:391
  7.1 2.4 %collective-permute-done.1.r_ref.refs_3_.refs_12_ = bf16[4,80,128]{2,1,0:T(8,128)(2,1)S(1)} collective-permute-done((bf16[4,80,128]{2,1,0:T(8,128)(2,1)S(1)}, bf16[4,80,128]{2,1,0:T(8,128)(2,1)S(1)}, u32[]{:S(2)}, u32[]{:S(2)}) %collective-permute-start.1) | collective-permute-done | bytes 81952 | tf_op jit(solution)/shard_map/ppermute | solution.py:391
  9.5 0.1 shard_map.141
  9.7 1.3 %collective-permute-start.2 = (bf16[6,80,128]{2,1,0:T(8,128)(2,1)S(1)}, bf16[6,80,128]{2,1,0:T(8,128)(2,1)S(1)}, u32[]{:S(2)}, u32[]{:S(2)}) collective-permute-start(bf16[6,80,128]{2,1,0:T(8,128)(2,1)S(1)} %get-tuple-element.37), channel_id=1, source_target_pairs={{32,0},{64,32},{96,64},{128,96},{160,128},{192,160},{224,192},{33,... | collective-permute-start | bytes 368648 | tf_op jit(solution)/shard_map/ppermute | solution.py:391
  11.0 4.0 %collective-permute-start.3 = (bf16[6,80,128]{2,1,0:T(8,128)(2,1)S(1)}, bf16[6,80,128]{2,1,0:T(8,128)(2,1)S(1)}, u32[]{:S(2)}, u32[]{:S(2)}) collective-permute-start(bf16[6,80,128]{2,1,0:T(8,128)(2,1)S(1)} %get-tuple-element.38), channel_id=1, source_target_pairs={{0,32},{32,64},{64,96},{96,128},{128,160},{160,192},{192,224},{1,3... | collective-permute-start | bytes 368648 | tf_op jit(solution)/shard_map/ppermute | solution.py:391
  15.0 0.0 copy-done.21
  15.0 0.0 copy-done.22
  15.0 0.0 copy-done.23
  15.0 0.0 copy-done.24
  15.0 0.0 copy-start.27
  15.0 0.0 copy-start.28
  15.0 0.9 shard_map.142
  15.9 0.0 copy-start.25
  16.0 0.0 copy-start.26
  16.0 0.0 copy-done.4
  16.0 0.0 copy-done.3
  16.0 0.0 copy-done.11
  16.0 0.0 copy-done.27
  16.0 0.0 copy-done.28
  16.0 0.6 copy-done.25
  16.6 0.5 shard_map.143
  17.1 0.0 collective-permute-done.2.refs_4_.refs_13_
  17.1 0.0 collective-permute-done.3.refs_5_.refs_14_
  17.1 4.1 %shard_map.144 = (f32[8,80,128]{2,1,0:T(8,128)S(1)}, bf16[4,80,128]{2,1,0:T(8,128)(2,1)S(1)}, bf16[4,80,128]{2,1,0:T(8,128)(2,1)S(1)}, f32[256,128]{1,0:T(8,128)S(1)}) custom-call(s32[1,128]{1,0:T(1,128)S(1)} %get-tuple-element.33.refs_0_, f32[8,80,128]{2,1,0:T(8,128)S(1)} %get-tuple-element.34.x_ref.refs_1_.refs_10_, ...), custom_call_target="tpu_custom_call" | custom-call | tf_op jit(solution)/shard_map/pallas_call | solution.py:34
  21.3 0.0 copy-done.1
  21.3 0.0 copy-start.12
  21.3 0.6 copy-done.12
  21.9 0.6 copy-done.17
  22.6 0.6 copy-done.19
  23.2 17.3 %all-to-all-start = ((f32[256,1,128]{2,1,0:T(1,128)}), f32[256,1,128]{2,1,0:T(1,128)S(1)}, u32[]{:S(2)}, u32[]{:S(2)}) async-start(f32[256,1,128]{2,1,0:T(1,128)} %bitcast.26), calls=%async_computation | async-start | bytes 262144 | tf_op jit(solution)/shard_map/all_to_all | solution.py:418
  40.6 1.8 %collective-permute-start.4 = (bf16[4,80,128]{2,1,0:T(8,128)(2,1)}, bf16[4,80,128]{2,1,0:T(8,128)(2,1)S(1)}, u32[]{:S(2)}, u32[]{:S(2)}) collective-permute-start(bf16[4,80,128]{2,1,0:T(8,128)(2,1)} %copy-done.19), channel_id=1, source_target_pairs={{0,1},{1,2},{2,3},{3,4},{4,5},{5,6},{6,7},{7,8},{8,9},{9,10},{10,1... | collective-permute-start | bytes 245768 | tf_op jit(solution)/shard_map/ppermute | solution.py:391
  42.4 0.5 collective-permute-start.5
  42.9 1.8 %collective-permute-done.4.l_ref.refs_4_ = bf16[4,80,128]{2,1,0:T(8,128)(2,1)S(1)} collective-permute-done((bf16[4,80,128]{2,1,0:T(8,128)(2,1)}, bf16[4,80,128]{2,1,0:T(8,128)(2,1)S(1)}, u32[]{:S(2)}, u32[]{:S(2)}) %collective-permute-start.4) | collective-permute-done | bytes 81952 | tf_op jit(solution)/shard_map/ppermute | solution.py:391
  44.7 2.2 %collective-permute-done.5.r_ref.refs_5_ = bf16[4,80,128]{2,1,0:T(8,128)(2,1)S(1)} collective-permute-done((bf16[4,80,128]{2,1,0:T(8,128)(2,1)}, bf16[4,80,128]{2,1,0:T(8,128)(2,1)S(1)}, u32[]{:S(2)}, u32[]{:S(2)}) %collective-permute-start.5) | collective-permute-done | bytes 81952 | tf_op jit(solution)/shard_map/ppermute | solution.py:391
  46.8 0.9 copy-done.18
  47.7 0.9 copy-done.20
  48.6 0.1 shard_map.145
  48.8 0.5 copy-done.9
  49.3 3.1 %collective-permute-start.7 = (bf16[6,80,128]{2,1,0:T(8,128)(2,1)S(1)}, bf16[6,80,128]{2,1,0:T(8,128)(2,1)S(1)}, u32[]{:S(2)}, u32[]{:S(2)}) collective-permute-start(bf16[6,80,128]{2,1,0:T(8,128)(2,1)S(1)} %get-tuple-element.53), channel_id=1, source_target_pairs={{0,32},{32,64},{64,96},{96,128},{128,160},{160,192},{192,224},{1,3... | collective-permute-start | bytes 368648 | tf_op jit(solution)/shard_map/ppermute | solution.py:391
  52.4 1.5 %collective-permute-start.6 = (bf16[6,80,128]{2,1,0:T(8,128)(2,1)S(1)}, bf16[6,80,128]{2,1,0:T(8,128)(2,1)S(1)}, u32[]{:S(2)}, u32[]{:S(2)}) collective-permute-start(bf16[6,80,128]{2,1,0:T(8,128)(2,1)S(1)} %get-tuple-element.52), channel_id=1, source_target_pairs={{32,0},{64,32},{96,64},{128,96},{160,128},{192,160},{224,192},{33,... | collective-permute-start | bytes 368648 | tf_op jit(solution)/shard_map/ppermute | solution.py:391
  53.8 0.9 shard_map.146
  54.7 0.0 copy-start.5
  54.8 0.7 copy-done.5
  55.5 0.0 collective-permute-done.7.refs_7_
  55.5 0.7 copy-done.13
  56.1 1.9 %collective-permute-done.6.refs_6_ = bf16[6,80,128]{2,1,0:T(8,128)(2,1)S(1)} collective-permute-done((bf16[6,80,128]{2,1,0:T(8,128)(2,1)S(1)}, bf16[6,80,128]{2,1,0:T(8,128)(2,1)S(1)}, u32[]{:S(2)}, u32[]{:S(2)}) %collective-permute-start.6) | collective-permute-done | bytes 122912 | tf_op jit(solution)/shard_map/ppermute | solution.py:391
  58.0 0.6 copy-done.15
  58.6 0.0 all-to-all-done
  58.6 0.9 copy-done.2
  59.5 1.0 copy-done.6
  60.5 0.9 copy-done.8
  61.4 0.9 copy-done.10
  62.3 0.9 copy-done.14
  63.2 0.9 copy-done.16
  64.1 4.3 %shard_map.147 = (f32[8,80,128]{2,1,0:T(8,128)S(1)}, f32[8,80,128]{2,1,0:T(8,128)S(1)}, f32[256,128]{1,0:T(8,128)S(1)}) custom-call(s32[1,128]{1,0:T(1,128)S(1)} %get-tuple-element.33.refs_0_, f32[1,128]{1,0:T(1,128)S(1)} %get-tuple-element.32.refs_1_.step_ref, f32[256,128]{1,0:T(8,128)S(1)} %bitcast.20, f32[8,80,128]{2,1,0:T(8,128)S(1)} %get-tuple-element.54.x_ref.refs_3_, ...), custom_call_target="tpu_custom_call" | custom-call | tf_op jit(solution)/shard_map/pallas_call | solution.py:34
  68.4 27.7 %all_to_all.22 = f32[256,1,128]{2,1,0:T(1,128)S(1)} all-to-all(f32[256,1,128]{2,1,0:T(1,128)S(1)} %bitcast.27), channel_id=1, replica_groups=mesh['tm_0'=4,'tm_1'=2,'lon_0'=2,'lon_1'=8,'lon_2'=2] {'tm_0','tm_1','lo..., dimensions={0} | all-to-all | bytes 262144 | tf_op jit(solution)/shard_map/all_to_all | solution.py:424
  96.1 1.2 %shard_map.148 = (f32[2,8,64,80]{3,2,1,0:T(8,128)}, f32[1,2]{1,0:T(1,128)}) custom-call(f32[1,128]{1,0:T(1,128)S(1)} %get-tuple-element.32.refs_1_.step_ref, f32[256,128]{1,0:T(8,128)S(1)} %bitcast.21, f32[256,128]{1,0:T(8,128)S(1)} %bitcast.22, f32[8,80,128]{2,1,0:T(8,128)S(1)} %get-tuple-element.58.x_ref, f32[8,80,128]{2,1,0:T(8,128)S(1)} %get-tuple-element.59.g_ref), custom_call_target="tpu_custom_call" | custom-call | tf_op jit(solution)/shard_map/pallas_call | solution.py:34
  (22 shorter events, 0.0 us)
Async XLA Ops:
  1.3 1.0 %copy-start = (f32[2,8,80,64]{2,3,1,0:T(8,128)S(1)}, f32[2,8,80,64]{2,3,1,0:T(8,128)}, u32[]{:S(2)}) copy-start(f32[2,8,80,64]{2,3,1,0:T(8,128)} %param.13) | copy-start | bytes 983044
  2.3 12.6 %copy-start.21 = (f32[2,256]{1,0:T(2,128)S(1)}, f32[2,256]{1,0:T(2,128)}, u32[]{:S(2)}) copy-start(f32[2,256]{1,0:T(2,128)} %refs_18_.1) | copy-start | bytes 6148
  2.3 12.6 %copy-start.22 = (s32[2,256]{1,0:T(2,128)S(1)}, s32[2,256]{1,0:T(2,128)}, u32[]{:S(2)}) copy-start(s32[2,256]{1,0:T(2,128)} %cell_ref.3) | copy-start | bytes 6148
  2.3 12.6 %copy-start.23 = (s32[2,256]{1,0:T(2,128)S(1)}, s32[2,256]{1,0:T(2,128)}, u32[]{:S(2)}) copy-start(s32[2,256]{1,0:T(2,128)} %chan_ref.3) | copy-start | bytes 6148
  2.3 12.7 %copy-start.24 = (f32[2,256]{1,0:T(2,128)S(1)}, f32[2,256]{1,0:T(2,128)}, u32[]{:S(2)}) copy-start(f32[2,256]{1,0:T(2,128)} %val_ref.3) | copy-start | bytes 6148
  2.3 13.6 %copy-start.4 = (bf16[80,2304]{1,0:T(8,128)(2,1)S(1)}, bf16[80,2304]{1,0:T(8,128)(2,1)}, u32[]{:S(2)}) copy-start(bf16[80,2304]{1,0:T(8,128)(2,1)} %c_ref.1) | copy-start | bytes 1105924
  2.5 13.4 %copy-start.3 = (bf16[256,720]{0,1:T(8,128)(2,1)S(1)}, bf16[256,720]{0,1:T(8,128)(2,1)}, u32[]{:S(2)}) copy-start(bf16[256,720]{0,1:T(8,128)(2,1)} %param.15) | copy-start | bytes 1105924
  2.6 4.6 %collective-permute-start = (bf16[4,80,128]{2,1,0:T(8,128)(2,1)S(1)}, bf16[4,80,128]{2,1,0:T(8,128)(2,1)S(1)}, u32[]{:S(2)}, u32[]{:S(2)}) collective-permute-start(bf16[4,80,128]{2,1,0:T(8,128)(2,1)S(1)} %get-tuple-element.35.b_ref), channel_id=1, source_target_pairs={{0,1},{1,2},{2,3},{3,4},{4,5},{5,6},{6,7},{7,8},{8,9},{9,10},{10,1... | collective-permute-start | bytes 245768 | tf_op jit(solution)/shard_map/ppermute | solution.py:391
  5.6 10.3 %copy-start.11 = (f32[8,80,64]{1,2,0:T(8,128)S(1)}, f32[8,80,64]{1,2,0:T(8,128)}, u32[]{:S(2)}) copy-start(f32[8,80,64]{1,2,0:T(8,128)} %param.14) | copy-start | bytes 491524
  5.6 3.9 %collective-permute-start.1 = (bf16[4,80,128]{2,1,0:T(8,128)(2,1)S(1)}, bf16[4,80,128]{2,1,0:T(8,128)(2,1)S(1)}, u32[]{:S(2)}, u32[]{:S(2)}) collective-permute-start(bf16[4,80,128]{2,1,0:T(8,128)(2,1)S(1)} %get-tuple-element.36.a_ref), channel_id=1, source_target_pairs={{0,31},{1,0},{2,1},{3,2},{4,3},{5,4},{6,5},{7,6},{8,7},{9,8},{10,9... | collective-permute-start | bytes 245768 | tf_op jit(solution)/shard_map/ppermute | solution.py:391
  9.7 7.5 %collective-permute-start.2 = (bf16[6,80,128]{2,1,0:T(8,128)(2,1)S(1)}, bf16[6,80,128]{2,1,0:T(8,128)(2,1)S(1)}, u32[]{:S(2)}, u32[]{:S(2)}) collective-permute-start(bf16[6,80,128]{2,1,0:T(8,128)(2,1)S(1)} %get-tuple-element.37), channel_id=1, source_target_pairs={{32,0},{64,32},{96,64},{128,96},{160,128},{192,160},{224,192},{33,... | collective-permute-start | bytes 368648 | tf_op jit(solution)/shard_map/ppermute | solution.py:391
  11.0 6.2 %collective-permute-start.3 = (bf16[6,80,128]{2,1,0:T(8,128)(2,1)S(1)}, bf16[6,80,128]{2,1,0:T(8,128)(2,1)S(1)}, u32[]{:S(2)}, u32[]{:S(2)}) collective-permute-start(bf16[6,80,128]{2,1,0:T(8,128)(2,1)S(1)} %get-tuple-element.38), channel_id=1, source_target_pairs={{0,32},{32,64},{64,96},{96,128},{128,160},{160,192},{192,224},{1,3... | collective-permute-start | bytes 368648 | tf_op jit(solution)/shard_map/ppermute | solution.py:391
  15.0 1.0 %copy-start.27 = (f32[80]{0:T(128)S(1)}, f32[80]{0:T(128)}, u32[]{:S(2)}) copy-start(f32[80]{0:T(128)} %param.19) | copy-start | bytes 964
  15.0 1.0 %copy-start.28 = (f32[80]{0:T(128)S(1)}, f32[80]{0:T(128)}, u32[]{:S(2)}) copy-start(f32[80]{0:T(128)} %param.20) | copy-start | bytes 964
  15.9 0.7 copy-start.25
  16.0 0.7 copy-start.26
  17.1 4.2 %copy-start.1 = (f32[3,80,128]{2,1,0:T(8,128)}, f32[3,80,128]{2,1,0:T(8,128)S(1)}, u32[]{:S(2)}) copy-start(f32[3,80,128]{2,1,0:T(8,128)S(1)} %get-tuple-element.47.refs_15_.refs_24_) | copy-start | bytes 368644
  21.3 0.7 copy-start.12
  21.9 0.6 copy-start.17
  22.6 0.6 copy-start.19
  23.2 35.4 %all-to-all-start = ((f32[256,1,128]{2,1,0:T(1,128)}), f32[256,1,128]{2,1,0:T(1,128)S(1)}, u32[]{:S(2)}, u32[]{:S(2)}) async-start(f32[256,1,128]{2,1,0:T(1,128)} %bitcast.26), calls=%async_computation | async-start | bytes 262144 | tf_op jit(solution)/shard_map/all_to_all | solution.py:418
  40.6 4.1 %collective-permute-start.4 = (bf16[4,80,128]{2,1,0:T(8,128)(2,1)}, bf16[4,80,128]{2,1,0:T(8,128)(2,1)S(1)}, u32[]{:S(2)}, u32[]{:S(2)}) collective-permute-start(bf16[4,80,128]{2,1,0:T(8,128)(2,1)} %copy-done.19), channel_id=1, source_target_pairs={{0,1},{1,2},{2,3},{3,4},{4,5},{5,6},{6,7},{7,8},{8,9},{9,10},{10,1... | collective-permute-start | bytes 245768 | tf_op jit(solution)/shard_map/ppermute | solution.py:391
  42.4 4.5 %collective-permute-start.5 = (bf16[4,80,128]{2,1,0:T(8,128)(2,1)}, bf16[4,80,128]{2,1,0:T(8,128)(2,1)S(1)}, u32[]{:S(2)}, u32[]{:S(2)}) collective-permute-start(bf16[4,80,128]{2,1,0:T(8,128)(2,1)} %copy-done.17), channel_id=1, source_target_pairs={{0,31},{1,0},{2,1},{3,2},{4,3},{5,4},{6,5},{7,6},{8,7},{9,8},{10,9... | collective-permute-start | bytes 245768 | tf_op jit(solution)/shard_map/ppermute | solution.py:391
  44.6 4.1 %copy-start.7 = (bf16[4,80,128]{2,1,0:T(8,128)(2,1)}, bf16[4,80,128]{2,1,0:T(8,128)(2,1)S(1)}, u32[]{:S(2)}) copy-start(bf16[4,80,128]{2,1,0:T(8,128)(2,1)S(1)} %collective-permute-done.4.l_ref.refs_4_) | copy-start | bytes 245764
  46.8 0.9 copy-start.18
  47.7 0.9 copy-start.20
  48.6 0.6 copy-start.9
  49.3 6.2 %collective-permute-start.7 = (bf16[6,80,128]{2,1,0:T(8,128)(2,1)S(1)}, bf16[6,80,128]{2,1,0:T(8,128)(2,1)S(1)}, u32[]{:S(2)}, u32[]{:S(2)}) collective-permute-start(bf16[6,80,128]{2,1,0:T(8,128)(2,1)S(1)} %get-tuple-element.53), channel_id=1, source_target_pairs={{0,32},{32,64},{64,96},{96,128},{128,160},{160,192},{192,224},{1,3... | collective-permute-start | bytes 368648 | tf_op jit(solution)/shard_map/ppermute | solution.py:391
  52.4 5.6 %collective-permute-start.6 = (bf16[6,80,128]{2,1,0:T(8,128)(2,1)S(1)}, bf16[6,80,128]{2,1,0:T(8,128)(2,1)S(1)}, u32[]{:S(2)}, u32[]{:S(2)}) collective-permute-start(bf16[6,80,128]{2,1,0:T(8,128)(2,1)S(1)} %get-tuple-element.52), channel_id=1, source_target_pairs={{32,0},{64,32},{96,64},{128,96},{160,128},{192,160},{224,192},{33,... | collective-permute-start | bytes 368648 | tf_op jit(solution)/shard_map/ppermute | solution.py:391
  54.7 0.7 copy-start.5
  55.5 0.7 copy-start.13
  58.0 0.6 copy-start.15
  58.6 0.9 copy-start.2
  59.5 1.0 copy-start.6
  60.5 0.9 copy-start.8
  61.4 0.9 copy-start.10
  62.3 0.9 copy-start.14
  63.2 0.9 copy-start.16

commit v2 on v1

--- a/solution.py
+++ b/solution.py
@@ -214,64 +214,32 @@
     return step[:, :1] / jnp.sqrt(norm / total + 1e-06)
 
 
-def gradient_kernel(total, second, n_tm, n_all):
+def forward_kernel(total, second):
     def kernel(*refs):
         refs = list(refs)
         take = lambda n: [refs.pop(0) for _ in range(n)]
-        (place_ref,) = take(1)
         if second:
-            step_ref, sums_ref = take(2)
-            g0_ref, glft, grgt, upp1, dwn1, r1_ref, s1_ref = take(7)
-        own_ref, lft, rgt, upp0, dwn0, r0_ref, s0_ref = take(7)
-        bg_ref, wt_ref, o_ref, k2_ref, wia_ref, woa_ref, bias_ref, small_ref = take(8)
-        if second:
-            g_ref, x1_ref, row_ref = take(3)
-        else:
-            g_ref, gl_ref, gr_ref, row_ref = take(4)
-        vx, hid, slope, vl, x_ext, x_prev, ln, gh = refs
-        place = place_ref[...]
-        left = lanes() < LAT
+            step_ref, sums_ref, g0_ref, glft, grgt = take(5)
+        own_ref, lft, rgt, o_ref, k2_ref, bias_ref, small_ref = take(7)
+        x_ref, m_ref, slope = take(3)
+        alpha_ref = take(1)[0] if second else None
+        vx, hid = refs
         if second:
             alpha = step_from(sums_ref[...], step_ref[...], total)
-
-            def upp(n):
-                return upp0[n].astype(F32) - alpha * upp1[n].astype(F32)
-
-            def dwn(n):
-                return dwn0[n].astype(F32) - alpha * dwn1[n].astype(F32)
-
-            def obs(n):
-                return s0_ref[n] - alpha * s1_ref[n]
-
-            for e in range(16):
-                v = lft[e] if e < HALO else own_ref[e - HALO] if e < HALO + BAND else rgt[e - HALO - BAND]
-                g = glft[e] if e < HALO else g0_ref[e - HALO] if e < HALO + BAND else grgt[e - HALO - BAND]
-                v = v.astype(F32) - alpha * g.astype(F32)
-                x_ext[e] = v
-                if HALO <= e < HALO + BAND:
-                    x1_ref[e - HALO] = v
-                stack_lats(vx, e, v)
-        else:
-
-            def upp(n):
-                return upp0[n].astype(F32)
-
-            def dwn(n):
-                return dwn0[n].astype(F32)
-
-            def obs(n):
-                return s0_ref[n]
-
-            for e in range(16):
-                v = lft[e] if e < HALO else own_ref[e - HALO] if e < HALO + BAND else rgt[e - HALO - BAND]
-                v = v.astype(F32)
-                x_ext[e] = v
-                stack_lats(vx, e, v)
+            alpha_ref[...] = jnp.broadcast_to(alpha, (1, W2))
+
+        def pick(e, one, two, three):
+            return one[e] if e < HALO else two[e - HALO] if e < HALO + BAND else three[e - HALO - BAND]
+
+        for e in range(16):
+            v = pick(e, lft, own_ref, rgt).astype(F32)
+            if second:
+                v = v - alpha * pick(e, glft, g0_ref, grgt).astype(F32)
+            if 2 <= e < 14:
+                x_ref[e - 2] = v
+            stack_lats(vx, e, v)
         bias = bias_ref[...]
         bias2 = jnp.concatenate([bias, bias], axis=1)
-        b2 = small_ref[0]
-        mw = small_ref[1]
-        bw = small_ref[2]
         for h in range(0, 14, 2):
             pre = dot(o_ref[...], window(vx, h, 3 * C)) + bias2
             act, sl = gelu_pair(pre)
@@ -283,15 +251,38 @@
         for o in range(0, 12, 2):
             s = sum_lats(dot(k2_ref[...], window(hid, o, F)))
             for k in range(2):
-                n = o + k
-                x = x_ext[n + 2]
-                m = x + s[k] + b2
-                u = upp(n % 6)
-                nxt = jnp.where(left, halves(x), u if n >= 6 else halves(u))
-                keep = left | (place < n_tm - 1)
-                lv = jnp.where(keep, mw * (nxt - m), 0.0)
-                ln[n] = lv
-                stack_lats(vl, n, lv)
+                m_ref[o + k] = x_ref[o + k] + s[k] + small_ref[0]
+
+    return kernel
+
+
+def forward(total, ins, second):
+    outs = [((12, C, W2), F32), ((12, C, W2), F32), ((10, F, W2), F32)] + ([((1, W2), F32)] if second else [])
+    scratch = [pltpu.VMEM((16 * 3 * C, W2), BF16), pltpu.VMEM((14 * F, W2), BF16)]
+    return call(forward_kernel(total, second), ins, outs, scratch, limit=16)
+
+
+def adjoint_kernel(second, n_tm):
+    def kernel(*refs):
+        refs = list(refs)
+        take = lambda n: [refs.pop(0) for _ in range(n)]
+        place_ref, x_ref, m_ref, slope, upp0 = take(5)
+        alpha_ref, upp1 = take(2) if second else (None, None)
+        woa_ref, wia_ref, small_ref = take(3)
+        pulled, held, vl, hid, ln = refs
+        place = place_ref[...]
+        left = lanes() < LAT
+        keep = left | (place < n_tm - 1)
+        for n in range(12):
+            u = upp0[n % 6].astype(F32)
+            if second:
+                u = u - alpha_ref[...] * upp1[n % 6].astype(F32)
+            nxt = jnp.where(left, halves(x_ref[n]), u if n >= 6 else halves(u))
+            lv = jnp.where(keep, small_ref[1] * (nxt - m_ref[n]), 0.0)
+            if 2 <= n < 10:
+                ln[n - 2] = lv
+                held[n - 2] = halves(lv)
+            stack_lats(vl, n, lv)
         for h in range(0, 10, 2):
             z = dot(woa_ref[...], window(vl, h, 3 * C))
             for k in range(2):
@@ -300,13 +291,44 @@
         for o in range(0, BAND, 2):
             s = sum_lats(dot(wia_ref[...], window(hid, o, F)))
             for k in range(2):
-                gh[o + k] = ln[o + k + 2] + s[k]
+                pulled[o + k] = ln[o + k] + s[k]
+
+    return kernel
+
+
+def adjoint(n_tm, ins, second):
+    full = ((BAND, C, W2), F32)
+    scratch = [pltpu.VMEM((12 * 3 * C, W2), BF16), pltpu.VMEM((10 * F, W2), BF16), pltpu.VMEM((BAND, C, W2), F32)]
+    return call(adjoint_kernel(second, n_tm), ins, [full, full], scratch, limit=16)
+
+
+def gradient_kernel(second, n_all):
+    def kernel(*refs):
+        refs = list(refs)
+        take = lambda n: [refs.pop(0) for _ in range(n)]
+        place_ref, x_ref, pulled, held, dwn0, r0_ref, s0_ref = take(7)
+        if second:
+            alpha_ref, dwn1, r1_ref, s1_ref = take(4)
+        bg_ref, wt_ref, o_ref, k2_ref, bias_ref, small_ref = take(6)
+        g_ref, row_ref = take(2)
+        gl_ref, gr_ref = (None, None) if second else take(2)
+        vx, hid, x_prev = refs
+        place = place_ref[...]
+        left = lanes() < LAT
+        b2, mw, bw = small_ref[0], small_ref[1], small_ref[2]
+
+        def dwn(n):
+            v = dwn0[n].astype(F32)
+            return v - alpha_ref[...] * dwn1[n].astype(F32) if second else v
+
         for r in range(8):
             one = dwn(r) if r < 6 else halves(dwn(r - 6))
             two = dwn(r - 2) if r >= 2 else halves(dwn(r + 4))
             v = jnp.where(left, one, two)
             x_prev[r] = v
             stack_lats(vx, r, v)
+        bias = bias_ref[...]
+        bias2 = jnp.concatenate([bias, bias], axis=1)
         for h in range(0, 6, 2):
             act, _ = gelu_pair(dot(o_ref[...], window(vx, h, 3 * C)) + bias2)
             for k in range(2):
@@ -320,12 +342,15 @@
                 m = x_prev[o + k + 2] + s[k] + b2
                 for side in range(2):
                     i = o + k + 4 * side
-                    x = x_ext[i + HALO]
+                    x = x_ref[i + 2]
                     before = m if side == 0 else halves(m)
                     first = jnp.where(place > 0, mw * (x - before), 0.0)
-                    lo = jnp.where(left, first, halves(ln[i + 2]))
+                    lo = jnp.where(left, first, held[i])
                     dep = jnp.where(left & (place == 0), x - bg_ref[i], 0.0)
-                    g = lo - gh[i] + obs(i) + bw * dep
+                    seen = s0_ref[i]
+                    if second:
+                        seen = seen - alpha_ref[...] * s1_ref[i]
+                    g = lo - pulled[i] + seen + bw * dep
                     g_ref[i] = g
                     if not second:
                         edge = gl_ref if i < HALO else gr_ref
@@ -334,7 +359,7 @@
                     cost = cost + lo * lo / mw + bw * dep * dep
         r = r0_ref[...]
         if second:
-            r = r - alpha * r1_ref[...]
+            r = r - alpha_ref[:, :1] * r1_ref[...]
         paid = jnp.sum(jnp.sum(wt_ref[...] * r * r, axis=0, keepdims=True), axis=1, keepdims=True)
         norm = jnp.sum(jnp.sum(squares, axis=0, keepdims=True), axis=1, keepdims=True)
         paid = 0.5 * (paid + jnp.sum(jnp.sum(cost, axis=0, keepdims=True), axis=1, keepdims=True))
@@ -344,34 +369,18 @@
     return kernel
 
 
-def gradient(total, n_tm, n_all, ins, second):
-    full = ((BAND, C, W2), F32)
+def gradient(n_all, ins, second):
     edge = ((HALO, C, W2), BF16)
-    row = ((n_all, W2), F32)
-    outs = [full, full, row] if second else [full, edge, edge, row]
-    return call(
-        gradient_kernel(total, second, n_tm, n_all),
-        ins,
-        outs,
-        [
-            pltpu.VMEM((16 * 3 * C, W2), BF16),
-            pltpu.VMEM((14 * F, W2), BF16),
-            pltpu.VMEM((10, F, W2), F32),
-            pltpu.VMEM((12 * 3 * C, W2), BF16),
-            pltpu.VMEM((16, C, W2), F32),
-            pltpu.VMEM((8, C, W2), F32),
-            pltpu.VMEM((12, C, W2), F32),
-            pltpu.VMEM((BAND, C, W2), F32),
-        ],
-        limit=24,
-    )
+    outs = [((BAND, C, W2), F32), ((n_all, W2), F32)] + ([] if second else [edge, edge])
+    scratch = [pltpu.VMEM((8 * 3 * C, W2), BF16), pltpu.VMEM((6 * F, W2), BF16), pltpu.VMEM((8, C, W2), F32)]
+    return call(gradient_kernel(second, n_all), ins, outs, scratch, limit=16)
 
 
 def final_kernel(total):
     def kernel(step_ref, first_ref, sums_ref, x_ref, g_ref, x_out, cost_out):
         alpha = step_from(sums_ref[...], step_ref[...], total)
         for i in range(BAND):
-            v = x_ref[i] - alpha * g_ref[i]
+            v = x_ref[i + 2] - alpha * g_ref[i]
             v = jnp.concatenate([v, jnp.zeros((W2 - C, W2), F32)], axis=0).T[:, :C]
             x_out[0, i] = v[:LAT]
             x_out[1, i] = v[LAT:]
@@ -397,7 +406,7 @@
     up, down = strips(from_left, mine_left, mine_right, from_right)
     after = shifted(up, TM, -1, False)
     before = shifted(down, TM, 1, False)
-    return (from_left, from_right, after, before), up
+    return from_left, from_right, after, before, up
 
 
 def per_device(x, background, opening, b1, closing, b2, mw, bw, cell, chan, val, wt, step):
@@ -407,20 +416,24 @@
     place = lax.axis_index(TM).astype(jnp.int32)[None]
     step = step[None]
     xp, xl, xr, place, step = pack(place, step, jnp.swapaxes(x, 2, 3))
-    halo, _ = exchange(xl, xr)
+    lft, rgt, upp, dwn, _ = exchange(xl, xr)
     o, k2, wia, woa, bias, small, bgp = prepare_weights(
         opening.T, closing, b1, b2, mw, bw, jnp.swapaxes(background, 1, 2)
     )
+    nets = (o, k2, bias, small)
+    own = (xp, lft, rgt) + nets
+    x0, m0, slope = forward(total, own, False)
     r0, s0 = observe(cell, chan, val, wt, xp, False)
-    consts = (bgp, wt, o, k2, wia, woa, bias, small)
-    base = (xp,) + halo + (r0, s0)
-    g0, gl, gr, row = gradient(total, n_tm, n_all, (place,) + base + consts, False)
+    pulled, held = adjoint(n_tm, (place, x0, m0, slope, upp, woa, wia, small), False)
+    rest = (bgp, wt) + nets
+    g0, row, gl, gr = gradient(n_all, (place, x0, pulled, held, dwn, r0, s0) + rest, False)
     sums0 = lax.all_to_all(row, TM_LON, 0, 0, tiled=True)
-    ghalo, up = exchange(gl, gr)
+    glft, grgt, gupp, gdwn, up = exchange(gl, gr)
     later_g0, _ = lax.optimization_barrier((g0, up))
+    x1, m1, slope, alpha = forward(total, (step, sums0, g0, glft, grgt) + own, True)
     rg, sg = observe(cell, chan, val, wt, later_g0, True)
-    ins = (place, step, sums0, g0) + ghalo + (rg, sg) + base + consts
-    g1, x1, row = gradient(total, n_tm, n_all, ins, True)
+    pulled, held = adjoint(n_tm, (place, x1, m1, slope, upp, alpha, gupp, woa, wia, small), True)
+    g1, row = gradient(n_all, (place, x1, pulled, held, dwn, r0, s0, alpha, gdwn, rg, sg) + rest, True)
     sums1 = lax.all_to_all(row, TM_LON, 0, 0, tiled=True)
     x2, costs = call(
         final_kernel(total),

time: 97.9 us -> 98.6 us (level)
  Pallas kernels: 12.4 us -> 17.3 us
  waiting for transfers between devices: 9.41 us -> 7.58 us
  blocking collectives: 27.7 us -> 26.3 us
    pallas_call x9 -> x13, Pallas kernels: 12.4 us -> 17.3 us  [call(): pl.pallas_call(kernel, out_shape=tuple((jax.ShapeDtypeStruct(shape, dtype...]
    all_to_all x1, starting transfers between devices: 17.3 us -> 15.1 us  [per_device(): sums0 = lax.all_to_all(row, TM_LON, 0, 0, tiled=True)]
    ppermute x8, waiting for transfers between devices: 9.41 us -> 7.57 us  [shifted(): return lax.ppermute(value, axes, pairs)]
    all_to_all x1, blocking collectives: 27.7 us -> 26.3 us  [per_device(): sums1 = lax.all_to_all(row, TM_LON, 0, 0, tiled=True)]
    ppermute x8, starting transfers between devices: 15.5 us -> 16.9 us  [shifted(): return lax.ppermute(value, axes, pairs)]
  transfers between devices with their start and end apart: 9 -> 9, of which waited for: 5 -> 4; matrix products, arithmetic and copies ran while one was open for 0% -> 0% of each run, Pallas kernels for 2% -> 12%
where the time goes in v2:
time: 98.6 us; the launch traced here: 97.9 us
  starting transfers between devices  32 us (32%)
  blocking collectives  26.3 us (27%)
  Pallas kernels  17.3 us (18%)
  local copies, waits for them, and re-layouts  13.3 us (13%)
  waiting for transfers between devices  7.58 us (8%)
  between operations  1.59 us (2%)
    all_to_all x1, blocking collectives, per_device(): sums1 = lax.all_to_all(row, TM_LON, 0, 0, tiled=True)  26.3 us
    pallas_call x13, Pallas kernels, call(): pl.pallas_call(kernel, out_shape=tuple((jax.ShapeDtypeStruct(shape, dtype...  17.3 us
    ppermute x8, starting transfers between devices, shifted(): return lax.ppermute(value, axes, pairs)  16.9 us
    all_to_all x1, starting transfers between devices, per_device(): sums0 = lax.all_to_all(row, TM_LON, 0, 0, tiled=True)  15.1 us
    unnamed x58, local copies, waits for them, and re-layouts  13.3 us
    ppermute x8, waiting for transfers between devices, shifted(): return lax.ppermute(value, axes, pairs)  7.57 us
  transfers between devices with their start and end apart: 9, of which 4 were waited for; matrix products, arithmetic and copies ran while one was open for 0% of the time, Pallas kernels for 12%

profile of v2, /device:TPU:1, one launch (start us, length us, event | category | flops | bytes accessed | tf_op | source)
XLA Modules:
  0.0 97.9 jit_solution(12090792804977519932)
XLA Ops:
  1.3 0.0 copy-start
  1.3 1.0 %copy-done = f32[2,8,80,64]{2,3,1,0:T(8,128)S(1)} copy-done((f32[2,8,80,64]{2,3,1,0:T(8,128)S(1)}, f32[2,8,80,64]{2,3,1,0:T(8,128)}, u32[]{:S(2)}) %copy-start) | copy-done | bytes 327704
  2.3 0.2 shard_map.140
  2.5 3.1 %collective-permute-start = (bf16[4,80,128]{2,1,0:T(8,128)(2,1)S(1)}, bf16[4,80,128]{2,1,0:T(8,128)(2,1)S(1)}, u32[]{:S(2)}, u32[]{:S(2)}) collective-permute-start(bf16[4,80,128]{2,1,0:T(8,128)(2,1)S(1)} %get-tuple-element.45.b_ref), channel_id=1, source_target_pairs={{0,1},{1,2},{2,3},{3,4},{4,5},{5,6},{6,7},{7,8},{8,9},{9,10},{10,1... | collective-permute-start | bytes 245768 | tf_op jit(solution)/shard_map/ppermute | solution.py:400
  5.6 0.3 collective-permute-start.1
  5.9 1.2 %collective-permute-done.refs_1_.l_ref.refs_6_ = bf16[4,80,128]{2,1,0:T(8,128)(2,1)S(1)} collective-permute-done((bf16[4,80,128]{2,1,0:T(8,128)(2,1)S(1)}, bf16[4,80,128]{2,1,0:T(8,128)(2,1)S(1)}, u32[]{:S(2)}, u32[]{:S(2)}) %collective-permute-start) | collective-permute-done | bytes 81952 | tf_op jit(solution)/shard_map/ppermute | solution.py:400
  7.1 2.4 %collective-permute-done.1.refs_2_.r_ref.refs_7_ = bf16[4,80,128]{2,1,0:T(8,128)(2,1)S(1)} collective-permute-done((bf16[4,80,128]{2,1,0:T(8,128)(2,1)S(1)}, bf16[4,80,128]{2,1,0:T(8,128)(2,1)S(1)}, u32[]{:S(2)}, u32[]{:S(2)}) %collective-permute-start.1) | collective-permute-done | bytes 81952 | tf_op jit(solution)/shard_map/ppermute | solution.py:400
  9.5 0.1 shard_map.143
  9.6 1.3 %collective-permute-start.2 = (bf16[6,80,128]{2,1,0:T(8,128)(2,1)S(1)}, bf16[6,80,128]{2,1,0:T(8,128)(2,1)S(1)}, u32[]{:S(2)}, u32[]{:S(2)}) collective-permute-start(bf16[6,80,128]{2,1,0:T(8,128)(2,1)S(1)} %get-tuple-element.54), channel_id=1, source_target_pairs={{32,0},{64,32},{96,64},{128,96},{160,128},{192,160},{224,192},{33,... | collective-permute-start | bytes 368648 | tf_op jit(solution)/shard_map/ppermute | solution.py:400
  10.9 4.0 %collective-permute-start.3 = (bf16[6,80,128]{2,1,0:T(8,128)(2,1)S(1)}, bf16[6,80,128]{2,1,0:T(8,128)(2,1)S(1)}, u32[]{:S(2)}, u32[]{:S(2)}) collective-permute-start(bf16[6,80,128]{2,1,0:T(8,128)(2,1)S(1)} %get-tuple-element.59), channel_id=1, source_target_pairs={{0,32},{32,64},{64,96},{96,128},{128,160},{160,192},{192,224},{1,3... | collective-permute-start | bytes 368648 | tf_op jit(solution)/shard_map/ppermute | solution.py:400
  14.9 0.0 copy-start.17
  14.9 0.7 copy-done.17
  15.6 0.7 copy-done.19
  16.3 0.7 copy-done.21
  17.0 0.7 copy-done.23
  17.7 0.9 shard_map.145
  18.6 0.0 copy-done.3
  18.6 0.0 copy-done.4
  18.6 0.0 copy-done.11
  18.6 0.0 copy-start.25
  18.6 0.7 copy-done.25
  19.3 0.7 copy-done.26
  19.9 0.7 copy-done.27
  20.6 0.7 copy-done.28
  21.3 0.5 shard_map.141
  21.7 2.1 %shard_map.142 = (f32[12,80,128]{2,1,0:T(8,128)S(1)}, f32[12,80,128]{2,1,0:T(8,128)S(1)}, f32[10,256,128]{2,1,0:T(8,128)S(1)}) custom-call(f32[8,80,128]{2,1,0:T(8,128)S(1)} %get-tuple-element.44.refs_0_.x_ref.refs_5_, bf16[4,80,128]{2,1,0:T(8,128)(2,1)S(1)} %collective-permute-done.refs_1_.l_ref.refs_6_, ...), custom_call_target="tpu_custom_call" | custom-call | tf_op jit(solution)/shard_map/pallas_call | solution.py:34
  23.9 0.0 collective-permute-done.2.refs_4_
  23.9 0.0 copy-start.1
  23.9 0.0 copy-start.18
  23.9 1.6 %shard_map.144 = (f32[8,80,128]{2,1,0:T(8,128)S(1)}, f32[8,80,128]{2,1,0:T(8,128)S(1)}) custom-call(s32[1,128]{1,0:T(1,128)S(1)} %get-tuple-element.43.refs_0_, f32[12,80,128]{2,1,0:T(8,128)S(1)} %get-tuple-element.51.refs_1_, f32[12,80,128]{2,1,0:T(8,128)S(1)} %get-tuple-element.52.refs_2_, f32[10,256,128]{2,1,0:T(8,128)S(1)} %get-tuple-element.53.refs_3_, ...), custom_call_target="tpu_custom_call" | custom-call | tf_op jit(solution)/shard_map/pallas_call | solution.py:34
  25.5 0.0 collective-permute-done.3.refs_4_
  25.6 0.0 copy-start.20
  25.6 0.0 copy-start.22
  25.6 0.0 copy-start.24
  25.6 1.5 %shard_map.146 = (f32[8,80,128]{2,1,0:T(8,128)S(1)}, f32[256,128]{1,0:T(8,128)S(1)}, bf16[4,80,128]{2,1,0:T(8,128)(2,1)S(1)}, bf16[4,80,128]{2,1,0:T(8,128)(2,1)S(1)}) custom-call(s32[1,128]{1,0:T(1,128)S(1)} %get-tuple-element.43.refs_0_, f32[12,80,128]{2,1,0:T(8,128)S(1)} %get-tuple-element.51.refs_1_, f32[8,80,128]{2,1,0:T(8,128)S(1)} %get-tuple-element.57.refs_2_, ...), custom_call_target="tpu_custom_call" | custom-call | tf_op jit(solution)/shard_map/pallas_call | solution.py:34
  27.1 0.6 copy-done.12
  27.8 0.6 copy-done.13
  28.4 0.6 copy-done.15
  29.0 15.1 %all-to-all-start = ((f32[256,1,128]{2,1,0:T(1,128)}), f32[256,1,128]{2,1,0:T(1,128)S(1)}, u32[]{:S(2)}, u32[]{:S(2)}) async-start(f32[256,1,128]{2,1,0:T(1,128)} %bitcast.26), calls=%async_computation | async-start | bytes 262144 | tf_op jit(solution)/shard_map/all_to_all | solution.py:430
  44.1 1.8 %collective-permute-start.4 = (bf16[4,80,128]{2,1,0:T(8,128)(2,1)}, bf16[4,80,128]{2,1,0:T(8,128)(2,1)S(1)}, u32[]{:S(2)}, u32[]{:S(2)}) collective-permute-start(bf16[4,80,128]{2,1,0:T(8,128)(2,1)} %copy-done.15), channel_id=1, source_target_pairs={{0,1},{1,2},{2,3},{3,4},{4,5},{5,6},{6,7},{7,8},{8,9},{9,10},{10,1... | collective-permute-start | bytes 245768 | tf_op jit(solution)/shard_map/ppermute | solution.py:400
  45.9 0.5 collective-permute-start.5
  46.4 1.8 %collective-permute-done.4.refs_3_.l_ref = bf16[4,80,128]{2,1,0:T(8,128)(2,1)S(1)} collective-permute-done((bf16[4,80,128]{2,1,0:T(8,128)(2,1)}, bf16[4,80,128]{2,1,0:T(8,128)(2,1)S(1)}, u32[]{:S(2)}, u32[]{:S(2)}) %collective-permute-start.4) | collective-permute-done | bytes 81952 | tf_op jit(solution)/shard_map/ppermute | solution.py:400
  48.2 2.2 %collective-permute-done.5.refs_4_.r_ref = bf16[4,80,128]{2,1,0:T(8,128)(2,1)S(1)} collective-permute-done((bf16[4,80,128]{2,1,0:T(8,128)(2,1)}, bf16[4,80,128]{2,1,0:T(8,128)(2,1)S(1)}, u32[]{:S(2)}, u32[]{:S(2)}) %collective-permute-start.5) | collective-permute-done | bytes 81952 | tf_op jit(solution)/shard_map/ppermute | solution.py:400
  50.4 0.9 copy-done.14
  51.3 0.9 copy-done.16
  52.2 0.8 shard_map.148
  53.0 0.6 copy-done.5
  53.6 1.3 %collective-permute-start.6 = (bf16[6,80,128]{2,1,0:T(8,128)(2,1)}, bf16[6,80,128]{2,1,0:T(8,128)(2,1)}, u32[]{:S(2)}, u32[]{:S(2)}) collective-permute-start(bf16[6,80,128]{2,1,0:T(8,128)(2,1)} %get-tuple-element.71), channel_id=1, source_target_pairs={{32,0},{64,32},{96,64},{128,96},{160,128},{192,160},{224,192},{33,... | collective-permute-start | bytes 368648 | tf_op jit(solution)/shard_map/ppermute | solution.py:400
  54.9 4.6 %collective-permute-start.7 = (bf16[6,80,128]{2,1,0:T(8,128)(2,1)}, bf16[6,80,128]{2,1,0:T(8,128)(2,1)}, u32[]{:S(2)}, u32[]{:S(2)}) collective-permute-start(bf16[6,80,128]{2,1,0:T(8,128)(2,1)} %get-tuple-element.74), channel_id=1, source_target_pairs={{0,32},{32,64},{64,96},{96,128},{128,160},{160,192},{192,224},{1,3... | collective-permute-start | bytes 368648 | tf_op jit(solution)/shard_map/ppermute | solution.py:400
  59.6 0.0 copy-done.20
  59.6 0.9 shard_map.150
  60.5 0.0 copy-start.9
  60.5 0.7 copy-done.9
  61.2 0.0 all-to-all-done
  61.2 0.9 copy-done.6
  62.1 0.9 copy-done.8
  63.0 2.3 %shard_map.147 = (f32[12,80,128]{2,1,0:T(8,128)S(1)}, f32[12,80,128]{2,1,0:T(8,128)S(1)}, f32[10,256,128]{2,1,0:T(8,128)S(1)}, f32[1,128]{1,0:T(1,128)S(1)}) custom-call(f32[1,128]{1,0:T(1,128)S(1)} %get-tuple-element.42.refs_0_.step_ref, f32[256,128]{1,0:T(8,128)S(1)} %bitcast.20, f32[8,80,128]{2,1,0:T(8,128)S(1)} %get-tuple-element.75.refs_2_.x_ref, ...), custom_call_target="tpu_custom_call" | custom-call | tf_op jit(solution)/shard_map/pallas_call | solution.py:34
  65.3 0.0 collective-permute-done.6.refs_6_
  65.3 0.0 copy-start.10
  65.3 2.6 %shard_map.149 = (f32[8,80,128]{2,1,0:T(8,128)S(1)}, f32[8,80,128]{2,1,0:T(8,128)S(1)}) custom-call(s32[1,128]{1,0:T(1,128)S(1)} %get-tuple-element.43.refs_0_, f32[12,80,128]{2,1,0:T(8,128)S(1)} %get-tuple-element.67.refs_1_.x_ref, f32[12,80,128]{2,1,0:T(8,128)S(1)} %get-tuple-element.68.refs_2_, f32[10,256,128]{2,1,0:T(8,128)S(1)} %get-tuple-element.69.refs_3_, ...), custom_call_target="tpu_custom_call" | custom-call | tf_op jit(solution)/shard_map/pallas_call | solution.py:34
  68.0 0.0 collective-permute-done.7.refs_8_
  68.0 2.4 %shard_map.151 = (f32[8,80,128]{2,1,0:T(8,128)S(1)}, f32[256,128]{1,0:T(8,128)S(1)}) custom-call(s32[1,128]{1,0:T(1,128)S(1)} %get-tuple-element.43.refs_0_, f32[12,80,128]{2,1,0:T(8,128)S(1)} %get-tuple-element.67.refs_1_.x_ref, f32[8,80,128]{2,1,0:T(8,128)S(1)} %get-tuple-element.72.refs_2_, f32[8,80,128]{2,1,0:T(8,128)S(1)} %get-tuple-element.73.refs_3_, ...), custom_call_target="tpu_custom_call" | custom-call | tf_op jit(solution)/shard_map/pallas_call | solution.py:34
  70.4 26.3 %all_to_all.22 = f32[256,1,128]{2,1,0:T(1,128)S(1)} all-to-all(f32[256,1,128]{2,1,0:T(1,128)S(1)} %bitcast.27), channel_id=1, replica_groups=mesh['tm_0'=4,'tm_1'=2,'lon_0'=2,'lon_1'=8,'lon_2'=2] {'tm_0','tm_1','lo..., dimensions={0} | all-to-all | bytes 262144 | tf_op jit(solution)/shard_map/all_to_all | solution.py:437
  96.7 1.2 %shard_map.152 = (f32[2,8,64,80]{3,2,1,0:T(8,128)}, f32[1,2]{1,0:T(1,128)}) custom-call(f32[1,128]{1,0:T(1,128)S(1)} %get-tuple-element.42.refs_0_.step_ref, f32[256,128]{1,0:T(8,128)S(1)} %bitcast.21, f32[256,128]{1,0:T(8,128)S(1)} %bitcast.23, f32[12,80,128]{2,1,0:T(8,128)S(1)} %get-tuple-element.67.refs_1_.x_ref, f32[8,80,128]{2,1,0:T(8,128)S(1)} %get-tuple-element.79.g_ref), custom_call_target="tpu_custom_call" | custom-call | tf_op jit(solution)/shard_map/pallas_call | solution.py:34
  (26 shorter events, 0.0 us)
Async XLA Ops:
  1.3 1.0 %copy-start = (f32[2,8,80,64]{2,3,1,0:T(8,128)S(1)}, f32[2,8,80,64]{2,3,1,0:T(8,128)}, u32[]{:S(2)}) copy-start(f32[2,8,80,64]{2,3,1,0:T(8,128)} %param.13) | copy-start | bytes 983044
  2.3 16.3 %copy-start.3 = (bf16[256,720]{0,1:T(8,128)(2,1)S(1)}, bf16[256,720]{0,1:T(8,128)(2,1)}, u32[]{:S(2)}) copy-start(bf16[256,720]{0,1:T(8,128)(2,1)} %param.15) | copy-start | bytes 1105924
  2.3 16.3 %copy-start.4 = (bf16[80,2304]{1,0:T(8,128)(2,1)S(1)}, bf16[80,2304]{1,0:T(8,128)(2,1)}, u32[]{:S(2)}) copy-start(bf16[80,2304]{1,0:T(8,128)(2,1)} %c_ref.1) | copy-start | bytes 1105924
  2.3 16.3 %copy-start.11 = (f32[8,80,64]{1,2,0:T(8,128)S(1)}, f32[8,80,64]{1,2,0:T(8,128)}, u32[]{:S(2)}) copy-start(f32[8,80,64]{1,2,0:T(8,128)} %param.14) | copy-start | bytes 491524
  2.5 4.6 %collective-permute-start = (bf16[4,80,128]{2,1,0:T(8,128)(2,1)S(1)}, bf16[4,80,128]{2,1,0:T(8,128)(2,1)S(1)}, u32[]{:S(2)}, u32[]{:S(2)}) collective-permute-start(bf16[4,80,128]{2,1,0:T(8,128)(2,1)S(1)} %get-tuple-element.45.b_ref), channel_id=1, source_target_pairs={{0,1},{1,2},{2,3},{3,4},{4,5},{5,6},{6,7},{7,8},{8,9},{9,10},{10,1... | collective-permute-start | bytes 245768 | tf_op jit(solution)/shard_map/ppermute | solution.py:400
  5.6 3.9 %collective-permute-start.1 = (bf16[4,80,128]{2,1,0:T(8,128)(2,1)S(1)}, bf16[4,80,128]{2,1,0:T(8,128)(2,1)S(1)}, u32[]{:S(2)}, u32[]{:S(2)}) collective-permute-start(bf16[4,80,128]{2,1,0:T(8,128)(2,1)S(1)} %get-tuple-element.46.a_ref), channel_id=1, source_target_pairs={{0,31},{1,0},{2,1},{3,2},{4,3},{5,4},{6,5},{7,6},{8,7},{9,8},{10,9... | collective-permute-start | bytes 245768 | tf_op jit(solution)/shard_map/ppermute | solution.py:400
  9.6 14.2 %collective-permute-start.2 = (bf16[6,80,128]{2,1,0:T(8,128)(2,1)S(1)}, bf16[6,80,128]{2,1,0:T(8,128)(2,1)S(1)}, u32[]{:S(2)}, u32[]{:S(2)}) collective-permute-start(bf16[6,80,128]{2,1,0:T(8,128)(2,1)S(1)} %get-tuple-element.54), channel_id=1, source_target_pairs={{32,0},{64,32},{96,64},{128,96},{160,128},{192,160},{224,192},{33,... | collective-permute-start | bytes 368648 | tf_op jit(solution)/shard_map/ppermute | solution.py:400
  10.9 14.6 %collective-permute-start.3 = (bf16[6,80,128]{2,1,0:T(8,128)(2,1)S(1)}, bf16[6,80,128]{2,1,0:T(8,128)(2,1)S(1)}, u32[]{:S(2)}, u32[]{:S(2)}) collective-permute-start(bf16[6,80,128]{2,1,0:T(8,128)(2,1)S(1)} %get-tuple-element.59), channel_id=1, source_target_pairs={{0,32},{32,64},{64,96},{96,128},{128,160},{160,192},{192,224},{1,3... | collective-permute-start | bytes 368648 | tf_op jit(solution)/shard_map/ppermute | solution.py:400
  14.9 0.7 copy-start.17
  15.6 0.7 copy-start.19
  16.3 0.7 copy-start.21
  17.0 0.7 copy-start.23
  18.6 0.7 copy-start.25
  19.3 0.7 copy-start.26
  19.9 0.7 copy-start.27
  20.6 0.7 copy-start.28
  23.9 1.7 %copy-start.1 = (bf16[6,80,128]{2,1,0:T(8,128)(2,1)}, bf16[6,80,128]{2,1,0:T(8,128)(2,1)S(1)}, u32[]{:S(2)}) copy-start(bf16[6,80,128]{2,1,0:T(8,128)(2,1)S(1)} %collective-permute-done.2.refs_4_) | copy-start | bytes 368644
  23.9 1.7 %copy-start.18 = (f32[2,256]{1,0:T(2,128)S(1)}, f32[2,256]{1,0:T(2,128)}, u32[]{:S(2)}) copy-start(f32[2,256]{1,0:T(2,128)} %refs_12_.1) | copy-start | bytes 6148
  25.6 34.0 %copy-start.20 = (s32[2,256]{1,0:T(2,128)S(1)}, s32[2,256]{1,0:T(2,128)}, u32[]{:S(2)}) copy-start(s32[2,256]{1,0:T(2,128)} %cell_ref.3) | copy-start | bytes 6148
  25.6 34.0 %copy-start.22 = (s32[2,256]{1,0:T(2,128)S(1)}, s32[2,256]{1,0:T(2,128)}, u32[]{:S(2)}) copy-start(s32[2,256]{1,0:T(2,128)} %chan_ref.3) | copy-start | bytes 6148
  25.6 34.0 %copy-start.24 = (f32[2,256]{1,0:T(2,128)S(1)}, f32[2,256]{1,0:T(2,128)}, u32[]{:S(2)}) copy-start(f32[2,256]{1,0:T(2,128)} %val_ref.3) | copy-start | bytes 6148
  27.1 0.6 copy-start.12
  27.8 0.6 copy-start.13
  28.4 0.6 copy-start.15
  29.0 32.2 %all-to-all-start = ((f32[256,1,128]{2,1,0:T(1,128)}), f32[256,1,128]{2,1,0:T(1,128)S(1)}, u32[]{:S(2)}, u32[]{:S(2)}) async-start(f32[256,1,128]{2,1,0:T(1,128)} %bitcast.26), calls=%async_computation | async-start | bytes 262144 | tf_op jit(solution)/shard_map/all_to_all | solution.py:430
  44.1 4.1 %collective-permute-start.4 = (bf16[4,80,128]{2,1,0:T(8,128)(2,1)}, bf16[4,80,128]{2,1,0:T(8,128)(2,1)S(1)}, u32[]{:S(2)}, u32[]{:S(2)}) collective-permute-start(bf16[4,80,128]{2,1,0:T(8,128)(2,1)} %copy-done.15), channel_id=1, source_target_pairs={{0,1},{1,2},{2,3},{3,4},{4,5},{5,6},{6,7},{7,8},{8,9},{9,10},{10,1... | collective-permute-start | bytes 245768 | tf_op jit(solution)/shard_map/ppermute | solution.py:400
  45.9 4.5 %collective-permute-start.5 = (bf16[4,80,128]{2,1,0:T(8,128)(2,1)}, bf16[4,80,128]{2,1,0:T(8,128)(2,1)S(1)}, u32[]{:S(2)}, u32[]{:S(2)}) collective-permute-start(bf16[4,80,128]{2,1,0:T(8,128)(2,1)} %copy-done.13), channel_id=1, source_target_pairs={{0,31},{1,0},{2,1},{3,2},{4,3},{5,4},{6,5},{7,6},{8,7},{9,8},{10,9... | collective-permute-start | bytes 245768 | tf_op jit(solution)/shard_map/ppermute | solution.py:400
  50.4 0.9 copy-start.14
  51.3 0.9 copy-start.16
  52.2 7.4 %copy-start.7 = (bf16[4,80,128]{2,1,0:T(8,128)(2,1)}, bf16[4,80,128]{2,1,0:T(8,128)(2,1)S(1)}, u32[]{:S(2)}) copy-start(bf16[4,80,128]{2,1,0:T(8,128)(2,1)S(1)} %collective-permute-done.5.refs_4_.r_ref) | copy-start | bytes 245764
  53.0 0.6 copy-start.5
  53.6 11.7 %collective-permute-start.6 = (bf16[6,80,128]{2,1,0:T(8,128)(2,1)}, bf16[6,80,128]{2,1,0:T(8,128)(2,1)}, u32[]{:S(2)}, u32[]{:S(2)}) collective-permute-start(bf16[6,80,128]{2,1,0:T(8,128)(2,1)} %get-tuple-element.71), channel_id=1, source_target_pairs={{32,0},{64,32},{96,64},{128,96},{160,128},{192,160},{224,192},{33,... | collective-permute-start | bytes 368648 | tf_op jit(solution)/shard_map/ppermute | solution.py:400
  54.9 13.0 %collective-permute-start.7 = (bf16[6,80,128]{2,1,0:T(8,128)(2,1)}, bf16[6,80,128]{2,1,0:T(8,128)(2,1)}, u32[]{:S(2)}, u32[]{:S(2)}) collective-permute-start(bf16[6,80,128]{2,1,0:T(8,128)(2,1)} %get-tuple-element.74), channel_id=1, source_target_pairs={{0,32},{32,64},{64,96},{96,128},{128,160},{160,192},{192,224},{1,3... | collective-permute-start | bytes 368648 | tf_op jit(solution)/shard_map/ppermute | solution.py:400
  60.5 0.7 copy-start.9
  61.2 4.1 %copy-start.2 = (bf16[6,80,128]{2,1,0:T(8,128)(2,1)S(1)}, bf16[6,80,128]{2,1,0:T(8,128)(2,1)}, u32[]{:S(2)}) copy-start(bf16[6,80,128]{2,1,0:T(8,128)(2,1)} %copy-done.1) | copy-start | bytes 368644
  61.2 0.9 copy-start.6
  62.1 0.9 copy-start.8
  65.3 2.6 %copy-start.10 = (f32[8,80,128]{2,1,0:T(8,128)S(1)}, f32[8,80,128]{2,1,0:T(8,128)}, u32[]{:S(2)}) copy-start(f32[8,80,128]{2,1,0:T(8,128)} %copy-done.9) | copy-start | bytes 983044

commit v3 on v2

v3 whole, which is shorter than its diff:
```python
import jax
import jax.numpy as jnp
from jax import lax
from jax.experimental import pallas as pl
from jax.experimental.pallas import tpu as pltpu
from jax.sharding import Mesh
from jax.sharding import PartitionSpec as P


LON = ("lon_0", "lon_1", "lon_2")
TM = ("tm_0", "tm_1")
TM_LON = TM + LON
C = 80
F = 256
LAT = 64
BAND = 8
HALO = 4
OBS = 256
W2 = 2 * LAT
F32 = jnp.float32
BF16 = jnp.bfloat16
KC = 0.7978845608028654


def lanes(rows=C):
    return lax.broadcasted_iota(jnp.int32, (rows, W2), 1)


def call(kernel, ins, outs, scratch=(), limit=8, scalars=0):
    smem = pl.BlockSpec(memory_space=pltpu.SMEM)
    vmem = pl.BlockSpec(memory_space=pltpu.VMEM)
    return pl.pallas_call(
        kernel,
        out_shape=tuple(jax.ShapeDtypeStruct(shape, dtype) for shape, dtype in outs),
        in_specs=[smem] * scalars + [vmem] * (len(ins) - scalars),
        out_specs=tuple(vmem for _ in outs),
        scratch_shapes=list(scratch),
        compiler_params=pltpu.CompilerParams(vmem_limit_bytes=limit << 20),
    )(*ins)


def dot(a, b):
    return jnp.dot(a, b, preferred_element_type=F32)


def earlier_lat(v):
    lane = lanes(v.shape[0])
    return jnp.where((lane == 0) | (lane == LAT), 0.0, pltpu.roll(v, 1, 1))


def later_lat(v):
    lane = lanes(v.shape[0])
    return jnp.where((lane == LAT - 1) | (lane == W2 - 1), 0.0, pltpu.roll(v, W2 - 1, 1))


def halves(v):
    return pltpu.roll(v, LAT, 1)


def pick(even, one, two):
    return jnp.where(even, one.astype(F32), two.astype(F32))


def pack_kernel(place_ref, band_ref, step_ref, x_ref, table_ref,
                xp_ref, s0_ref, s1_ref, place_row, band_row, step_row, spot_row, chan_row, val_row, wt_row, b1_row, small_row):
    place_row[...] = jnp.full((1, W2), place_ref[0], jnp.int32)
    band_row[...] = jnp.full((1, W2), band_ref[0], jnp.int32)
    step_row[...] = jnp.full((1, W2), step_ref[0], F32)

    def line(n):
        return jnp.concatenate([table_ref[n : n + 1, :], table_ref[n + 1 : n + 2, :]], axis=1)

    cell = line(0).astype(jnp.int32)
    sub = (lax.broadcasted_iota(jnp.int32, cell.shape, 1) >= OBS).astype(jnp.int32)
    spot_row[...] = (cell >> 6) * W2 + sub * LAT + (cell & (LAT - 1))
    chan_row[...] = line(2).astype(jnp.int32)
    val_row[...] = line(4)
    wt_row[...] = line(6)
    b1_row[...] = table_ref[8:9, :]
    small_row[...] = table_ref[9:12, :C]
    even = (jnp.full((1, W2), band_ref[0], jnp.int32) & 1) == 0
    for i in range(HALO):
        one = jnp.concatenate([x_ref[0, i], x_ref[1, i]], axis=0).T
        two = jnp.concatenate([x_ref[0, i + HALO], x_ref[1, i + HALO]], axis=0).T
        xp_ref[i] = one
        xp_ref[i + HALO] = two
        s0_ref[i] = jnp.where(even, two, one).astype(BF16)
        s1_ref[i] = jnp.where(even, one, two).astype(BF16)


def pack(place, band, step, x, obs, small):
    edge = ((HALO, C, W2), BF16)
    row = lambda n, dtype: ((1, n), dtype)
    outs = [((BAND, C, W2), F32), edge, edge, row(W2, jnp.int32), row(W2, jnp.int32), row(W2, F32)]
    outs += [row(2 * OBS, jnp.int32), row(2 * OBS, jnp.int32), row(2 * OBS, F32), row(2 * OBS, F32), row(F, F32), ((3, C), F32)]
    rows = [v.astype(F32) for v in obs] + [jnp.pad(v, (0, OBS - v.shape[0]))[None] for v in small]
    return call(pack_kernel, [place, band, step, x, jnp.concatenate(rows, axis=0)], outs, scalars=3)


def weights_kernel(ot_ref, c_ref, b1_ref, row_ref, bg_ref,
                   o_ref, k2_ref, wia_ref, woa_ref, bias_ref, small_ref, bgp_ref, tall, row):
    tall[9 * C :, :] = jnp.zeros((768 - 9 * C, F), F32)
    tall[: 9 * C, :] = ot_ref[...].astype(F32)
    o_ref[...] = tall[...].T[:, : 9 * C].astype(BF16)
    turned = ot_ref
    for t in range(9):
        a, b = divmod(t, 3)
        block = c_ref[:, F * t : F * (t + 1)]
        k2_ref[C * b : C * (b + 1), F * a : F * (a + 1)] = block
        tall[C * (8 - t) : C * (9 - t), :] = block.astype(F32)
        wia_ref[C * b : C * (b + 1), F * a : F * (a + 1)] = turned[C * (8 - t) : C * (9 - t), :]
    back = tall[...].T
    woa_ref[...] = back[:, : 9 * C].astype(BF16)
    bias_ref[...] = jnp.broadcast_to(b1_ref[...], (W2, F)).T
    row[...] = jnp.zeros((W2, W2), F32)
    for n in range(3):
        row[:, :C] = jnp.broadcast_to(row_ref[n : n + 1, :], (W2, C))
        small_ref[n] = row[...].T[:C]
    for i in range(BAND):
        bgp_ref[i] = jnp.concatenate([bg_ref[i], jnp.zeros((LAT, C), F32)], axis=0).T


def prepare_weights(opening_t, closing, b1, small, bg):
    ins = [opening_t, closing, b1, small, bg]
    outs = [((F, 9 * C), BF16), ((3 * C, 3 * F), BF16), ((3 * C, 3 * F), BF16), ((F, 9 * C), BF16)]
    outs += [((F, W2), F32), ((3, C, W2), F32), ((BAND, C, W2), F32)]
    return call(
        weights_kernel,
        ins,
        outs,
        [pltpu.VMEM((768, F), F32), pltpu.VMEM((W2, W2), F32)],
    )


def split3(v):
    hi = v.astype(BF16)
    rest = v - hi.astype(F32)
    mid = rest.astype(BF16)
    low = (rest - mid.astype(F32)).astype(BF16)
    return jnp.concatenate([hi, mid, low], axis=0)


def join3(v):
    return (v[2 * C :] + v[C : 2 * C]) + v[:C]


def obs_kernel(spot_ref, chan_ref, val_ref, wt_ref, x_ref, *refs):
    first = len(refs) == 3 and refs[0].shape[0] == 1
    if first:
        r_ref, s_ref, hot = refs
        spot = spot_ref[...]
        rows = 2 * W2
        for p in range(BAND // 2):
            at = lax.broadcasted_iota(jnp.int32, (rows, 2 * OBS), 0) + p * rows
            hot[p] = jnp.where(at == spot, 1.0, 0.0).astype(BF16)
    else:
        hot, r_ref, s_ref = refs
    total = jnp.zeros((3 * C, 2 * OBS), F32)
    for p in range(BAND // 2):
        total = total + dot(split3(jnp.concatenate([x_ref[2 * p], x_ref[2 * p + 1]], axis=1)), hot[p])
    mine = lax.broadcasted_iota(jnp.int32, (C, 2 * OBS), 0) == chan_ref[...]
    r = jnp.sum(jnp.where(mine, join3(total), 0.0), axis=0, keepdims=True)
    if first:
        r = r - val_ref[...]
    r_ref[...] = r
    spread = split3(jnp.where(mine, wt_ref[...] * r, 0.0))
    for p in range(BAND // 2):
        got = lax.dot_general(spread, hot[p], (((1,), (1,)), ((), ())), preferred_element_type=F32)
        got = join3(got)
        s_ref[2 * p] = got[:, :W2]
        s_ref[2 * p + 1] = got[:, W2:]


def observe(lines, field, hot=None):
    outs = [((1, 2 * OBS), F32), ((BAND, C, W2), F32)]
    if hot is None:
        return call(obs_kernel, list(lines) + [field], outs + [((BAND // 2, 2 * W2, 2 * OBS), BF16)])
    return call(obs_kernel, list(lines) + [field, hot], outs)


def strip_kernel(place_ref, band_ref, mine0, mine1, got0, got1, send0, send1):
    even = (band_ref[...] & 1) == 0
    even_tm = (place_ref[...] & 1) == 0

    def at(e):
        if e < 0:
            return pick(even, got1[HALO + e], got0[HALO + e])
        if e < HALO:
            return pick(even, mine1[e], mine0[e])
        if e < BAND:
            return pick(even, mine0[e - HALO], mine1[e - HALO])
        return pick(even, got0[e - BAND], got1[e - BAND])

    left = lanes() < LAT
    for p in range(6):
        one, two = at(p - 2), at(p + 4)
        up = jnp.where(left, one, halves(two))
        down = jnp.where(left, halves(one), two)
        send0[p] = jnp.where(even_tm, down, up).astype(BF16)
        send1[p] = jnp.where(even_tm, up, down).astype(BF16)


def strips(*args):
    strip = ((6, C, W2), BF16)
    return call(strip_kernel, list(args), [strip, strip])


def gelu_pair(v):
    sq = v * v
    t = jnp.tanh(v * (KC + (KC * 0.044715) * sq))
    half = 0.5 * (1.0 + t)
    slope = half + (0.5 * v) * (1.0 - t * t) * (KC + (3 * KC * 0.044715) * sq)
    return v * half, slope


def stack_lats(ref, n, v):
    ref[3 * C * n : 3 * C * n + C] = earlier_lat(v).astype(BF16)
    ref[3 * C * n + C : 3 * C * n + 2 * C] = v.astype(BF16)
    ref[3 * C * n + 2 * C : 3 * C * n + 3 * C] = later_lat(v).astype(BF16)


def window(ref, n, rows):
    return jnp.concatenate([ref[rows * n : rows * (n + 3)], ref[rows * (n + 1) : rows * (n + 4)]], axis=1)


def sum_lats(s):
    res = []
    for k in range(2):
        part = s[:, W2 * k : W2 * (k + 1)]
        res.append(earlier_lat(part[:C]) + part[C : 2 * C] + later_lat(part[2 * C :]))
    return res


def step_from(sums, step, total):
    whole = jnp.sum(sums, axis=0, keepdims=True)
    lane = lax.broadcasted_iota(jnp.int32, whole.shape, 1)
    norm = jnp.sum(jnp.where(lane == 0, whole, 0.0), axis=1, keepdims=True)
    return step[:, :1] / jnp.sqrt(norm / total + 1e-06)


def forward_kernel(total, second):
    def kernel(*refs):
        refs = list(refs)
        take = lambda n: [refs.pop(0) for _ in range(n)]
        if second:
            step_ref, sums_ref, g0_ref, ggot0, ggot1 = take(5)
        band_ref, own_ref, got0, got1, o_ref, k2_ref, bias_ref, small_ref = take(8)
        x_ref, m_ref, slope = take(3)
        alpha_ref = take(1)[0] if second else None
        vx, hid = refs
        if second:
            alpha = step_from(sums_ref[...], step_ref[...], total)
            alpha_ref[...] = jnp.broadcast_to(alpha, (1, W2))

        even = (band_ref[...] & 1) == 0

        def at(e, own, zero, one):
            if e < HALO:
                return pick(even, one[e], zero[e])
            if e < HALO + BAND:
                return own[e - HALO]
            return pick(even, zero[e - HALO - BAND], one[e - HALO - BAND])

        for e in range(16):
            v = at(e, own_ref, got0, got1)
            if second:
                v = v - alpha * at(e, g0_ref, ggot0, ggot1)
            if 2 <= e < 14:
                x_ref[e - 2] = v
            stack_lats(vx, e, v)
        bias = bias_ref[...]
        bias2 = jnp.concatenate([bias, bias], axis=1)
        for h in range(0, 14, 2):
            pre = dot(o_ref[...], window(vx, h, 3 * C)) + bias2
            act, sl = gelu_pair(pre)
            for k in range(2):
                n = h + k
                hid[F * n : F * (n + 1)] = act[:, W2 * k : W2 * (k + 1)].astype(BF16)
                if 2 <= n < 12:
                    slope[n - 2] = sl[:, W2 * k : W2 * (k + 1)]
        for o in range(0, 12, 2):
            s = sum_lats(dot(k2_ref[...], window(hid, o, F)))
            for k in range(2):
                m_ref[o + k] = x_ref[o + k] + s[k] + small_ref[0]

    return kernel


def forward(total, ins, second):
    outs = [((12, C, W2), F32), ((12, C, W2), F32), ((10, F, W2), F32)] + ([((1, W2), F32)] if second else [])
    scratch = [pltpu.VMEM((16 * 3 * C, W2), BF16), pltpu.VMEM((14 * F, W2), BF16)]
    return call(forward_kernel(total, second), ins, outs, scratch, limit=16)


def gradient_kernel(second, n_tm, n_all):
    def kernel(*refs):
        refs = list(refs)
        take = lambda n: [refs.pop(0) for _ in range(n)]
        place_ref, band_ref, x_ref, m_ref, slope, got0, got1, r0_ref, s0_ref = take(9)
        if second:
            alpha_ref, ggot0, ggot1, r1_ref, s1_ref = take(5)
        bg_ref, wt_ref, woa_ref, wia_ref, o_ref, k2_ref, bias_ref, small_ref = take(8)
        g_ref, row_ref = take(2)
        send0, send1 = (None, None) if second else take(2)
        vl, hid, ln, gh, vx, hid_prev, x_prev = refs
        place = place_ref[...]
        even_tm = (place & 1) == 0
        even = (band_ref[...] & 1) == 0
        left = lanes() < LAT
        b2, mw, bw = small_ref[0], small_ref[1], small_ref[2]

        def strip(n, ahead):
            one, two = (0, 1) if ahead else (1, 0)
            v = pick(even_tm, (got0, got1)[one][n], (got0, got1)[two][n])
            if second:
                v = v - alpha_ref[...] * pick(even_tm, (ggot0, ggot1)[one][n], (ggot0, ggot1)[two][n])
            return v

        keep = left | (place < n_tm - 1)
        for n in range(6):
            u = strip(n, True)
            for k, part in ((n, halves(u)), (n + 6, u)):
                nxt = jnp.where(left, halves(x_ref[k]), part)
                lv = jnp.where(keep, mw * (nxt - m_ref[k]), 0.0)
                ln[k] = lv
                stack_lats(vl, k, lv)
        dwn = [strip(n, False) for n in range(6)]
        for r in range(8):
            one = dwn[r] if r < 6 else halves(dwn[r - 6])
            two = dwn[r - 2] if r >= 2 else halves(dwn[r + 4])
            v = jnp.where(left, one, two)
            x_prev[r] = v
            stack_lats(vx, r, v)
        bias = bias_ref[...]
        bias2 = jnp.concatenate([bias, bias], axis=1)
        for h in range(0, 6, 2):
            act, _ = gelu_pair(dot(o_ref[...], window(vx, h, 3 * C)) + bias2)
            for k in range(2):
                n = h + k
                hid_prev[F * n : F * (n + 1)] = act[:, W2 * k : W2 * (k + 1)].astype(BF16)
        for h in range(0, 10, 2):
            z = dot(woa_ref[...], window(vl, h, 3 * C))
            for k in range(2):
                n = h + k
                hid[F * n : F * (n + 1)] = (slope[n] * z[:, W2 * k : W2 * (k + 1)]).astype(BF16)
        for o in range(0, BAND, 2):
            s = sum_lats(dot(wia_ref[...], window(hid, o, F)))
            for k in range(2):
                gh[o + k] = ln[o + k + 2] + s[k]
        squares = jnp.zeros((C, W2), F32)
        cost = jnp.zeros((C, W2), F32)
        for o in range(0, 4, 2):
            s = sum_lats(dot(k2_ref[...], window(hid_prev, o, F)))
            for k in range(2):
                m = x_prev[o + k + 2] + s[k] + b2
                sides = []
                for side in range(2):
                    i = o + k + 4 * side
                    x = x_ref[i + 2]
                    before = m if side == 0 else halves(m)
                    first = jnp.where(place > 0, mw * (x - before), 0.0)
                    lo = jnp.where(left, first, halves(ln[i + 2]))
                    dep = jnp.where(left & (place == 0), x - bg_ref[i], 0.0)
                    seen = s0_ref[i]
                    if second:
                        seen = seen - alpha_ref[...] * s1_ref[i]
                    g = lo - gh[i] + seen + bw * dep
                    g_ref[i] = g
                    sides.append(g)
                    squares = squares + g * g
                    cost = cost + lo * lo / mw + bw * dep * dep
                if not second:
                    send0[o + k] = jnp.where(even, sides[1], sides[0]).astype(BF16)
                    send1[o + k] = jnp.where(even, sides[0], sides[1]).astype(BF16)
        r = r0_ref[...]
        if second:
            r = r - alpha_ref[:, :1] * r1_ref[...]
        paid = jnp.sum(wt_ref[...] * r * r, axis=1, keepdims=True)
        norm = jnp.sum(jnp.sum(squares, axis=0, keepdims=True), axis=1, keepdims=True)
        paid = 0.5 * (paid + jnp.sum(jnp.sum(cost, axis=0, keepdims=True), axis=1, keepdims=True))
        lane = lax.broadcasted_iota(jnp.int32, (n_all, W2), 1)
        row_ref[...] = jnp.where(lane == 0, norm, jnp.where(lane == 1, paid, 0.0))

    return kernel


def gradient(n_tm, n_all, ins, second):
    edge = ((HALO, C, W2), BF16)
    outs = [((BAND, C, W2), F32), ((n_all, W2), F32)] + ([] if second else [edge, edge])
    scratch = [pltpu.VMEM((12 * 3 * C, W2), BF16), pltpu.VMEM((10 * F, W2), BF16), pltpu.VMEM((12, C, W2), F32)]
    scratch += [pltpu.VMEM((BAND, C, W2), F32), pltpu.VMEM((8 * 3 * C, W2), BF16), pltpu.VMEM((6 * F, W2), BF16)]
    scratch += [pltpu.VMEM((8, C, W2), F32)]
    return call(gradient_kernel(second, n_tm, n_all), ins, outs, scratch, limit=16)


def final_kernel(total):
    def kernel(step_ref, first_ref, sums_ref, x_ref, g_ref, x_out, cost_out):
        alpha = step_from(sums_ref[...], step_ref[...], total)
        for i in range(BAND):
            v = x_ref[i + 2] - alpha * g_ref[i]
            v = jnp.concatenate([v, jnp.zeros((W2 - C, W2), F32)], axis=0).T[:, :C]
            x_out[0, i] = v[:LAT]
            x_out[1, i] = v[LAT:]
        c0 = jnp.sum(first_ref[...], axis=0, keepdims=True)
        c1 = jnp.sum(sums_ref[...], axis=0, keepdims=True)
        lane = lax.broadcasted_iota(jnp.int32, c0.shape, 1)
        one = jnp.sum(jnp.where(lane == 1, c0, 0.0), axis=1, keepdims=True)
        two = jnp.sum(jnp.where(lane == 1, c1, 0.0), axis=1, keepdims=True)
        cost_out[...] = jnp.where(lane == 0, one, two)[:, :2]

    return kernel


def swapped(value, axes, first):
    n = lax.axis_size(axes)
    closed = axes == LON
    pairs = []
    for i in range(first, n, 2):
        j = (i + 1) % n
        if closed or j > i:
            pairs += [(i, j), (j, i)]
    return lax.ppermute(value, axes, pairs)


def exchange(place, band, mine0, mine1):
    got0 = swapped(mine0, LON, 0)
    got1 = swapped(mine1, LON, 1)
    send0, send1 = strips(place, band, mine0, mine1, got0, got1)
    strip0 = swapped(send0, TM, 0)
    strip1 = swapped(send1, TM, 1)
    return got0, got1, strip0, strip1, send0


def per_device(x, background, opening, b1, closing, b2, mw, bw, cell, chan, val, wt, step):
    n_tm = lax.axis_size(TM)
    n_all = n_tm * lax.axis_size(LON)
    total = float(2 * BAND * C * LAT * n_all)
    place = lax.axis_index(TM).astype(jnp.int32)[None]
    band = lax.axis_index(LON).astype(jnp.int32)[None]
    xp, mine0, mine1, place, band, step, spot, chan, val, wt, b1, small = pack(
        place, band, step[None], jnp.swapaxes(x, 2, 3), (cell, chan, val, wt), (b1, b2, mw, bw)
    )
    got0, got1, strip0, strip1, _ = exchange(place, band, mine0, mine1)
    o, k2, wia, woa, bias, small, bgp = prepare_weights(opening.T, closing, b1, small, jnp.swapaxes(background, 1, 2))
    nets = (o, k2, bias, small)
    own = (band, xp, got0, got1) + nets
    lines = (spot, chan, val, wt)
    x0, m0, slope = forward(total, own, False)
    r0, s0, hot = observe(lines, xp)
    rest = (bgp, wt, woa, wia) + nets
    g0, row, mine0, mine1 = gradient(n_tm, n_all, (place, band, x0, m0, slope, strip0, strip1, r0, s0) + rest, False)
    sums0 = lax.all_to_all(row, TM_LON, 0, 0, tiled=True)
    ggot0, ggot1, gstrip0, gstrip1, sent = exchange(place, band, mine0, mine1)
    later_g0, _ = lax.optimization_barrier((g0, sent))
    x1, m1, slope, alpha = forward(total, (step, sums0, g0, ggot0, ggot1) + own, True)
    r1, s1 = observe(lines, later_g0, hot)
    ins = (place, band, x1, m1, slope, strip0, strip1, r0, s0, alpha, gstrip0, gstrip1, r1, s1)
    g1, row = gradient(n_tm, n_all, ins + rest, True)
    sums1 = lax.all_to_all(row, TM_LON, 0, 0, tiled=True)
    x2, costs = call(
        final_kernel(total),
        [step, sums0, sums1, x1, g1],
        [((2, BAND, LAT, C), F32), ((1, 2), F32)],
    )
    return jnp.swapaxes(x2, 2, 3), costs.reshape(2)


def solution(mesh):
    n_tm, n_lon = mesh.devices.shape
    if (n_tm, n_lon) == (8, 32):
        shape = (4, 2, 2, 8, 2)
    else:
        shape = (n_tm, 1, 1, n_lon // 2, 2)
    split = Mesh(mesh.devices.reshape(shape), TM_LON)
    placed = (
        P(TM, LON, None, None),
        P(LON, None, None),
        P(), P(), P(), P(), P(), P(),
        P(TM, LON), P(TM, LON), P(TM, LON), P(TM, LON),
        P(),
    )
    return jax.shard_map(
        per_device,
        mesh=split,
        in_specs=placed,
        out_specs=(P(TM, LON, None, None), P()),
        check_vma=False,
    )
```

time: 98.6 us -> 94.2 us (0.955)
  starting transfers between devices: 32 us -> 27.8 us
  Pallas kernels: 17.3 us -> 15.2 us
  other arithmetic: 0 us -> 1.37 us
    ppermute x8, starting transfers between devices: 16.9 us -> 9.79 us  [swapped(): return lax.ppermute(value, axes, pairs)]
    unnamed x58 -> x38, local copies, waits for them, and re-layouts: 13.3 us -> 9.49 us
    all_to_all x1, starting transfers between devices: 15.1 us -> 18 us  [per_device(): sums0 = lax.all_to_all(row, TM_LON, 0, 0, tiled=True)]
    pallas_call x13 -> x11, Pallas kernels: 17.3 us -> 15.2 us  [call(): pl.pallas_call(kernel, out_shape=tuple((jax.ShapeDtypeStruct(shape, dtype...]
    pad x0 -> x3, local copies, waits for them, and re-layouts: none -> 1.98 us  [pack(): jnp.pad(v, (0, OBS - v.shape[0]))[None]]
    concatenate x0 -> x1, local copies, waits for them, and re-layouts: none -> 1.41 us  [pack(): jnp.concatenate(rows, axis=0)]
    convert_element_type x0 -> x2, other arithmetic: none -> 1.37 us  [pack(): v.astype(F32)]
  transfers between devices with their start and end apart: 9 -> 9, of which waited for: 4 -> 4; matrix products, arithmetic and copies ran while one was open for 0% -> 0% of each run, Pallas kernels for 12% -> 8%
where the time goes in v3:
time: 94.2 us; the launch traced here: 93.7 us
  starting transfers between devices  27.8 us (30%)
  blocking collectives  26.6 us (28%)
  Pallas kernels  15.2 us (16%)
  local copies, waits for them, and re-layouts  12.9 us (14%)
  waiting for transfers between devices  8.26 us (9%)
  between operations  1.49 us (2%)
  other arithmetic  1.37 us (1%)
    all_to_all x1, blocking collectives, per_device(): sums1 = lax.all_to_all(row, TM_LON, 0, 0, tiled=True)  26.6 us
    all_to_all x1, starting transfers between devices, per_device(): sums0 = lax.all_to_all(row, TM_LON, 0, 0, tiled=True)  18 us
    pallas_call x11, Pallas kernels, call(): pl.pallas_call(kernel, out_shape=tuple((jax.ShapeDtypeStruct(shape, dtype...  15.2 us
    ppermute x8, starting transfers between devices, swapped(): return lax.ppermute(value, axes, pairs)  9.79 us
    unnamed x38, local copies, waits for them, and re-layouts  9.49 us
    ppermute x8, waiting for transfers between devices, swapped(): return lax.ppermute(value, axes, pairs)  8.26 us
    pad x3, local copies, waits for them, and re-layouts, pack(): jnp.pad(v, (0, OBS - v.shape[0]))[None]  1.98 us
  transfers between devices with their start and end apart: 9, of which 4 were waited for; matrix products, arithmetic and copies ran while one was open for 0% of the time, Pallas kernels for 8%

profile of v3, /device:TPU:1, one launch (start us, length us, event | category | flops | bytes accessed | tf_op | source)
XLA Modules:
  0.0 93.7 jit_solution(11664652165325058005)
XLA Ops:
  1.3 0.7 pad.10
  1.9 0.7 pad.11
  2.6 0.7 pad.12
  3.3 0.7 convert_element_type.10
  3.9 0.7 convert_element_type.11
  4.6 1.4 %concatenate.3.table_ref = f32[12,256]{1,0:T(8,128)S(1)} concatenate(f32[2,256]{1,0:T(2,128)S(1)} %convert_element_type.10, f32[2,256]{1,0:T(2,128)S(1)} %convert_element_type.11, f32[2,256]{1,0:T(2,128)} %param.23, f32[2,256]{1,0:T(2,128)} %param.24, f32[1,256]{1,0:T(1,128)} %bitcast.32, f32[1,256]{1,0:T(1,128)S(1)} %bitcast.29, f32[1,256]{1,0:T(1,128)S(1)} %bitcast.30, ...), dimensions={0} | concatenate | bytes 24576 | tf_op jit(solution)/shard_map/concatenate | solution.py:97
  6.0 0.0 copy-start.2
  6.1 1.0 %copy-done.2 = f32[2,8,80,64]{2,3,1,0:T(8,128)S(1)} copy-done((f32[2,8,80,64]{2,3,1,0:T(8,128)S(1)}, f32[2,8,80,64]{2,3,1,0:T(8,128)}, u32[]{:S(2)}) %copy-start.2) | copy-done | bytes 327704
  7.1 0.0 copy-start.5
  7.1 0.0 copy-start.6
  7.1 0.0 copy-start.13
  7.1 0.2 shard_map.140
  7.3 3.3 %collective-permute-start = (bf16[4,80,128]{2,1,0:T(8,128)(2,1)S(1)}, bf16[4,80,128]{2,1,0:T(8,128)(2,1)S(1)}, u32[]{:S(2)}, u32[]{:S(2)}) collective-permute-start(bf16[4,80,128]{2,1,0:T(8,128)(2,1)S(1)} %get-tuple-element.50.mine0), channel_id=1, source_target_pairs={{0,1},{1,0},{2,3},{3,2},{4,5},{5,4},{6,7},{7,6},{8,9},{9,8},{10,11... | collective-permute-start | bytes 245768 | tf_op jit(solution)/shard_map/ppermute | solution.py:422
  10.6 0.0 collective-permute-start.1
  10.6 0.9 collective-permute-done.refs_2_.got0.refs_7_
  11.5 2.9 %collective-permute-done.1.refs_3_.got1.refs_8_ = bf16[4,80,128]{2,1,0:T(8,128)(2,1)S(1)} collective-permute-done((bf16[4,80,128]{2,1,0:T(8,128)(2,1)S(1)}, bf16[4,80,128]{2,1,0:T(8,128)(2,1)S(1)}, u32[]{:S(2)}, u32[]{:S(2)}) %collective-permute-start.1) | collective-permute-done | bytes 81952 | tf_op jit(solution)/shard_map/ppermute | solution.py:422
  14.4 0.1 shard_map.143
  14.6 0.1 collective-permute-start.2
  14.7 0.7 collective-permute-start.3
  15.4 0.9 shard_map.144
  16.2 0.0 copy-start
  16.2 1.0 %copy-done = bf16[4,256,512]{2,1,0:T(8,128)(2,1)} copy-done((bf16[4,256,512]{2,1,0:T(8,128)(2,1)}, bf16[4,256,512]{2,1,0:T(8,128)(2,1)S(1)}, u32[]{:S(2)}) %copy-start) | copy-done | bytes 1048600
  17.2 0.0 copy-done.5
  17.2 0.0 copy-done.6
  17.2 0.0 copy-done.13
  17.2 0.5 shard_map.141
  17.7 2.1 %shard_map.142 = (f32[12,80,128]{2,1,0:T(8,128)S(1)}, f32[12,80,128]{2,1,0:T(8,128)S(1)}, f32[10,256,128]{2,1,0:T(8,128)S(1)}) custom-call(s32[1,128]{1,0:T(1,128)S(1)} %get-tuple-element.48.refs_0_.band_ref.refs_1_.refs_5_, f32[8,80,128]{2,1,0:T(8,128)S(1)} %get-tuple-element.49.refs_1_.x_ref.refs_6_, ...), custom_call_target="tpu_custom_call" | custom-call | tf_op jit(solution)/shard_map/pallas_call | solution.py:32
  19.8 0.0 collective-permute-done.2.refs_5_
  19.8 0.0 collective-permute-done.3.refs_6_
  19.8 0.0 copy-start.3
  19.8 2.6 %shard_map.145 = (f32[8,80,128]{2,1,0:T(8,128)S(1)}, f32[256,128]{1,0:T(8,128)S(1)}, bf16[4,80,128]{2,1,0:T(8,128)(2,1)S(1)}, bf16[4,80,128]{2,1,0:T(8,128)(2,1)S(1)}) custom-call(s32[1,128]{1,0:T(1,128)S(1)} %get-tuple-element.47.place_ref.refs_0_, s32[1,128]{1,0:T(1,128)S(1)} %get-tuple-element.48.refs_0_.band_ref.refs_1_.refs_5_, ...), custom_call_target="tpu_custom_call" | custom-call | tf_op jit(solution)/shard_map/pallas_call | solution.py:32
  22.5 0.0 copy-done.3
  22.5 0.0 copy-start.14
  22.5 0.6 copy-done.14
  23.1 0.0 copy-start.15
  23.1 0.6 copy-done.15
  23.8 0.6 copy-done.17
  24.4 18.0 %all-to-all-start = ((f32[256,1,128]{2,1,0:T(1,128)}), f32[256,1,128]{2,1,0:T(1,128)S(1)}, u32[]{:S(2)}, u32[]{:S(2)}) async-start(f32[256,1,128]{2,1,0:T(1,128)} %bitcast.27), calls=%async_computation | async-start | bytes 262144 | tf_op jit(solution)/shard_map/all_to_all | solution.py:452
  42.4 2.2 %collective-permute-start.4 = (bf16[4,80,128]{2,1,0:T(8,128)(2,1)}, bf16[4,80,128]{2,1,0:T(8,128)(2,1)S(1)}, u32[]{:S(2)}, u32[]{:S(2)}) collective-permute-start(bf16[4,80,128]{2,1,0:T(8,128)(2,1)} %copy-done.15), channel_id=1, source_target_pairs={{0,1},{1,0},{2,3},{3,2},{4,5},{5,4},{6,7},{7,6},{8,9},{9,8},{10,11... | collective-permute-start | bytes 245768 | tf_op jit(solution)/shard_map/ppermute | solution.py:422
  44.7 0.0 collective-permute-start.5
  44.7 1.1 %collective-permute-done.4.refs_3_.got0 = bf16[4,80,128]{2,1,0:T(8,128)(2,1)S(1)} collective-permute-done((bf16[4,80,128]{2,1,0:T(8,128)(2,1)}, bf16[4,80,128]{2,1,0:T(8,128)(2,1)S(1)}, u32[]{:S(2)}, u32[]{:S(2)}) %collective-permute-start.4) | collective-permute-done | bytes 81952 | tf_op jit(solution)/shard_map/ppermute | solution.py:422
  45.8 3.3 %collective-permute-done.5.refs_4_.got1 = bf16[4,80,128]{2,1,0:T(8,128)(2,1)S(1)} collective-permute-done((bf16[4,80,128]{2,1,0:T(8,128)(2,1)}, bf16[4,80,128]{2,1,0:T(8,128)(2,1)S(1)}, u32[]{:S(2)}, u32[]{:S(2)}) %collective-permute-start.5) | collective-permute-done | bytes 81952 | tf_op jit(solution)/shard_map/ppermute | solution.py:422
  49.1 0.9 copy-done.16
  49.9 0.9 copy-done.18
  50.8 0.8 shard_map.147
  51.7 1.3 %collective-permute-start.7 = (bf16[6,80,128]{2,1,0:T(8,128)(2,1)}, bf16[6,80,128]{2,1,0:T(8,128)(2,1)}, u32[]{:S(2)}, u32[]{:S(2)}) collective-permute-start(bf16[6,80,128]{2,1,0:T(8,128)(2,1)} %get-tuple-element.81), channel_id=1, source_target_pairs={{32,64},{64,32},{96,128},{128,96},{160,192},{192,160},{33,65},{65,... | collective-permute-start | bytes 368648 | tf_op jit(solution)/shard_map/ppermute | solution.py:422
  53.0 2.2 %collective-permute-start.6 = (bf16[6,80,128]{2,1,0:T(8,128)(2,1)}, bf16[6,80,128]{2,1,0:T(8,128)(2,1)}, u32[]{:S(2)}, u32[]{:S(2)}) collective-permute-start(bf16[6,80,128]{2,1,0:T(8,128)(2,1)} %get-tuple-element.80), channel_id=1, source_target_pairs={{0,32},{32,0},{64,96},{96,64},{128,160},{160,128},{192,224},{224,1... | collective-permute-start | bytes 368648 | tf_op jit(solution)/shard_map/ppermute | solution.py:422
  55.2 0.0 copy-done.9
  55.2 0.0 copy-done.11
  55.2 1.2 %copy-done.1 = bf16[4,256,512]{2,1,0:T(8,128)(2,1)S(1)} copy-done((bf16[4,256,512]{2,1,0:T(8,128)(2,1)S(1)}, bf16[4,256,512]{2,1,0:T(8,128)(2,1)}, u32[]{:S(2)}) %copy-start.1) | copy-done | bytes 1048600
  56.4 0.9 shard_map.148
  57.3 0.0 copy-start.7
  57.3 0.7 copy-done.7
  58.0 0.0 all-to-all-done
  58.0 0.9 %copy-done.10 = bf16[4,80,128]{2,1,0:T(8,128)(2,1)S(1)} copy-done((bf16[4,80,128]{2,1,0:T(8,128)(2,1)S(1)}, bf16[4,80,128]{2,1,0:T(8,128)(2,1)}, u32[]{:S(2)}) %copy-start.10) | copy-done | bytes 81944
  58.9 0.9 copy-done.12
  59.8 2.3 %shard_map.146 = (f32[12,80,128]{2,1,0:T(8,128)S(1)}, f32[12,80,128]{2,1,0:T(8,128)S(1)}, f32[10,256,128]{2,1,0:T(8,128)S(1)}, f32[1,128]{1,0:T(1,128)S(1)}) custom-call(f32[1,128]{1,0:T(1,128)S(1)} %get-tuple-element.46.refs_0_.step_ref, f32[256,128]{1,0:T(8,128)S(1)} %bitcast.21, f32[8,80,128]{2,1,0:T(8,128)S(1)} %get-tuple-element.82.refs_2_.x_ref, ...), custom_call_target="tpu_custom_call" | custom-call | tf_op jit(solution)/shard_map/pallas_call | solution.py:32
  62.1 0.0 collective-permute-done.7.refs_11_
  62.1 0.0 collective-permute-done.6.refs_10_
  62.1 0.0 copy-done.4
  62.1 0.0 copy-done.8
  62.1 3.6 %shard_map.149 = (f32[8,80,128]{2,1,0:T(8,128)S(1)}, f32[256,128]{1,0:T(8,128)S(1)}) custom-call(s32[1,128]{1,0:T(1,128)S(1)} %get-tuple-element.47.place_ref.refs_0_, s32[1,128]{1,0:T(1,128)S(1)} %get-tuple-element.48.refs_0_.band_ref.refs_1_.refs_5_, f32[12,80,128]{2,1,0:T(8,128)S(1)} %get-tuple-element.76.refs_2_.x_ref, ...), custom_call_target="tpu_custom_call" | custom-call | tf_op jit(solution)/shard_map/pallas_call | solution.py:32
  65.8 26.6 %all_to_all.22 = f32[256,1,128]{2,1,0:T(1,128)S(1)} all-to-all(f32[256,1,128]{2,1,0:T(1,128)S(1)} %bitcast.28), channel_id=1, replica_groups=mesh['tm_0'=4,'tm_1'=2,'lon_0'=2,'lon_1'=8,'lon_2'=2] {'tm_0','tm_1','lo..., dimensions={0} | all-to-all | bytes 262144 | tf_op jit(solution)/shard_map/all_to_all | solution.py:459
  92.4 1.2 %shard_map.150 = (f32[2,8,64,80]{3,2,1,0:T(8,128)}, f32[1,2]{1,0:T(1,128)}) custom-call(f32[1,128]{1,0:T(1,128)S(1)} %get-tuple-element.46.refs_0_.step_ref, f32[256,128]{1,0:T(8,128)S(1)} %bitcast.22, f32[256,128]{1,0:T(8,128)S(1)} %bitcast.24, f32[12,80,128]{2,1,0:T(8,128)S(1)} %get-tuple-element.76.refs_2_.x_ref, f32[8,80,128]{2,1,0:T(8,128)S(1)} %get-tuple-element.87.g_ref), custom_call_target="tpu_custom_call" | custom-call | tf_op jit(solution)/shard_map/pallas_call | solution.py:32
  (10 shorter events, 0.0 us)
Async XLA Ops:
  6.0 1.0 %copy-start.2 = (f32[2,8,80,64]{2,3,1,0:T(8,128)S(1)}, f32[2,8,80,64]{2,3,1,0:T(8,128)}, u32[]{:S(2)}) copy-start(f32[2,8,80,64]{2,3,1,0:T(8,128)} %param.13) | copy-start | bytes 983044
  7.1 10.1 %copy-start.5 = (bf16[256,720]{0,1:T(8,128)(2,1)S(1)}, bf16[256,720]{0,1:T(8,128)(2,1)}, u32[]{:S(2)}) copy-start(bf16[256,720]{0,1:T(8,128)(2,1)} %param.15) | copy-start | bytes 1105924
  7.1 10.1 %copy-start.6 = (bf16[80,2304]{1,0:T(8,128)(2,1)S(1)}, bf16[80,2304]{1,0:T(8,128)(2,1)}, u32[]{:S(2)}) copy-start(bf16[80,2304]{1,0:T(8,128)(2,1)} %c_ref.1) | copy-start | bytes 1105924
  7.1 10.1 %copy-start.13 = (f32[8,80,64]{1,2,0:T(8,128)S(1)}, f32[8,80,64]{1,2,0:T(8,128)}, u32[]{:S(2)}) copy-start(f32[8,80,64]{1,2,0:T(8,128)} %param.14) | copy-start | bytes 491524
  7.3 4.2 %collective-permute-start = (bf16[4,80,128]{2,1,0:T(8,128)(2,1)S(1)}, bf16[4,80,128]{2,1,0:T(8,128)(2,1)S(1)}, u32[]{:S(2)}, u32[]{:S(2)}) collective-permute-start(bf16[4,80,128]{2,1,0:T(8,128)(2,1)S(1)} %get-tuple-element.50.mine0), channel_id=1, source_target_pairs={{0,1},{1,0},{2,3},{3,2},{4,5},{5,4},{6,7},{7,6},{8,9},{9,8},{10,11... | collective-permute-start | bytes 245768 | tf_op jit(solution)/shard_map/ppermute | solution.py:422
  10.6 3.9 %collective-permute-start.1 = (bf16[4,80,128]{2,1,0:T(8,128)(2,1)S(1)}, bf16[4,80,128]{2,1,0:T(8,128)(2,1)S(1)}, u32[]{:S(2)}, u32[]{:S(2)}) collective-permute-start(bf16[4,80,128]{2,1,0:T(8,128)(2,1)S(1)} %get-tuple-element.51.mine1), channel_id=1, source_target_pairs={{1,2},{2,1},{3,4},{4,3},{5,6},{6,5},{7,8},{8,7},{9,10},{10,9},{11,... | collective-permute-start | bytes 245768 | tf_op jit(solution)/shard_map/ppermute | solution.py:422
  14.6 5.2 %collective-permute-start.2 = (bf16[6,80,128]{2,1,0:T(8,128)(2,1)S(1)}, bf16[6,80,128]{2,1,0:T(8,128)(2,1)S(1)}, u32[]{:S(2)}, u32[]{:S(2)}) collective-permute-start(bf16[6,80,128]{2,1,0:T(8,128)(2,1)S(1)} %get-tuple-element.61), channel_id=1, source_target_pairs={{0,32},{32,0},{64,96},{96,64},{128,160},{160,128},{192,224},{224,1... | collective-permute-start | bytes 368648 | tf_op jit(solution)/shard_map/ppermute | solution.py:422
  14.7 5.1 %collective-permute-start.3 = (bf16[6,80,128]{2,1,0:T(8,128)(2,1)S(1)}, bf16[6,80,128]{2,1,0:T(8,128)(2,1)S(1)}, u32[]{:S(2)}, u32[]{:S(2)}) collective-permute-start(bf16[6,80,128]{2,1,0:T(8,128)(2,1)S(1)} %get-tuple-element.62), channel_id=1, source_target_pairs={{32,64},{64,32},{96,128},{128,96},{160,192},{192,160},{33,65},{65,... | collective-permute-start | bytes 368648 | tf_op jit(solution)/shard_map/ppermute | solution.py:422
  16.2 1.0 %copy-start = (bf16[4,256,512]{2,1,0:T(8,128)(2,1)}, bf16[4,256,512]{2,1,0:T(8,128)(2,1)S(1)}, u32[]{:S(2)}) copy-start(bf16[4,256,512]{2,1,0:T(8,128)(2,1)S(1)} %get-tuple-element.83.refs_0_) | copy-start | bytes 3145732
  19.8 2.6 %copy-start.3 = (bf16[6,80,128]{2,1,0:T(8,128)(2,1)}, bf16[6,80,128]{2,1,0:T(8,128)(2,1)S(1)}, u32[]{:S(2)}) copy-start(bf16[6,80,128]{2,1,0:T(8,128)(2,1)S(1)} %collective-permute-done.3.refs_6_) | copy-start | bytes 368644
  22.5 0.7 copy-start.14
  23.1 0.6 copy-start.15
  23.8 0.6 copy-start.17
  24.4 33.6 %all-to-all-start = ((f32[256,1,128]{2,1,0:T(1,128)}), f32[256,1,128]{2,1,0:T(1,128)S(1)}, u32[]{:S(2)}, u32[]{:S(2)}) async-start(f32[256,1,128]{2,1,0:T(1,128)} %bitcast.27), calls=%async_computation | async-start | bytes 262144 | tf_op jit(solution)/shard_map/all_to_all | solution.py:452
  42.4 3.4 %collective-permute-start.4 = (bf16[4,80,128]{2,1,0:T(8,128)(2,1)}, bf16[4,80,128]{2,1,0:T(8,128)(2,1)S(1)}, u32[]{:S(2)}, u32[]{:S(2)}) collective-permute-start(bf16[4,80,128]{2,1,0:T(8,128)(2,1)} %copy-done.15), channel_id=1, source_target_pairs={{0,1},{1,0},{2,3},{3,2},{4,5},{5,4},{6,7},{7,6},{8,9},{9,8},{10,11... | collective-permute-start | bytes 245768 | tf_op jit(solution)/shard_map/ppermute | solution.py:422
  44.7 4.4 %collective-permute-start.5 = (bf16[4,80,128]{2,1,0:T(8,128)(2,1)}, bf16[4,80,128]{2,1,0:T(8,128)(2,1)S(1)}, u32[]{:S(2)}, u32[]{:S(2)}) collective-permute-start(bf16[4,80,128]{2,1,0:T(8,128)(2,1)} %copy-done.17), channel_id=1, source_target_pairs={{1,2},{2,1},{3,4},{4,3},{5,6},{6,5},{7,8},{8,7},{9,10},{10,9},{11,... | collective-permute-start | bytes 245768 | tf_op jit(solution)/shard_map/ppermute | solution.py:422
  45.8 9.4 %copy-start.9 = (bf16[4,80,128]{2,1,0:T(8,128)(2,1)}, bf16[4,80,128]{2,1,0:T(8,128)(2,1)S(1)}, u32[]{:S(2)}) copy-start(bf16[4,80,128]{2,1,0:T(8,128)(2,1)S(1)} %collective-permute-done.4.refs_3_.got0) | copy-start | bytes 245764
  49.1 0.9 copy-start.16
  49.9 0.9 copy-start.18
  50.8 4.3 %copy-start.11 = (bf16[4,80,128]{2,1,0:T(8,128)(2,1)}, bf16[4,80,128]{2,1,0:T(8,128)(2,1)S(1)}, u32[]{:S(2)}) copy-start(bf16[4,80,128]{2,1,0:T(8,128)(2,1)S(1)} %collective-permute-done.5.refs_4_.got1) | copy-start | bytes 245764
  51.7 10.4 %collective-permute-start.7 = (bf16[6,80,128]{2,1,0:T(8,128)(2,1)}, bf16[6,80,128]{2,1,0:T(8,128)(2,1)}, u32[]{:S(2)}, u32[]{:S(2)}) collective-permute-start(bf16[6,80,128]{2,1,0:T(8,128)(2,1)} %get-tuple-element.81), channel_id=1, source_target_pairs={{32,64},{64,32},{96,128},{128,96},{160,192},{192,160},{33,65},{65,... | collective-permute-start | bytes 368648 | tf_op jit(solution)/shard_map/ppermute | solution.py:422
  53.0 9.1 %collective-permute-start.6 = (bf16[6,80,128]{2,1,0:T(8,128)(2,1)}, bf16[6,80,128]{2,1,0:T(8,128)(2,1)}, u32[]{:S(2)}, u32[]{:S(2)}) collective-permute-start(bf16[6,80,128]{2,1,0:T(8,128)(2,1)} %get-tuple-element.80), channel_id=1, source_target_pairs={{0,32},{32,0},{64,96},{96,64},{128,160},{160,128},{192,224},{224,1... | collective-permute-start | bytes 368648 | tf_op jit(solution)/shard_map/ppermute | solution.py:422
  55.2 1.2 %copy-start.1 = (bf16[4,256,512]{2,1,0:T(8,128)(2,1)S(1)}, bf16[4,256,512]{2,1,0:T(8,128)(2,1)}, u32[]{:S(2)}) copy-start(bf16[4,256,512]{2,1,0:T(8,128)(2,1)} %copy-done) | copy-start | bytes 3145732
  57.3 0.7 copy-start.7
  58.0 4.1 %copy-start.4 = (bf16[6,80,128]{2,1,0:T(8,128)(2,1)S(1)}, bf16[6,80,128]{2,1,0:T(8,128)(2,1)}, u32[]{:S(2)}) copy-start(bf16[6,80,128]{2,1,0:T(8,128)(2,1)} %copy-done.3) | copy-start | bytes 368644
  58.0 4.1 %copy-start.8 = (f32[8,80,128]{2,1,0:T(8,128)S(1)}, f32[8,80,128]{2,1,0:T(8,128)}, u32[]{:S(2)}) copy-start(f32[8,80,128]{2,1,0:T(8,128)} %copy-done.7) | copy-start | bytes 983044
  58.0 0.9 %copy-start.10 = (bf16[4,80,128]{2,1,0:T(8,128)(2,1)S(1)}, bf16[4,80,128]{2,1,0:T(8,128)(2,1)}, u32[]{:S(2)}) copy-start(bf16[4,80,128]{2,1,0:T(8,128)(2,1)} %copy-done.9) | copy-start | bytes 245764
  58.9 0.9 copy-start.12

commit v4 on v3

--- a/solution.py
+++ b/solution.py
@@ -35,7 +35,7 @@
         in_specs=[smem] * scalars + [vmem] * (len(ins) - scalars),
         out_specs=tuple(vmem for _ in outs),
         scratch_shapes=list(scratch),
-        compiler_params=pltpu.CompilerParams(vmem_limit_bytes=limit << 20),
+        compiler_params=pltpu.CompilerParams(vmem_limit_bytes=int(limit * 2**20)),
     )(*ins)
 
 
@@ -61,23 +61,10 @@
     return jnp.where(even, one.astype(F32), two.astype(F32))
 
 
-def pack_kernel(place_ref, band_ref, step_ref, x_ref, table_ref,
-                xp_ref, s0_ref, s1_ref, place_row, band_row, step_row, spot_row, chan_row, val_row, wt_row, b1_row, small_row):
+def pack_kernel(place_ref, band_ref, step_ref, x_ref, xp_ref, s0_ref, s1_ref, place_row, band_row, step_row):
     place_row[...] = jnp.full((1, W2), place_ref[0], jnp.int32)
     band_row[...] = jnp.full((1, W2), band_ref[0], jnp.int32)
     step_row[...] = jnp.full((1, W2), step_ref[0], F32)
-
-    def line(n):
-        return jnp.concatenate([table_ref[n : n + 1, :], table_ref[n + 1 : n + 2, :]], axis=1)
-
-    cell = line(0).astype(jnp.int32)
-    sub = (lax.broadcasted_iota(jnp.int32, cell.shape, 1) >= OBS).astype(jnp.int32)
-    spot_row[...] = (cell >> 6) * W2 + sub * LAT + (cell & (LAT - 1))
-    chan_row[...] = line(2).astype(jnp.int32)
-    val_row[...] = line(4)
-    wt_row[...] = line(6)
-    b1_row[...] = table_ref[8:9, :]
-    small_row[...] = table_ref[9:12, :C]
     even = (jnp.full((1, W2), band_ref[0], jnp.int32) & 1) == 0
     for i in range(HALO):
         one = jnp.concatenate([x_ref[0, i], x_ref[1, i]], axis=0).T
@@ -88,16 +75,14 @@
         s1_ref[i] = jnp.where(even, one, two).astype(BF16)
 
 
-def pack(place, band, step, x, obs, small):
+def pack(place, band, step, x):
     edge = ((HALO, C, W2), BF16)
     row = lambda n, dtype: ((1, n), dtype)
     outs = [((BAND, C, W2), F32), edge, edge, row(W2, jnp.int32), row(W2, jnp.int32), row(W2, F32)]
-    outs += [row(2 * OBS, jnp.int32), row(2 * OBS, jnp.int32), row(2 * OBS, F32), row(2 * OBS, F32), row(F, F32), ((3, C), F32)]
-    rows = [v.astype(F32) for v in obs] + [jnp.pad(v, (0, OBS - v.shape[0]))[None] for v in small]
-    return call(pack_kernel, [place, band, step, x, jnp.concatenate(rows, axis=0)], outs, scalars=3)
-
-
-def weights_kernel(ot_ref, c_ref, b1_ref, row_ref, bg_ref,
+    return call(pack_kernel, [place, band, step, x], outs, limit=8, scalars=3)
+
+
+def weights_kernel(ot_ref, c_ref, b1_ref, b2_ref, mw_ref, bw_ref, bg_ref,
                    o_ref, k2_ref, wia_ref, woa_ref, bias_ref, small_ref, bgp_ref, tall, row):
     tall[9 * C :, :] = jnp.zeros((768 - 9 * C, F), F32)
     tall[: 9 * C, :] = ot_ref[...].astype(F32)
@@ -113,15 +98,15 @@
     woa_ref[...] = back[:, : 9 * C].astype(BF16)
     bias_ref[...] = jnp.broadcast_to(b1_ref[...], (W2, F)).T
     row[...] = jnp.zeros((W2, W2), F32)
-    for n in range(3):
-        row[:, :C] = jnp.broadcast_to(row_ref[n : n + 1, :], (W2, C))
+    for n, ref in enumerate((b2_ref, mw_ref, bw_ref)):
+        row[:, :C] = jnp.broadcast_to(ref[...], (W2, C))
         small_ref[n] = row[...].T[:C]
     for i in range(BAND):
         bgp_ref[i] = jnp.concatenate([bg_ref[i], jnp.zeros((LAT, C), F32)], axis=0).T
 
 
-def prepare_weights(opening_t, closing, b1, small, bg):
-    ins = [opening_t, closing, b1, small, bg]
+def prepare_weights(opening_t, closing, b1, b2, mw, bw, bg):
+    ins = [opening_t, closing, b1[None], b2[None], mw[None], bw[None], bg]
     outs = [((F, 9 * C), BF16), ((3 * C, 3 * F), BF16), ((3 * C, 3 * F), BF16), ((F, 9 * C), BF16)]
     outs += [((F, W2), F32), ((3, C, W2), F32), ((BAND, C, W2), F32)]
     return call(
@@ -129,6 +114,7 @@
         ins,
         outs,
         [pltpu.VMEM((768, F), F32), pltpu.VMEM((W2, W2), F32)],
+        limit=8,
     )
 
 
@@ -144,24 +130,35 @@
     return (v[2 * C :] + v[C : 2 * C]) + v[:C]
 
 
-def obs_kernel(spot_ref, chan_ref, val_ref, wt_ref, x_ref, *refs):
-    first = len(refs) == 3 and refs[0].shape[0] == 1
-    if first:
-        r_ref, s_ref, hot = refs
-        spot = spot_ref[...]
-        rows = 2 * W2
-        for p in range(BAND // 2):
-            at = lax.broadcasted_iota(jnp.int32, (rows, 2 * OBS), 0) + p * rows
-            hot[p] = jnp.where(at == spot, 1.0, 0.0).astype(BF16)
-    else:
-        hot, r_ref, s_ref = refs
+def lines(ref):
+    return jnp.concatenate([ref[0:1, :], ref[1:2, :]], axis=1)
+
+
+def first_obs_kernel(cell_ref, chan_ref, val_ref, wt_ref, x_ref, r_ref, s_ref, hot, chan_row, wt_row):
+    cell = lines(cell_ref)
+    sub = (lax.broadcasted_iota(jnp.int32, cell.shape, 1) >= OBS).astype(jnp.int32)
+    spot = (cell >> 6) * W2 + sub * LAT + (cell & (LAT - 1))
+    rows = 2 * W2
+    for p in range(BAND // 2):
+        at = lax.broadcasted_iota(jnp.int32, (rows, 2 * OBS), 0) + p * rows
+        hot[p] = jnp.where(at == spot, 1.0, 0.0).astype(BF16)
+    chan_row[...] = lines(chan_ref)
+    wt_row[...] = lines(wt_ref)
+    watch(chan_row, wt_row, hot, x_ref, r_ref, s_ref, lines(val_ref))
+
+
+def later_obs_kernel(chan_row, wt_row, hot, x_ref, r_ref, s_ref):
+    watch(chan_row, wt_row, hot, x_ref, r_ref, s_ref, None)
+
+
+def watch(chan_ref, wt_ref, hot, x_ref, r_ref, s_ref, val):
     total = jnp.zeros((3 * C, 2 * OBS), F32)
     for p in range(BAND // 2):
         total = total + dot(split3(jnp.concatenate([x_ref[2 * p], x_ref[2 * p + 1]], axis=1)), hot[p])
     mine = lax.broadcasted_iota(jnp.int32, (C, 2 * OBS), 0) == chan_ref[...]
     r = jnp.sum(jnp.where(mine, join3(total), 0.0), axis=0, keepdims=True)
-    if first:
-        r = r - val_ref[...]
+    if val is not None:
+        r = r - val
     r_ref[...] = r
     spread = split3(jnp.where(mine, wt_ref[...] * r, 0.0))
     for p in range(BAND // 2):
@@ -171,11 +168,16 @@
         s_ref[2 * p + 1] = got[:, W2:]
 
 
-def observe(lines, field, hot=None):
-    outs = [((1, 2 * OBS), F32), ((BAND, C, W2), F32)]
-    if hot is None:
-        return call(obs_kernel, list(lines) + [field], outs + [((BAND // 2, 2 * W2, 2 * OBS), BF16)])
-    return call(obs_kernel, list(lines) + [field, hot], outs)
+SEEN = [((1, 2 * OBS), F32), ((BAND, C, W2), F32)]
+
+
+def observe_first(cell, chan, val, wt, field):
+    more = [((BAND // 2, 2 * W2, 2 * OBS), BF16), ((1, 2 * OBS), jnp.int32), ((1, 2 * OBS), F32)]
+    return call(first_obs_kernel, [cell, chan, val, wt, field], SEEN + more, limit=8)
+
+
+def observe_later(chan, wt, hot, field):
+    return call(later_obs_kernel, [chan, wt, hot, field], SEEN, limit=8)
 
 
 def strip_kernel(place_ref, band_ref, mine0, mine1, got0, got1, send0, send1):
@@ -437,23 +439,22 @@
     total = float(2 * BAND * C * LAT * n_all)
     place = lax.axis_index(TM).astype(jnp.int32)[None]
     band = lax.axis_index(LON).astype(jnp.int32)[None]
-    xp, mine0, mine1, place, band, step, spot, chan, val, wt, b1, small = pack(
-        place, band, step[None], jnp.swapaxes(x, 2, 3), (cell, chan, val, wt), (b1, b2, mw, bw)
+    xp, mine0, mine1, place, band, step = pack(place, band, step[None], jnp.swapaxes(x, 2, 3))
+    got0, got1, strip0, strip1, _ = exchange(place, band, mine0, mine1)
+    o, k2, wia, woa, bias, small, bgp = prepare_weights(
+        opening.T, closing, b1, b2, mw, bw, jnp.swapaxes(background, 1, 2)
     )
-    got0, got1, strip0, strip1, _ = exchange(place, band, mine0, mine1)
-    o, k2, wia, woa, bias, small, bgp = prepare_weights(opening.T, closing, b1, small, jnp.swapaxes(background, 1, 2))
     nets = (o, k2, bias, small)
     own = (band, xp, got0, got1) + nets
-    lines = (spot, chan, val, wt)
     x0, m0, slope = forward(total, own, False)
-    r0, s0, hot = observe(lines, xp)
+    r0, s0, hot, chan, wt = observe_first(cell, chan, val, wt, xp)
     rest = (bgp, wt, woa, wia) + nets
     g0, row, mine0, mine1 = gradient(n_tm, n_all, (place, band, x0, m0, slope, strip0, strip1, r0, s0) + rest, False)
     sums0 = lax.all_to_all(row, TM_LON, 0, 0, tiled=True)
     ggot0, ggot1, gstrip0, gstrip1, sent = exchange(place, band, mine0, mine1)
     later_g0, _ = lax.optimization_barrier((g0, sent))
     x1, m1, slope, alpha = forward(total, (step, sums0, g0, ggot0, ggot1) + own, True)
-    r1, s1 = observe(lines, later_g0, hot)
+    r1, s1 = observe_later(chan, wt, hot, later_g0)
     ins = (place, band, x1, m1, slope, strip0, strip1, r0, s0, alpha, gstrip0, gstrip1, r1, s1)
     g1, row = gradient(n_tm, n_all, ins + rest, True)
     sums1 = lax.all_to_all(row, TM_LON, 0, 0, tiled=True)

time: 94.2 us -> 94.9 us (level)
  local copies, waits for them, and re-layouts: 12.9 us -> 14.9 us
  other arithmetic: 1.37 us -> 0 us
    unnamed x38 -> x54, local copies, waits for them, and re-layouts: 9.49 us -> 14.9 us
    pad x3 -> x0, local copies, waits for them, and re-layouts: 1.98 us -> none  [pack(): jnp.pad(v, (0, OBS - v.shape[0]))[None]]
    concatenate x1 -> x0, local copies, waits for them, and re-layouts: 1.41 us -> none  [pack(): jnp.concatenate(rows, axis=0)]
    convert_element_type x2 -> x0, other arithmetic: 1.37 us -> none  [pack(): v.astype(F32)]
where the time goes in v4:
time: 94.9 us; the launch traced here: 94.3 us
  starting transfers between devices  27.9 us (29%)
  blocking collectives  26.6 us (28%)
  Pallas kernels  15.2 us (16%)
  local copies, waits for them, and re-layouts  14.9 us (16%)
  waiting for transfers between devices  8.25 us (9%)
  between operations  1.51 us (2%)
    all_to_all x1, blocking collectives, per_device(): sums1 = lax.all_to_all(row, TM_LON, 0, 0, tiled=True)  26.6 us
    all_to_all x1, starting transfers between devices, per_device(): sums0 = lax.all_to_all(row, TM_LON, 0, 0, tiled=True)  18 us
    pallas_call x11, Pallas kernels, call(): pl.pallas_call(kernel, out_shape=tuple((jax.ShapeDtypeStruct(shape, dtype...  15.2 us
    unnamed x54, local copies, waits for them, and re-layouts  14.9 us
    ppermute x8, starting transfers between devices, swapped(): return lax.ppermute(value, axes, pairs)  9.84 us
    ppermute x8, waiting for transfers between devices, swapped(): return lax.ppermute(value, axes, pairs)  8.25 us
  transfers between devices with their start and end apart: 9, of which 4 were waited for; matrix products, arithmetic and copies ran while one was open for 0% of the time, Pallas kernels for 8%

profile of v4, /device:TPU:1, one launch (start us, length us, event | category | flops | bytes accessed | tf_op | source)
XLA Modules:
  0.0 94.3 jit_solution(17645619708779051691)
XLA Ops:
  1.3 0.0 copy-start.2
  1.3 1.0 %copy-done.2 = f32[2,8,80,64]{2,3,1,0:T(8,128)S(1)} copy-done((f32[2,8,80,64]{2,3,1,0:T(8,128)S(1)}, f32[2,8,80,64]{2,3,1,0:T(8,128)}, u32[]{:S(2)}) %copy-start.2) | copy-done | bytes 327704
  2.3 0.0 copy-start.5
  2.3 0.2 shard_map.140
  2.5 3.3 %collective-permute-start = (bf16[4,80,128]{2,1,0:T(8,128)(2,1)S(1)}, bf16[4,80,128]{2,1,0:T(8,128)(2,1)S(1)}, u32[]{:S(2)}, u32[]{:S(2)}) collective-permute-start(bf16[4,80,128]{2,1,0:T(8,128)(2,1)S(1)} %get-tuple-element.46.mine0), channel_id=1, source_target_pairs={{0,1},{1,0},{2,3},{3,2},{4,5},{5,4},{6,7},{7,6},{8,9},{9,8},{10,11... | collective-permute-start | bytes 245768 | tf_op jit(solution)/shard_map/ppermute | solution.py:424
  5.8 0.0 collective-permute-start.1
  5.8 0.9 collective-permute-done.refs_2_.got0.refs_7_
  6.7 2.9 %collective-permute-done.1.refs_3_.got1.refs_8_ = bf16[4,80,128]{2,1,0:T(8,128)(2,1)S(1)} collective-permute-done((bf16[4,80,128]{2,1,0:T(8,128)(2,1)S(1)}, bf16[4,80,128]{2,1,0:T(8,128)(2,1)S(1)}, u32[]{:S(2)}, u32[]{:S(2)}) %collective-permute-start.1) | collective-permute-done | bytes 81952 | tf_op jit(solution)/shard_map/ppermute | solution.py:424
  9.7 0.1 shard_map.143
  9.8 0.1 collective-permute-start.2
  9.9 0.7 collective-permute-start.3
  10.6 0.0 copy-start.19
  10.6 0.7 copy-done.19
  11.3 0.7 copy-done.20
  12.0 0.7 copy-done.21
  12.7 0.7 copy-done.22
  13.3 0.9 shard_map.144
  14.3 0.0 copy-start
  14.3 1.0 %copy-done = bf16[4,256,512]{2,1,0:T(8,128)(2,1)} copy-done((bf16[4,256,512]{2,1,0:T(8,128)(2,1)}, bf16[4,256,512]{2,1,0:T(8,128)(2,1)S(1)}, u32[]{:S(2)}) %copy-start) | copy-done | bytes 1048600
  15.3 0.0 copy-done.5
  15.3 0.0 copy-done.6
  15.3 0.0 copy-done.13
  15.3 0.7 copy-done.23
  16.0 0.7 copy-done.24
  16.6 0.7 copy-done.25
  17.3 0.7 copy-done.26
  17.9 0.5 shard_map.141
  18.4 2.1 %shard_map.142 = (f32[12,80,128]{2,1,0:T(8,128)S(1)}, f32[12,80,128]{2,1,0:T(8,128)S(1)}, f32[10,256,128]{2,1,0:T(8,128)S(1)}) custom-call(s32[1,128]{1,0:T(1,128)S(1)} %get-tuple-element.44.refs_0_.band_ref.refs_1_.refs_5_, f32[8,80,128]{2,1,0:T(8,128)S(1)} %get-tuple-element.45.refs_1_.x_ref.refs_6_, ...), custom_call_target="tpu_custom_call" | custom-call | tf_op jit(solution)/shard_map/pallas_call | solution.py:32
  20.5 0.0 collective-permute-done.2.refs_5_
  20.5 0.0 collective-permute-done.3.refs_6_
  20.5 0.0 copy-start.3
  20.5 2.6 %shard_map.145 = (f32[8,80,128]{2,1,0:T(8,128)S(1)}, f32[256,128]{1,0:T(8,128)S(1)}, bf16[4,80,128]{2,1,0:T(8,128)(2,1)S(1)}, bf16[4,80,128]{2,1,0:T(8,128)(2,1)S(1)}) custom-call(s32[1,128]{1,0:T(1,128)S(1)} %get-tuple-element.43.place_ref.refs_0_, s32[1,128]{1,0:T(1,128)S(1)} %get-tuple-element.44.refs_0_.band_ref.refs_1_.refs_5_, ...), custom_call_target="tpu_custom_call" | custom-call | tf_op jit(solution)/shard_map/pallas_call | solution.py:32
  23.1 0.0 copy-done.3
  23.2 0.0 copy-start.14
  23.2 0.6 copy-done.14
  23.8 0.6 copy-done.15
  24.4 0.6 copy-done.17
  25.1 18.0 %all-to-all-start = ((f32[256,1,128]{2,1,0:T(1,128)}), f32[256,1,128]{2,1,0:T(1,128)S(1)}, u32[]{:S(2)}, u32[]{:S(2)}) async-start(f32[256,1,128]{2,1,0:T(1,128)} %bitcast.27), calls=%async_computation | async-start | bytes 262144 | tf_op jit(solution)/shard_map/all_to_all | solution.py:453
  43.1 2.2 %collective-permute-start.4 = (bf16[4,80,128]{2,1,0:T(8,128)(2,1)}, bf16[4,80,128]{2,1,0:T(8,128)(2,1)S(1)}, u32[]{:S(2)}, u32[]{:S(2)}) collective-permute-start(bf16[4,80,128]{2,1,0:T(8,128)(2,1)} %copy-done.15), channel_id=1, source_target_pairs={{0,1},{1,0},{2,3},{3,2},{4,5},{5,4},{6,7},{7,6},{8,9},{9,8},{10,11... | collective-permute-start | bytes 245768 | tf_op jit(solution)/shard_map/ppermute | solution.py:424
  45.3 0.0 collective-permute-start.5
  45.3 1.1 %collective-permute-done.4.refs_3_.got0 = bf16[4,80,128]{2,1,0:T(8,128)(2,1)S(1)} collective-permute-done((bf16[4,80,128]{2,1,0:T(8,128)(2,1)}, bf16[4,80,128]{2,1,0:T(8,128)(2,1)S(1)}, u32[]{:S(2)}, u32[]{:S(2)}) %collective-permute-start.4) | collective-permute-done | bytes 81952 | tf_op jit(solution)/shard_map/ppermute | solution.py:424
  46.5 3.2 %collective-permute-done.5.refs_4_.got1 = bf16[4,80,128]{2,1,0:T(8,128)(2,1)S(1)} collective-permute-done((bf16[4,80,128]{2,1,0:T(8,128)(2,1)}, bf16[4,80,128]{2,1,0:T(8,128)(2,1)S(1)}, u32[]{:S(2)}, u32[]{:S(2)}) %collective-permute-start.5) | collective-permute-done | bytes 81952 | tf_op jit(solution)/shard_map/ppermute | solution.py:424
  49.7 0.9 copy-done.16
  50.6 0.9 copy-done.18
  51.5 0.8 shard_map.147
  52.3 1.3 %collective-permute-start.7 = (bf16[6,80,128]{2,1,0:T(8,128)(2,1)}, bf16[6,80,128]{2,1,0:T(8,128)(2,1)}, u32[]{:S(2)}, u32[]{:S(2)}) collective-permute-start(bf16[6,80,128]{2,1,0:T(8,128)(2,1)} %get-tuple-element.72), channel_id=1, source_target_pairs={{32,64},{64,32},{96,128},{128,96},{160,192},{192,160},{33,65},{65,... | collective-permute-start | bytes 368648 | tf_op jit(solution)/shard_map/ppermute | solution.py:424
  53.6 2.3 %collective-permute-start.6 = (bf16[6,80,128]{2,1,0:T(8,128)(2,1)}, bf16[6,80,128]{2,1,0:T(8,128)(2,1)}, u32[]{:S(2)}, u32[]{:S(2)}) collective-permute-start(bf16[6,80,128]{2,1,0:T(8,128)(2,1)} %get-tuple-element.71), channel_id=1, source_target_pairs={{0,32},{32,0},{64,96},{96,64},{128,160},{160,128},{192,224},{224,1... | collective-permute-start | bytes 368648 | tf_op jit(solution)/shard_map/ppermute | solution.py:424
  55.9 0.0 copy-done.9
  55.9 0.0 copy-done.11
  55.9 1.2 %copy-done.1 = bf16[4,256,512]{2,1,0:T(8,128)(2,1)S(1)} copy-done((bf16[4,256,512]{2,1,0:T(8,128)(2,1)S(1)}, bf16[4,256,512]{2,1,0:T(8,128)(2,1)}, u32[]{:S(2)}) %copy-start.1) | copy-done | bytes 1048600
  57.1 0.9 shard_map.148
  58.0 0.0 copy-start.7
  58.0 0.7 copy-done.7
  58.7 0.0 all-to-all-done
  58.7 0.9 copy-done.10
  59.7 0.9 copy-done.12
  60.5 2.3 %shard_map.146 = (f32[12,80,128]{2,1,0:T(8,128)S(1)}, f32[12,80,128]{2,1,0:T(8,128)S(1)}, f32[10,256,128]{2,1,0:T(8,128)S(1)}, f32[1,128]{1,0:T(1,128)S(1)}) custom-call(f32[1,128]{1,0:T(1,128)S(1)} %get-tuple-element.42.refs_0_.step_ref, f32[256,128]{1,0:T(8,128)S(1)} %bitcast.21, f32[8,80,128]{2,1,0:T(8,128)S(1)} %get-tuple-element.75.refs_2_.x_ref, ...), custom_call_target="tpu_custom_call" | custom-call | tf_op jit(solution)/shard_map/pallas_call | solution.py:32
  62.8 0.0 collective-permute-done.7.refs_11_
  62.8 0.0 collective-permute-done.6.refs_10_
  62.8 0.0 copy-done.4
  62.8 0.0 copy-done.8
  62.9 3.6 %shard_map.149 = (f32[8,80,128]{2,1,0:T(8,128)S(1)}, f32[256,128]{1,0:T(8,128)S(1)}) custom-call(s32[1,128]{1,0:T(1,128)S(1)} %get-tuple-element.43.place_ref.refs_0_, s32[1,128]{1,0:T(1,128)S(1)} %get-tuple-element.44.refs_0_.band_ref.refs_1_.refs_5_, f32[12,80,128]{2,1,0:T(8,128)S(1)} %get-tuple-element.67.refs_2_.x_ref, ...), custom_call_target="tpu_custom_call" | custom-call | tf_op jit(solution)/shard_map/pallas_call | solution.py:32
  66.5 26.6 %all_to_all.22 = f32[256,1,128]{2,1,0:T(1,128)S(1)} all-to-all(f32[256,1,128]{2,1,0:T(1,128)S(1)} %bitcast.28), channel_id=1, replica_groups=mesh['tm_0'=4,'tm_1'=2,'lon_0'=2,'lon_1'=8,'lon_2'=2] {'tm_0','tm_1','lo..., dimensions={0} | all-to-all | bytes 262144 | tf_op jit(solution)/shard_map/all_to_all | solution.py:460
  93.1 1.2 %shard_map.150 = (f32[2,8,64,80]{3,2,1,0:T(8,128)}, f32[1,2]{1,0:T(1,128)}) custom-call(f32[1,128]{1,0:T(1,128)S(1)} %get-tuple-element.42.refs_0_.step_ref, f32[256,128]{1,0:T(8,128)S(1)} %bitcast.22, f32[256,128]{1,0:T(8,128)S(1)} %bitcast.24, f32[12,80,128]{2,1,0:T(8,128)S(1)} %get-tuple-element.67.refs_2_.x_ref, f32[8,80,128]{2,1,0:T(8,128)S(1)} %get-tuple-element.79.g_ref), custom_call_target="tpu_custom_call" | custom-call | tf_op jit(solution)/shard_map/pallas_call | solution.py:32
  (20 shorter events, 0.0 us)
Async XLA Ops:
  1.3 1.0 %copy-start.2 = (f32[2,8,80,64]{2,3,1,0:T(8,128)S(1)}, f32[2,8,80,64]{2,3,1,0:T(8,128)}, u32[]{:S(2)}) copy-start(f32[2,8,80,64]{2,3,1,0:T(8,128)} %param.13) | copy-start | bytes 983044
  2.3 12.9 %copy-start.5 = (bf16[256,720]{0,1:T(8,128)(2,1)S(1)}, bf16[256,720]{0,1:T(8,128)(2,1)}, u32[]{:S(2)}) copy-start(bf16[256,720]{0,1:T(8,128)(2,1)} %param.15) | copy-start | bytes 1105924
  2.3 12.9 %copy-start.6 = (bf16[80,2304]{1,0:T(8,128)(2,1)S(1)}, bf16[80,2304]{1,0:T(8,128)(2,1)}, u32[]{:S(2)}) copy-start(bf16[80,2304]{1,0:T(8,128)(2,1)} %c_ref.1) | copy-start | bytes 1105924
  2.3 12.9 %copy-start.13 = (f32[8,80,64]{1,2,0:T(8,128)S(1)}, f32[8,80,64]{1,2,0:T(8,128)}, u32[]{:S(2)}) copy-start(f32[8,80,64]{1,2,0:T(8,128)} %param.14) | copy-start | bytes 491524
  2.5 4.2 %collective-permute-start = (bf16[4,80,128]{2,1,0:T(8,128)(2,1)S(1)}, bf16[4,80,128]{2,1,0:T(8,128)(2,1)S(1)}, u32[]{:S(2)}, u32[]{:S(2)}) collective-permute-start(bf16[4,80,128]{2,1,0:T(8,128)(2,1)S(1)} %get-tuple-element.46.mine0), channel_id=1, source_target_pairs={{0,1},{1,0},{2,3},{3,2},{4,5},{5,4},{6,7},{7,6},{8,9},{9,8},{10,11... | collective-permute-start | bytes 245768 | tf_op jit(solution)/shard_map/ppermute | solution.py:424
  5.8 3.9 %collective-permute-start.1 = (bf16[4,80,128]{2,1,0:T(8,128)(2,1)S(1)}, bf16[4,80,128]{2,1,0:T(8,128)(2,1)S(1)}, u32[]{:S(2)}, u32[]{:S(2)}) collective-permute-start(bf16[4,80,128]{2,1,0:T(8,128)(2,1)S(1)} %get-tuple-element.47.mine1), channel_id=1, source_target_pairs={{1,2},{2,1},{3,4},{4,3},{5,6},{6,5},{7,8},{8,7},{9,10},{10,9},{11,... | collective-permute-start | bytes 245768 | tf_op jit(solution)/shard_map/ppermute | solution.py:424
  9.8 10.7 %collective-permute-start.2 = (bf16[6,80,128]{2,1,0:T(8,128)(2,1)S(1)}, bf16[6,80,128]{2,1,0:T(8,128)(2,1)S(1)}, u32[]{:S(2)}, u32[]{:S(2)}) collective-permute-start(bf16[6,80,128]{2,1,0:T(8,128)(2,1)S(1)} %get-tuple-element.55), channel_id=1, source_target_pairs={{0,32},{32,0},{64,96},{96,64},{128,160},{160,128},{192,224},{224,1... | collective-permute-start | bytes 368648 | tf_op jit(solution)/shard_map/ppermute | solution.py:424
  9.9 10.6 %collective-permute-start.3 = (bf16[6,80,128]{2,1,0:T(8,128)(2,1)S(1)}, bf16[6,80,128]{2,1,0:T(8,128)(2,1)S(1)}, u32[]{:S(2)}, u32[]{:S(2)}) collective-permute-start(bf16[6,80,128]{2,1,0:T(8,128)(2,1)S(1)} %get-tuple-element.56), channel_id=1, source_target_pairs={{32,64},{64,32},{96,128},{128,96},{160,192},{192,160},{33,65},{65,... | collective-permute-start | bytes 368648 | tf_op jit(solution)/shard_map/ppermute | solution.py:424
  10.6 0.7 copy-start.19
  11.3 0.7 copy-start.20
  12.0 0.7 copy-start.21
  12.7 0.7 copy-start.22
  14.3 1.0 %copy-start = (bf16[4,256,512]{2,1,0:T(8,128)(2,1)}, bf16[4,256,512]{2,1,0:T(8,128)(2,1)S(1)}, u32[]{:S(2)}) copy-start(bf16[4,256,512]{2,1,0:T(8,128)(2,1)S(1)} %get-tuple-element.74.hot) | copy-start | bytes 3145732
  15.3 0.7 copy-start.23
  16.0 0.7 copy-start.24
  16.6 0.7 copy-start.25
  17.3 0.7 copy-start.26
  20.5 2.6 %copy-start.3 = (bf16[6,80,128]{2,1,0:T(8,128)(2,1)}, bf16[6,80,128]{2,1,0:T(8,128)(2,1)S(1)}, u32[]{:S(2)}) copy-start(bf16[6,80,128]{2,1,0:T(8,128)(2,1)S(1)} %collective-permute-done.3.refs_6_) | copy-start | bytes 368644
  23.2 0.6 copy-start.14
  23.8 0.6 copy-start.15
  24.4 0.6 copy-start.17
  25.1 33.6 %all-to-all-start = ((f32[256,1,128]{2,1,0:T(1,128)}), f32[256,1,128]{2,1,0:T(1,128)S(1)}, u32[]{:S(2)}, u32[]{:S(2)}) async-start(f32[256,1,128]{2,1,0:T(1,128)} %bitcast.27), calls=%async_computation | async-start | bytes 262144 | tf_op jit(solution)/shard_map/all_to_all | solution.py:453
  43.1 3.4 %collective-permute-start.4 = (bf16[4,80,128]{2,1,0:T(8,128)(2,1)}, bf16[4,80,128]{2,1,0:T(8,128)(2,1)S(1)}, u32[]{:S(2)}, u32[]{:S(2)}) collective-permute-start(bf16[4,80,128]{2,1,0:T(8,128)(2,1)} %copy-done.15), channel_id=1, source_target_pairs={{0,1},{1,0},{2,3},{3,2},{4,5},{5,4},{6,7},{7,6},{8,9},{9,8},{10,11... | collective-permute-start | bytes 245768 | tf_op jit(solution)/shard_map/ppermute | solution.py:424
  45.3 4.4 %collective-permute-start.5 = (bf16[4,80,128]{2,1,0:T(8,128)(2,1)}, bf16[4,80,128]{2,1,0:T(8,128)(2,1)S(1)}, u32[]{:S(2)}, u32[]{:S(2)}) collective-permute-start(bf16[4,80,128]{2,1,0:T(8,128)(2,1)} %copy-done.17), channel_id=1, source_target_pairs={{1,2},{2,1},{3,4},{4,3},{5,6},{6,5},{7,8},{8,7},{9,10},{10,9},{11,... | collective-permute-start | bytes 245768 | tf_op jit(solution)/shard_map/ppermute | solution.py:424
  46.5 9.4 %copy-start.9 = (bf16[4,80,128]{2,1,0:T(8,128)(2,1)}, bf16[4,80,128]{2,1,0:T(8,128)(2,1)S(1)}, u32[]{:S(2)}) copy-start(bf16[4,80,128]{2,1,0:T(8,128)(2,1)S(1)} %collective-permute-done.4.refs_3_.got0) | copy-start | bytes 245764
  49.7 0.9 copy-start.16
  50.6 0.9 copy-start.18
  51.5 4.4 %copy-start.11 = (bf16[4,80,128]{2,1,0:T(8,128)(2,1)}, bf16[4,80,128]{2,1,0:T(8,128)(2,1)S(1)}, u32[]{:S(2)}) copy-start(bf16[4,80,128]{2,1,0:T(8,128)(2,1)S(1)} %collective-permute-done.5.refs_4_.got1) | copy-start | bytes 245764
  52.3 10.5 %collective-permute-start.7 = (bf16[6,80,128]{2,1,0:T(8,128)(2,1)}, bf16[6,80,128]{2,1,0:T(8,128)(2,1)}, u32[]{:S(2)}, u32[]{:S(2)}) collective-permute-start(bf16[6,80,128]{2,1,0:T(8,128)(2,1)} %get-tuple-element.72), channel_id=1, source_target_pairs={{32,64},{64,32},{96,128},{128,96},{160,192},{192,160},{33,65},{65,... | collective-permute-start | bytes 368648 | tf_op jit(solution)/shard_map/ppermute | solution.py:424
  53.6 9.2 %collective-permute-start.6 = (bf16[6,80,128]{2,1,0:T(8,128)(2,1)}, bf16[6,80,128]{2,1,0:T(8,128)(2,1)}, u32[]{:S(2)}, u32[]{:S(2)}) collective-permute-start(bf16[6,80,128]{2,1,0:T(8,128)(2,1)} %get-tuple-element.71), channel_id=1, source_target_pairs={{0,32},{32,0},{64,96},{96,64},{128,160},{160,128},{192,224},{224,1... | collective-permute-start | bytes 368648 | tf_op jit(solution)/shard_map/ppermute | solution.py:424
  55.9 1.2 %copy-start.1 = (bf16[4,256,512]{2,1,0:T(8,128)(2,1)S(1)}, bf16[4,256,512]{2,1,0:T(8,128)(2,1)}, u32[]{:S(2)}) copy-start(bf16[4,256,512]{2,1,0:T(8,128)(2,1)} %copy-done) | copy-start | bytes 3145732
  58.0 0.7 copy-start.7
  58.7 4.1 %copy-start.4 = (bf16[6,80,128]{2,1,0:T(8,128)(2,1)S(1)}, bf16[6,80,128]{2,1,0:T(8,128)(2,1)}, u32[]{:S(2)}) copy-start(bf16[6,80,128]{2,1,0:T(8,128)(2,1)} %copy-done.3) | copy-start | bytes 368644
  58.7 4.1 %copy-start.8 = (f32[8,80,128]{2,1,0:T(8,128)S(1)}, f32[8,80,128]{2,1,0:T(8,128)}, u32[]{:S(2)}) copy-start(f32[8,80,128]{2,1,0:T(8,128)} %copy-done.7) | copy-start | bytes 983044
  58.7 0.9 copy-start.10
  59.7 0.9 copy-start.12

commit v5 on v4

--- a/solution.py
+++ b/solution.py
@@ -26,14 +26,14 @@
     return lax.broadcasted_iota(jnp.int32, (rows, W2), 1)
 
 
-def call(kernel, ins, outs, scratch=(), limit=8, scalars=0):
+def call(kernel, ins, outs, scratch=(), limit=8, scalars=0, far=0):
     smem = pl.BlockSpec(memory_space=pltpu.SMEM)
     vmem = pl.BlockSpec(memory_space=pltpu.VMEM)
     return pl.pallas_call(
         kernel,
         out_shape=tuple(jax.ShapeDtypeStruct(shape, dtype) for shape, dtype in outs),
         in_specs=[smem] * scalars + [vmem] * (len(ins) - scalars),
-        out_specs=tuple(vmem for _ in outs),
+        out_specs=tuple(pl.BlockSpec(memory_space=pl.ANY) if n < far else vmem for n in range(len(outs))),
         scratch_shapes=list(scratch),
         compiler_params=pltpu.CompilerParams(vmem_limit_bytes=int(limit * 2**20)),
     )(*ins)
@@ -396,19 +396,25 @@
 
 
 def final_kernel(total):
-    def kernel(step_ref, first_ref, sums_ref, x_ref, g_ref, x_out, cost_out):
+    def kernel(step_ref, first_ref, sums_ref, x_ref, g_ref, x_out, cost_out, buf, sems):
         alpha = step_from(sums_ref[...], step_ref[...], total)
+        copies = []
         for i in range(BAND):
             v = x_ref[i + 2] - alpha * g_ref[i]
             v = jnp.concatenate([v, jnp.zeros((W2 - C, W2), F32)], axis=0).T[:, :C]
-            x_out[0, i] = v[:LAT]
-            x_out[1, i] = v[LAT:]
+            buf[0, i] = v[:LAT]
+            buf[1, i] = v[LAT:]
+            copies += [pltpu.make_async_copy(buf.at[k, i], x_out.at[k, i], sems.at[k, i]) for k in range(2)]
+            copies[-2].start()
+            copies[-1].start()
         c0 = jnp.sum(first_ref[...], axis=0, keepdims=True)
         c1 = jnp.sum(sums_ref[...], axis=0, keepdims=True)
         lane = lax.broadcasted_iota(jnp.int32, c0.shape, 1)
         one = jnp.sum(jnp.where(lane == 1, c0, 0.0), axis=1, keepdims=True)
         two = jnp.sum(jnp.where(lane == 1, c1, 0.0), axis=1, keepdims=True)
         cost_out[...] = jnp.where(lane == 0, one, two)[:, :2]
+        for copy in copies:
+            copy.wait()
 
     return kernel
 
@@ -462,6 +468,8 @@
         final_kernel(total),
         [step, sums0, sums1, x1, g1],
         [((2, BAND, LAT, C), F32), ((1, 2), F32)],
+        [pltpu.VMEM((2, BAND, LAT, C), F32), pltpu.SemaphoreType.DMA((2, BAND))],
+        far=1,
     )
     return jnp.swapaxes(x2, 2, 3), costs.reshape(2)
 

time: 94.9 us -> 95.6 us (level)
  no operation moved by 1% of the time
where the time goes in v5:
time: 95.6 us; the launch traced here: 95 us
  starting transfers between devices  27.9 us (29%)
  blocking collectives  26.6 us (28%)
  Pallas kernels  15.7 us (16%)
  local copies, waits for them, and re-layouts  14.9 us (16%)
  waiting for transfers between devices  8.25 us (9%)
  between operations  1.67 us (2%)
    all_to_all x1, blocking collectives, per_device(): sums1 = lax.all_to_all(row, TM_LON, 0, 0, tiled=True)  26.6 us
    all_to_all x1, starting transfers between devices, per_device(): sums0 = lax.all_to_all(row, TM_LON, 0, 0, tiled=True)  18 us
    pallas_call x11, Pallas kernels, call(): pl.pallas_call(kernel, out_shape=tuple((jax.ShapeDtypeStruct(shape, dtype...  15.7 us
    unnamed x54, local copies, waits for them, and re-layouts  14.9 us
    ppermute x8, starting transfers between devices, swapped(): return lax.ppermute(value, axes, pairs)  9.84 us
    ppermute x8, waiting for transfers between devices, swapped(): return lax.ppermute(value, axes, pairs)  8.25 us
  transfers between devices with their start and end apart: 9, of which 4 were waited for; matrix products, arithmetic and copies ran while one was open for 0% of the time, Pallas kernels for 8%

profile of v5, /device:TPU:1, one launch (start us, length us, event | category | flops | bytes accessed | tf_op | source)
XLA Modules:
  0.0 95.0 jit_solution(15105581484691110842)
XLA Ops:
  1.3 0.0 copy-start.2
  1.3 1.0 %copy-done.2 = f32[2,8,80,64]{2,3,1,0:T(8,128)S(1)} copy-done((f32[2,8,80,64]{2,3,1,0:T(8,128)S(1)}, f32[2,8,80,64]{2,3,1,0:T(8,128)}, u32[]{:S(2)}) %copy-start.2) | copy-done | bytes 327704
  2.3 0.0 copy-start.5
  2.3 0.2 shard_map.140
  2.5 3.3 %collective-permute-start = (bf16[4,80,128]{2,1,0:T(8,128)(2,1)S(1)}, bf16[4,80,128]{2,1,0:T(8,128)(2,1)S(1)}, u32[]{:S(2)}, u32[]{:S(2)}) collective-permute-start(bf16[4,80,128]{2,1,0:T(8,128)(2,1)S(1)} %get-tuple-element.46.mine0), channel_id=1, source_target_pairs={{0,1},{1,0},{2,3},{3,2},{4,5},{5,4},{6,7},{7,6},{8,9},{9,8},{10,11... | collective-permute-start | bytes 245768 | tf_op jit(solution)/shard_map/ppermute | solution.py:430
  5.8 0.0 collective-permute-start.1
  5.8 0.9 collective-permute-done.refs_2_.got0.refs_7_
  6.7 2.9 %collective-permute-done.1.refs_3_.got1.refs_8_ = bf16[4,80,128]{2,1,0:T(8,128)(2,1)S(1)} collective-permute-done((bf16[4,80,128]{2,1,0:T(8,128)(2,1)S(1)}, bf16[4,80,128]{2,1,0:T(8,128)(2,1)S(1)}, u32[]{:S(2)}, u32[]{:S(2)}) %collective-permute-start.1) | collective-permute-done | bytes 81952 | tf_op jit(solution)/shard_map/ppermute | solution.py:430
  9.7 0.1 shard_map.143
  9.8 0.1 collective-permute-start.2
  9.9 0.7 collective-permute-start.3
  10.6 0.0 copy-start.19
  10.6 0.7 copy-done.19
  11.3 0.7 copy-done.20
  12.0 0.7 copy-done.21
  12.7 0.7 copy-done.22
  13.3 0.9 shard_map.144
  14.3 0.0 copy-start
  14.3 1.0 %copy-done = bf16[4,256,512]{2,1,0:T(8,128)(2,1)} copy-done((bf16[4,256,512]{2,1,0:T(8,128)(2,1)}, bf16[4,256,512]{2,1,0:T(8,128)(2,1)S(1)}, u32[]{:S(2)}) %copy-start) | copy-done | bytes 1048600
  15.3 0.0 copy-done.5
  15.3 0.0 copy-done.6
  15.3 0.0 copy-done.13
  15.3 0.7 copy-done.23
  16.0 0.7 copy-done.24
  16.6 0.7 copy-done.25
  17.3 0.7 copy-done.26
  17.9 0.5 shard_map.141
  18.4 2.1 %shard_map.142 = (f32[12,80,128]{2,1,0:T(8,128)S(1)}, f32[12,80,128]{2,1,0:T(8,128)S(1)}, f32[10,256,128]{2,1,0:T(8,128)S(1)}) custom-call(s32[1,128]{1,0:T(1,128)S(1)} %get-tuple-element.44.refs_0_.band_ref.refs_1_.refs_5_, f32[8,80,128]{2,1,0:T(8,128)S(1)} %get-tuple-element.45.refs_1_.x_ref.refs_6_, ...), custom_call_target="tpu_custom_call" | custom-call | tf_op jit(solution)/shard_map/pallas_call | solution.py:32
  20.5 0.0 collective-permute-done.2.refs_5_
  20.5 0.0 collective-permute-done.3.refs_6_
  20.5 0.0 copy-start.3
  20.5 2.6 %shard_map.145 = (f32[8,80,128]{2,1,0:T(8,128)S(1)}, f32[256,128]{1,0:T(8,128)S(1)}, bf16[4,80,128]{2,1,0:T(8,128)(2,1)S(1)}, bf16[4,80,128]{2,1,0:T(8,128)(2,1)S(1)}) custom-call(s32[1,128]{1,0:T(1,128)S(1)} %get-tuple-element.43.place_ref.refs_0_, s32[1,128]{1,0:T(1,128)S(1)} %get-tuple-element.44.refs_0_.band_ref.refs_1_.refs_5_, ...), custom_call_target="tpu_custom_call" | custom-call | tf_op jit(solution)/shard_map/pallas_call | solution.py:32
  23.1 0.0 copy-done.3
  23.2 0.0 copy-start.14
  23.2 0.6 copy-done.14
  23.8 0.6 copy-done.15
  24.4 0.6 copy-done.17
  25.1 18.0 %all-to-all-start = ((f32[256,1,128]{2,1,0:T(1,128)}), f32[256,1,128]{2,1,0:T(1,128)S(1)}, u32[]{:S(2)}, u32[]{:S(2)}) async-start(f32[256,1,128]{2,1,0:T(1,128)} %bitcast.27), calls=%async_computation | async-start | bytes 262144 | tf_op jit(solution)/shard_map/all_to_all | solution.py:459
  43.1 2.2 %collective-permute-start.4 = (bf16[4,80,128]{2,1,0:T(8,128)(2,1)}, bf16[4,80,128]{2,1,0:T(8,128)(2,1)S(1)}, u32[]{:S(2)}, u32[]{:S(2)}) collective-permute-start(bf16[4,80,128]{2,1,0:T(8,128)(2,1)} %copy-done.15), channel_id=1, source_target_pairs={{0,1},{1,0},{2,3},{3,2},{4,5},{5,4},{6,7},{7,6},{8,9},{9,8},{10,11... | collective-permute-start | bytes 245768 | tf_op jit(solution)/shard_map/ppermute | solution.py:430
  45.3 0.0 collective-permute-start.5
  45.3 1.1 %collective-permute-done.4.refs_3_.got0 = bf16[4,80,128]{2,1,0:T(8,128)(2,1)S(1)} collective-permute-done((bf16[4,80,128]{2,1,0:T(8,128)(2,1)}, bf16[4,80,128]{2,1,0:T(8,128)(2,1)S(1)}, u32[]{:S(2)}, u32[]{:S(2)}) %collective-permute-start.4) | collective-permute-done | bytes 81952 | tf_op jit(solution)/shard_map/ppermute | solution.py:430
  46.5 3.2 %collective-permute-done.5.refs_4_.got1 = bf16[4,80,128]{2,1,0:T(8,128)(2,1)S(1)} collective-permute-done((bf16[4,80,128]{2,1,0:T(8,128)(2,1)}, bf16[4,80,128]{2,1,0:T(8,128)(2,1)S(1)}, u32[]{:S(2)}, u32[]{:S(2)}) %collective-permute-start.5) | collective-permute-done | bytes 81952 | tf_op jit(solution)/shard_map/ppermute | solution.py:430
  49.7 0.9 copy-done.16
  50.6 0.9 copy-done.18
  51.5 0.8 shard_map.147
  52.3 1.3 %collective-permute-start.7 = (bf16[6,80,128]{2,1,0:T(8,128)(2,1)}, bf16[6,80,128]{2,1,0:T(8,128)(2,1)}, u32[]{:S(2)}, u32[]{:S(2)}) collective-permute-start(bf16[6,80,128]{2,1,0:T(8,128)(2,1)} %get-tuple-element.72), channel_id=1, source_target_pairs={{32,64},{64,32},{96,128},{128,96},{160,192},{192,160},{33,65},{65,... | collective-permute-start | bytes 368648 | tf_op jit(solution)/shard_map/ppermute | solution.py:430
  53.6 2.3 %collective-permute-start.6 = (bf16[6,80,128]{2,1,0:T(8,128)(2,1)}, bf16[6,80,128]{2,1,0:T(8,128)(2,1)}, u32[]{:S(2)}, u32[]{:S(2)}) collective-permute-start(bf16[6,80,128]{2,1,0:T(8,128)(2,1)} %get-tuple-element.71), channel_id=1, source_target_pairs={{0,32},{32,0},{64,96},{96,64},{128,160},{160,128},{192,224},{224,1... | collective-permute-start | bytes 368648 | tf_op jit(solution)/shard_map/ppermute | solution.py:430
  55.9 0.0 copy-done.9
  55.9 0.0 copy-done.11
  55.9 1.2 %copy-done.1 = bf16[4,256,512]{2,1,0:T(8,128)(2,1)S(1)} copy-done((bf16[4,256,512]{2,1,0:T(8,128)(2,1)S(1)}, bf16[4,256,512]{2,1,0:T(8,128)(2,1)}, u32[]{:S(2)}) %copy-start.1) | copy-done | bytes 1048600
  57.1 0.9 shard_map.148
  58.0 0.0 copy-start.7
  58.0 0.7 copy-done.7
  58.7 0.0 all-to-all-done
  58.7 0.9 copy-done.10
  59.7 0.9 copy-done.12
  60.5 2.3 %shard_map.146 = (f32[12,80,128]{2,1,0:T(8,128)S(1)}, f32[12,80,128]{2,1,0:T(8,128)S(1)}, f32[10,256,128]{2,1,0:T(8,128)S(1)}, f32[1,128]{1,0:T(1,128)S(1)}) custom-call(f32[1,128]{1,0:T(1,128)S(1)} %get-tuple-element.42.refs_0_.step_ref, f32[256,128]{1,0:T(8,128)S(1)} %bitcast.21, f32[8,80,128]{2,1,0:T(8,128)S(1)} %get-tuple-element.75.refs_2_.x_ref, ...), custom_call_target="tpu_custom_call" | custom-call | tf_op jit(solution)/shard_map/pallas_call | solution.py:32
  62.8 0.0 collective-permute-done.7.refs_11_
  62.8 0.0 collective-permute-done.6.refs_10_
  62.8 0.0 copy-done.4
  62.8 0.0 copy-done.8
  62.9 3.6 %shard_map.149 = (f32[8,80,128]{2,1,0:T(8,128)S(1)}, f32[256,128]{1,0:T(8,128)S(1)}) custom-call(s32[1,128]{1,0:T(1,128)S(1)} %get-tuple-element.43.place_ref.refs_0_, s32[1,128]{1,0:T(1,128)S(1)} %get-tuple-element.44.refs_0_.band_ref.refs_1_.refs_5_, f32[12,80,128]{2,1,0:T(8,128)S(1)} %get-tuple-element.67.refs_2_.x_ref, ...), custom_call_target="tpu_custom_call" | custom-call | tf_op jit(solution)/shard_map/pallas_call | solution.py:32
  66.5 26.6 %all_to_all.22 = f32[256,1,128]{2,1,0:T(1,128)S(1)} all-to-all(f32[256,1,128]{2,1,0:T(1,128)S(1)} %bitcast.28), channel_id=1, replica_groups=mesh['tm_0'=4,'tm_1'=2,'lon_0'=2,'lon_1'=8,'lon_2'=2] {'tm_0','tm_1','lo..., dimensions={0} | all-to-all | bytes 262144 | tf_op jit(solution)/shard_map/all_to_all | solution.py:466
  93.1 1.7 %shard_map.150 = (f32[2,8,64,80]{3,2,1,0:T(8,128)}, f32[1,2]{1,0:T(1,128)}) custom-call(f32[1,128]{1,0:T(1,128)S(1)} %get-tuple-element.42.refs_0_.step_ref, f32[256,128]{1,0:T(8,128)S(1)} %bitcast.22, f32[256,128]{1,0:T(8,128)S(1)} %bitcast.24, f32[12,80,128]{2,1,0:T(8,128)S(1)} %get-tuple-element.67.refs_2_.x_ref, f32[8,80,128]{2,1,0:T(8,128)S(1)} %get-tuple-element.79.g_ref), custom_call_target="tpu_custom_call" | custom-call | tf_op jit(solution)/shard_map/pallas_call | solution.py:32
  (20 shorter events, 0.0 us)
Async XLA Ops:
  1.3 1.0 %copy-start.2 = (f32[2,8,80,64]{2,3,1,0:T(8,128)S(1)}, f32[2,8,80,64]{2,3,1,0:T(8,128)}, u32[]{:S(2)}) copy-start(f32[2,8,80,64]{2,3,1,0:T(8,128)} %param.13) | copy-start | bytes 983044
  2.3 12.9 %copy-start.5 = (bf16[256,720]{0,1:T(8,128)(2,1)S(1)}, bf16[256,720]{0,1:T(8,128)(2,1)}, u32[]{:S(2)}) copy-start(bf16[256,720]{0,1:T(8,128)(2,1)} %param.15) | copy-start | bytes 1105924
  2.3 12.9 %copy-start.6 = (bf16[80,2304]{1,0:T(8,128)(2,1)S(1)}, bf16[80,2304]{1,0:T(8,128)(2,1)}, u32[]{:S(2)}) copy-start(bf16[80,2304]{1,0:T(8,128)(2,1)} %c_ref.1) | copy-start | bytes 1105924
  2.3 12.9 %copy-start.13 = (f32[8,80,64]{1,2,0:T(8,128)S(1)}, f32[8,80,64]{1,2,0:T(8,128)}, u32[]{:S(2)}) copy-start(f32[8,80,64]{1,2,0:T(8,128)} %param.14) | copy-start | bytes 491524
  2.5 4.2 %collective-permute-start = (bf16[4,80,128]{2,1,0:T(8,128)(2,1)S(1)}, bf16[4,80,128]{2,1,0:T(8,128)(2,1)S(1)}, u32[]{:S(2)}, u32[]{:S(2)}) collective-permute-start(bf16[4,80,128]{2,1,0:T(8,128)(2,1)S(1)} %get-tuple-element.46.mine0), channel_id=1, source_target_pairs={{0,1},{1,0},{2,3},{3,2},{4,5},{5,4},{6,7},{7,6},{8,9},{9,8},{10,11... | collective-permute-start | bytes 245768 | tf_op jit(solution)/shard_map/ppermute | solution.py:430
  5.8 3.9 %collective-permute-start.1 = (bf16[4,80,128]{2,1,0:T(8,128)(2,1)S(1)}, bf16[4,80,128]{2,1,0:T(8,128)(2,1)S(1)}, u32[]{:S(2)}, u32[]{:S(2)}) collective-permute-start(bf16[4,80,128]{2,1,0:T(8,128)(2,1)S(1)} %get-tuple-element.47.mine1), channel_id=1, source_target_pairs={{1,2},{2,1},{3,4},{4,3},{5,6},{6,5},{7,8},{8,7},{9,10},{10,9},{11,... | collective-permute-start | bytes 245768 | tf_op jit(solution)/shard_map/ppermute | solution.py:430
  9.8 10.7 %collective-permute-start.2 = (bf16[6,80,128]{2,1,0:T(8,128)(2,1)S(1)}, bf16[6,80,128]{2,1,0:T(8,128)(2,1)S(1)}, u32[]{:S(2)}, u32[]{:S(2)}) collective-permute-start(bf16[6,80,128]{2,1,0:T(8,128)(2,1)S(1)} %get-tuple-element.55), channel_id=1, source_target_pairs={{0,32},{32,0},{64,96},{96,64},{128,160},{160,128},{192,224},{224,1... | collective-permute-start | bytes 368648 | tf_op jit(solution)/shard_map/ppermute | solution.py:430
  9.9 10.6 %collective-permute-start.3 = (bf16[6,80,128]{2,1,0:T(8,128)(2,1)S(1)}, bf16[6,80,128]{2,1,0:T(8,128)(2,1)S(1)}, u32[]{:S(2)}, u32[]{:S(2)}) collective-permute-start(bf16[6,80,128]{2,1,0:T(8,128)(2,1)S(1)} %get-tuple-element.56), channel_id=1, source_target_pairs={{32,64},{64,32},{96,128},{128,96},{160,192},{192,160},{33,65},{65,... | collective-permute-start | bytes 368648 | tf_op jit(solution)/shard_map/ppermute | solution.py:430
  10.6 0.7 copy-start.19
  11.3 0.7 copy-start.20
  12.0 0.7 copy-start.21
  12.7 0.7 copy-start.22
  14.3 1.0 %copy-start = (bf16[4,256,512]{2,1,0:T(8,128)(2,1)}, bf16[4,256,512]{2,1,0:T(8,128)(2,1)S(1)}, u32[]{:S(2)}) copy-start(bf16[4,256,512]{2,1,0:T(8,128)(2,1)S(1)} %get-tuple-element.74.hot) | copy-start | bytes 3145732
  15.3 0.7 copy-start.23
  16.0 0.7 copy-start.24
  16.6 0.7 copy-start.25
  17.3 0.7 copy-start.26
  20.5 2.6 %copy-start.3 = (bf16[6,80,128]{2,1,0:T(8,128)(2,1)}, bf16[6,80,128]{2,1,0:T(8,128)(2,1)S(1)}, u32[]{:S(2)}) copy-start(bf16[6,80,128]{2,1,0:T(8,128)(2,1)S(1)} %collective-permute-done.3.refs_6_) | copy-start | bytes 368644
  23.2 0.6 copy-start.14
  23.8 0.6 copy-start.15
  24.4 0.6 copy-start.17
  25.1 33.6 %all-to-all-start = ((f32[256,1,128]{2,1,0:T(1,128)}), f32[256,1,128]{2,1,0:T(1,128)S(1)}, u32[]{:S(2)}, u32[]{:S(2)}) async-start(f32[256,1,128]{2,1,0:T(1,128)} %bitcast.27), calls=%async_computation | async-start | bytes 262144 | tf_op jit(solution)/shard_map/all_to_all | solution.py:459
  43.1 3.4 %collective-permute-start.4 = (bf16[4,80,128]{2,1,0:T(8,128)(2,1)}, bf16[4,80,128]{2,1,0:T(8,128)(2,1)S(1)}, u32[]{:S(2)}, u32[]{:S(2)}) collective-permute-start(bf16[4,80,128]{2,1,0:T(8,128)(2,1)} %copy-done.15), channel_id=1, source_target_pairs={{0,1},{1,0},{2,3},{3,2},{4,5},{5,4},{6,7},{7,6},{8,9},{9,8},{10,11... | collective-permute-start | bytes 245768 | tf_op jit(solution)/shard_map/ppermute | solution.py:430
  45.3 4.4 %collective-permute-start.5 = (bf16[4,80,128]{2,1,0:T(8,128)(2,1)}, bf16[4,80,128]{2,1,0:T(8,128)(2,1)S(1)}, u32[]{:S(2)}, u32[]{:S(2)}) collective-permute-start(bf16[4,80,128]{2,1,0:T(8,128)(2,1)} %copy-done.17), channel_id=1, source_target_pairs={{1,2},{2,1},{3,4},{4,3},{5,6},{6,5},{7,8},{8,7},{9,10},{10,9},{11,... | collective-permute-start | bytes 245768 | tf_op jit(solution)/shard_map/ppermute | solution.py:430
  46.5 9.4 %copy-start.9 = (bf16[4,80,128]{2,1,0:T(8,128)(2,1)}, bf16[4,80,128]{2,1,0:T(8,128)(2,1)S(1)}, u32[]{:S(2)}) copy-start(bf16[4,80,128]{2,1,0:T(8,128)(2,1)S(1)} %collective-permute-done.4.refs_3_.got0) | copy-start | bytes 245764
  49.7 0.9 copy-start.16
  50.6 0.9 copy-start.18
  51.5 4.4 %copy-start.11 = (bf16[4,80,128]{2,1,0:T(8,128)(2,1)}, bf16[4,80,128]{2,1,0:T(8,128)(2,1)S(1)}, u32[]{:S(2)}) copy-start(bf16[4,80,128]{2,1,0:T(8,128)(2,1)S(1)} %collective-permute-done.5.refs_4_.got1) | copy-start | bytes 245764
  52.3 10.5 %collective-permute-start.7 = (bf16[6,80,128]{2,1,0:T(8,128)(2,1)}, bf16[6,80,128]{2,1,0:T(8,128)(2,1)}, u32[]{:S(2)}, u32[]{:S(2)}) collective-permute-start(bf16[6,80,128]{2,1,0:T(8,128)(2,1)} %get-tuple-element.72), channel_id=1, source_target_pairs={{32,64},{64,32},{96,128},{128,96},{160,192},{192,160},{33,65},{65,... | collective-permute-start | bytes 368648 | tf_op jit(solution)/shard_map/ppermute | solution.py:430
  53.6 9.2 %collective-permute-start.6 = (bf16[6,80,128]{2,1,0:T(8,128)(2,1)}, bf16[6,80,128]{2,1,0:T(8,128)(2,1)}, u32[]{:S(2)}, u32[]{:S(2)}) collective-permute-start(bf16[6,80,128]{2,1,0:T(8,128)(2,1)} %get-tuple-element.71), channel_id=1, source_target_pairs={{0,32},{32,0},{64,96},{96,64},{128,160},{160,128},{192,224},{224,1... | collective-permute-start | bytes 368648 | tf_op jit(solution)/shard_map/ppermute | solution.py:430
  55.9 1.2 %copy-start.1 = (bf16[4,256,512]{2,1,0:T(8,128)(2,1)S(1)}, bf16[4,256,512]{2,1,0:T(8,128)(2,1)}, u32[]{:S(2)}) copy-start(bf16[4,256,512]{2,1,0:T(8,128)(2,1)} %copy-done) | copy-start | bytes 3145732
  58.0 0.7 copy-start.7
  58.7 4.1 %copy-start.4 = (bf16[6,80,128]{2,1,0:T(8,128)(2,1)S(1)}, bf16[6,80,128]{2,1,0:T(8,128)(2,1)}, u32[]{:S(2)}) copy-start(bf16[6,80,128]{2,1,0:T(8,128)(2,1)} %copy-done.3) | copy-start | bytes 368644
  58.7 4.1 %copy-start.8 = (f32[8,80,128]{2,1,0:T(8,128)S(1)}, f32[8,80,128]{2,1,0:T(8,128)}, u32[]{:S(2)}) copy-start(f32[8,80,128]{2,1,0:T(8,128)} %copy-done.7) | copy-start | bytes 983044
  58.7 0.9 copy-start.10
  59.7 0.9 copy-start.12
